TPU v7x, 512 devices: a whole 4x4x16 slice. The times are simulated.
512 devices in a mesh: ctx: 32 (over z, core), exp: 16 (over x, y).
Axes of the slice: x: 4, y: 4, z: 16, core: 2. Of those that a mesh axis runs over, the one named last changes fastest.
Arguments:
- scan_input: bfloat16 [4096, 4096], P('ctx', 'exp'), may hold values from -6 to 6
- step_size: bfloat16 [4096, 4096], P('ctx', 'exp'), may hold values from 0.5 to 2
- decay_rate: float32 [16, 4096], P(None, 'exp'), may hold values from 2e-06 to 0.1
- input_proj: float32 [16, 4096], P(None, 'ctx'), may hold values from -1.5 to 1.5
- output_proj: float32 [16, 4096], P(None, 'ctx'), may hold values from -0.4 to 0.4
- skip_gain: float32 [4096], P('exp'), may hold values from 0.5 to 1.5
- block_states: float32 [32, 16, 4096], P('ctx', None, 'exp'), may hold values from -24 to 24
- end_grad: float32 [16, 4096], P(None, 'exp'), may hold values from -6 to 6
- scan_grad: bfloat16 [4096, 4096], P('ctx', 'exp'), may hold values from -6 to 6
- moe_grad: bfloat16 [4096, 4096], P(('ctx', 'exp')), may hold values from -6 to 6
- route: int32 [4096, 2], P(('ctx', 'exp')), may hold values from 0 to 15, all different within a row; in each aligned block of 8 rows (0 to 7, 8 to 15, ...) at most 2 rows name the same one
- gate_prob: float32 [4096, 2], P(('ctx', 'exp')), may hold values from 0.1 to 0.9
- w_down: bfloat16 [16, 7168, 4096], P('exp', 'ctx'), may hold values from -0.0625 to 0.0625
- hidden_saved: bfloat16 [16, 1024, 7168], P('exp', None, 'ctx'), may hold values from -6 to 6
Outputs:
- input_grad: bfloat16 [4096, 4096], P('ctx', 'exp')
- step_grad: bfloat16 [4096, 4096], P('ctx', 'exp')
- in_proj_grad: float32 [16, 4096], P(None, 'ctx')
- out_proj_grad: float32 [16, 4096], P(None, 'ctx')
- decay_grad: float32 [16, 4096], P(None, 'exp')
- down_grad: bfloat16 [16, 7168, 4096], P('exp', 'ctx')
- hidden_grad: bfloat16 [16, 1024, 7168], P('exp', None, 'ctx')
Inputs may be any that keep to these rules, and one draw needn't show every extreme that they name: `route`: the experts of one token differ. Within the 8 tokens of one source (aligned blocks of 8 rows) no expert is named more than 2 times, a bound that some block reaches.
All inputs are finite; a program needn't handle non-finite values.
Results may differ from a plain program's by a relative error of at most 0.0049.
Values may be sent and summed in bfloat16 or wider, within the bound.
A program may use at most 64 MiB of HBM per device.

v0:
```python
import jax
import jax.numpy as jnp
from jax import lax
from jax.experimental import pallas as pl
from jax.experimental.pallas import tpu as pltpu
from jax.sharding import PartitionSpec as P

EXPERTS = 16


def shifted_from(value, axis, distance):
    count = lax.axis_size(axis)
    return lax.ppermute(value, axis, [(source, source - distance) for source in range(distance, count)])


def butterfly_sum(value, axis):
    count = lax.axis_size(axis)
    distance = 1
    while distance < count:
        pairs = [(source, source ^ distance) for source in range(count)]
        value = jax.tree.map(lambda part: part + lax.ppermute(part, axis, pairs), value)
        distance *= 2
    return value


def local_scans_kernel(decay_ref, drive_ref, source_ref, first_ref, states_ref, seed_ref):
    count = decay_ref.shape[0]

    def forward(t, state):
        state = decay_ref[t] * state + drive_ref[t]
        states_ref[t] = state
        return state

    lax.fori_loop(0, count, forward, first_ref[...], unroll=8)

    def backward(i, running):
        t = count - 1 - i
        return decay_ref[t] * (source_ref[t] + running)

    seed_ref[...] = lax.fori_loop(0, count, backward, jnp.zeros_like(first_ref[...]), unroll=8)


def local_scans(decays, driving, sources, first_state):
    return pl.pallas_call(
        local_scans_kernel,
        out_shape=(
            jax.ShapeDtypeStruct(decays.shape, jnp.float32),
            jax.ShapeDtypeStruct(first_state.shape, jnp.float32),
        ),
        cost_estimate=pl.CostEstimate(
            flops=4 * decays.size, bytes_accessed=16 * decays.size, transcendentals=0
        ),
    )(decays, driving, sources, first_state)


def adjoint_scan_kernel(decay_ref, source_ref, entering_ref, adjoint_ref):
    count = decay_ref.shape[0]

    def backward(i, running):
        t = count - 1 - i
        value = source_ref[t] + running
        adjoint_ref[t] = value
        return decay_ref[t] * value

    lax.fori_loop(0, count, backward, entering_ref[...], unroll=8)


def adjoint_scan(decays, sources, entering):
    return pl.pallas_call(
        adjoint_scan_kernel,
        out_shape=jax.ShapeDtypeStruct(decays.shape, jnp.float32),
        cost_estimate=pl.CostEstimate(
            flops=2 * decays.size, bytes_accessed=12 * decays.size, transcendentals=0
        ),
    )(decays, sources, entering)


def slot_buffer(moe_grad, route, gate_prob, capacity):
    pair_count = route.shape[0] * route.shape[1]
    weighted = (gate_prob[:, :, None] * moe_grad.astype(jnp.float32)[:, None, :]).astype(
        jnp.bfloat16
    )
    weighted = weighted.reshape(pair_count, moe_grad.shape[1])
    flat_route = route.reshape(pair_count)
    onehot = (flat_route[:, None] == jnp.arange(EXPERTS, dtype=jnp.int32)[None, :]).astype(
        jnp.int32
    )
    ranks = jnp.sum((jnp.cumsum(onehot, axis=0) - onehot) * onehot, axis=1)
    target = flat_route * capacity + ranks
    placing = (target[:, None] == jnp.arange(EXPERTS * capacity, dtype=jnp.int32)[None, :]).astype(
        jnp.bfloat16
    )
    buffer = jnp.einsum("ps,pd->sd", placing, weighted, preferred_element_type=jnp.float32).astype(
        jnp.bfloat16
    )
    return buffer.reshape(EXPERTS, capacity, moe_grad.shape[1])


def body(
    scan_input,
    step_size,
    decay_rate,
    input_proj,
    output_proj,
    skip_gain,
    block_states,
    end_grad,
    scan_grad,
    moe_grad,
    route,
    gate_prob,
    w_down,
    hidden_saved,
):
    inputs = scan_input.astype(jnp.float32)
    steps = step_size.astype(jnp.float32)
    grads = scan_grad.astype(jnp.float32)
    bmats = input_proj.T
    cmats = output_proj.T
    first_state = block_states[0]
    decays = jnp.exp(-steps[:, None, :] * decay_rate[None])
    driving = (steps * inputs)[:, None, :] * bmats[:, :, None]
    sources = cmats[:, :, None] * grads[:, None, :]
    states, seed = local_scans(decays, driving, sources, first_state)
    before = jnp.concatenate([first_state[None], states[:-1]], axis=0)
    out_cols = jnp.sum(states * grads[:, None, :], axis=2)
    shrink = jnp.exp(-decay_rate * jnp.sum(steps, axis=0)[None])
    position = lax.axis_index("ctx")
    count = lax.axis_size("ctx")
    is_last = position == count - 1
    pair = jnp.stack(
        [jnp.where(is_last, 0.0, shrink), jnp.where(is_last, shrink * end_grad + seed, seed)]
    )
    distance = 1
    while distance < count:
        later = shifted_from(pair, "ctx", distance)
        present = position + distance < count
        composed = jnp.stack([pair[0] * later[0], pair[0] * later[1] + pair[1]])
        pair = jnp.where(present, composed, pair)
        distance *= 2
    entering = jnp.where(is_last, end_grad, shifted_from(pair[1], "ctx", 1))
    adjoint = adjoint_scan(decays, sources, entering)
    input_grad = (
        steps * jnp.sum(bmats[:, :, None] * adjoint, axis=1) + skip_gain[None] * grads
    ).astype(jnp.bfloat16)
    step_grad = jnp.sum(
        adjoint * (bmats[:, :, None] * inputs[:, None, :] - decay_rate[None] * decays * before),
        axis=1,
    ).astype(jnp.bfloat16)
    in_cols = jnp.sum(adjoint * (steps * inputs)[:, None, :], axis=2)
    rate_local = jnp.sum(adjoint * (-steps[:, None, :] * decays * before), axis=0)
    in_proj_grad, out_proj_grad = butterfly_sum((in_cols.T, out_cols.T), "exp")
    decay_grad = butterfly_sum(rate_local, "ctx")
    slot_total = hidden_saved.shape[1]
    capacity = slot_total // (lax.axis_size("ctx") * lax.axis_size("exp"))
    buffer = slot_buffer(moe_grad, route, gate_prob, capacity)
    received_rows = lax.all_to_all(buffer, "exp", split_axis=0, concat_axis=1, tiled=True)
    all_rows = lax.all_gather(received_rows, "ctx", axis=1, tiled=True)
    weight_total = jnp.einsum(
        "lrf,lrd->lfd", hidden_saved, all_rows, preferred_element_type=jnp.float32
    )
    hidden_grad = jnp.einsum(
        "lrd,lfd->lrf", all_rows, w_down, preferred_element_type=jnp.float32
    ).astype(jnp.bfloat16)
    down_grad = weight_total.astype(jnp.bfloat16)
    return (input_grad, step_grad, in_proj_grad, out_proj_grad, decay_grad, down_grad, hidden_grad)


def solution(mesh):
    placed = (
        P("ctx", "exp"),
        P("ctx", "exp"),
        P(None, "exp"),
        P(None, "ctx"),
        P(None, "ctx"),
        P("exp"),
        P("ctx", None, "exp"),
        P(None, "exp"),
        P("ctx", "exp"),
        P(("ctx", "exp"), None),
        P(("ctx", "exp"), None),
        P(("ctx", "exp"), None),
        P("exp", "ctx", None),
        P("exp", None, "ctx"),
    )
    return jax.shard_map(
        body,
        mesh=mesh,
        in_specs=placed,
        out_specs=(
            P("ctx", "exp"),
            P("ctx", "exp"),
            P(None, "ctx"),
            P(None, "ctx"),
            P(None, "exp"),
            P("exp", "ctx", None),
            P("exp", None, "ctx"),
        ),
        check_vma=False,
    )
```

profile of v0, /device:TPU:2, one launch (start us, length us, event | category | flops | bytes accessed | tf_op | source)
XLA Modules:
  0.0 183.6 jit_solution(15907296854666320743)
XLA Ops:
  7.2 0.0 copy-start
  7.2 0.0 all-gather.2.cloned.1.call-start
  7.3 0.9 copy.31
  8.2 0.1 reshape.62
  8.2 0.1 fusion.33
  8.4 0.2 select_reduce_fusion
  8.5 0.9 mul.225
  9.5 0.2 mul.226
  9.7 0.8 copy.32
  10.4 0.1 mul.223
  10.5 0.3 convolution_convert_fusion
  10.9 0.2 reshape.63
  11.0 0.0 copy-start.2
  11.1 15.2 %all_to_all.12 = bf16[16,2,4096]{2,1,0:T(2,128)(2,1)S(1)} all-to-all(bf16[16,2,4096]{2,1,0:T(2,128)(2,1)S(1)} %reshape.63), channel_id=1, replica_groups=mesh['ctx'=32,'exp'=16] {'exp'}, dimensions={0} | all-to-all | bytes 524288 | tf_op jit(solution)/shard_map/all_to_all | solution.py:157
  26.3 0.8 all_to_all.10
  27.1 0.0 all-gather.2.cloned.1.call-update
  27.1 0.1 copy.29
  27.2 0.1 copy.30
  27.4 1.7 broadcast_multiply_fusion.1.source_ref
  29.1 2.5 %multiply_exponential_fusion = (f32[128,16,256]{2,1,0:T(8,128)}, f32[128,16,256]{2,1,0:T(8,128)}) fusion(f32[16,256]{1,0:T(8,128)S(1)} %copy-done.2, f32[128,256]{1,0:T(8,128)S(1)} %get-tuple-element.32, f32[128,16]{1,0:T(8,128)S(1)} %copy.29, f32[128,256]{1,0:T(8,128)S(1)} %get-tuple-element.31), kind=kLoop, calls=%fused_computation.13 | loop fusion | flops 1048576 | bytes 4481024 | tf_op jit(solution)/shard_map/exp | solution.py:121
  31.6 4.9 %shard_map.189 = (f32[128,16,256]{2,1,0:T(8,128)}, f32[16,256]{1,0:T(8,128)}) custom-call(f32[128,16,256]{2,1,0:T(8,128)} %get-tuple-element.37.decay_ref, f32[128,16,256]{2,1,0:T(8,128)} %get-tuple-element.38.drive_ref, f32[128,16,256]{2,1,0:T(8,128)} %broadcast_multiply_fusion.1.source_ref, f32[16,256]{1,0:T(8,128)} %bitcast.62), custom_call_target="tpu_custom_call" | custom-call | flops 2097152 | bytes 8388608 | tf_op jit(solution)/shard_map/pallas_call | solution.py:44
  36.5 0.7 select_bitcast_fusion
  37.3 1.3 collective-permute-start
  38.6 1.8 collective-permute-done
  40.4 0.7 fusion.32
  41.1 1.3 collective-permute-start.1
  42.4 5.3 %collective-permute-done.1 = f32[2,16,256]{2,1,0:T(8,128)S(1)} collective-permute-done((f32[2,16,256]{2,1,0:T(8,128)S(1)}, f32[2,16,256]{2,1,0:T(8,128)S(1)}, u32[]{:S(2)}, u32[]{:S(2)}) %collective-permute-start.1) | collective-permute-done | bytes 32800 | tf_op jit(solution)/shard_map/ppermute | solution.py:13
  47.7 1.3 collective-permute-start.2
  49.0 5.9 %collective-permute-done.2 = f32[2,16,256]{2,1,0:T(8,128)S(1)} collective-permute-done((f32[2,16,256]{2,1,0:T(8,128)S(1)}, f32[2,16,256]{2,1,0:T(8,128)S(1)}, u32[]{:S(2)}, u32[]{:S(2)}) %collective-permute-start.2) | collective-permute-done | bytes 32800 | tf_op jit(solution)/shard_map/ppermute | solution.py:13
  54.9 1.3 collective-permute-start.3
  56.2 9.5 %collective-permute-done.3 = f32[2,16,256]{2,1,0:T(8,128)S(1)} collective-permute-done((f32[2,16,256]{2,1,0:T(8,128)S(1)}, f32[2,16,256]{2,1,0:T(8,128)S(1)}, u32[]{:S(2)}, u32[]{:S(2)}) %collective-permute-start.3) | collective-permute-done | bytes 32800 | tf_op jit(solution)/shard_map/ppermute | solution.py:13
  65.7 1.3 collective-permute-start.4
  67.0 16.3 %collective-permute-done.4 = f32[2,16,256]{2,1,0:T(8,128)S(1)} collective-permute-done((f32[2,16,256]{2,1,0:T(8,128)S(1)}, f32[2,16,256]{2,1,0:T(8,128)S(1)}, u32[]{:S(2)}, u32[]{:S(2)}) %collective-permute-start.4) | collective-permute-done | bytes 32800 | tf_op jit(solution)/shard_map/ppermute | solution.py:13
  83.3 1.3 collective-permute-start.5
  84.6 3.1 %slice.83 = f32[127,16,256]{2,1,0:T(8,128)} slice(f32[128,16,256]{2,1,0:T(8,128)} %get-tuple-element.10), slice={[0:127], [0:16], [0:256]} | slice | bytes 4161536 | tf_op jit(solution)/shard_map/slice | solution.py:125
  87.7 0.6 broadcast_select_fusion.entering_ref
  88.4 4.0 %shard_map.190 = f32[128,16,256]{2,1,0:T(8,128)} custom-call(f32[128,16,256]{2,1,0:T(8,128)} %get-tuple-element.37.decay_ref, f32[128,16,256]{2,1,0:T(8,128)} %broadcast_multiply_fusion.1.source_ref, f32[16,256]{1,0:T(8,128)} %broadcast_select_fusion.entering_ref), custom_call_target="tpu_custom_call" | custom-call | flops 1048576 | bytes 6291456 | tf_op jit(solution)/shard_map/pallas_call | solution.py:69
  92.3 4.3 %multiply_reduce_fusion = (f32[16,256]{1,0:T(8,128)S(1)}, bf16[128,256]{1,0:T(8,128)(2,1)}, f32[128,256]{1,0:T(8,128)S(1)}, f32[128,16]{1,0:T(8,128)S(1)}) fusion(f32[128,16,256]{2,1,0:T(8,128)} %shard_map.190, f32[127,16,256]{2,1,0:T(8,128)} %slice.83, f32[1,16,256]{2,1,0:T(8,128)S(1)} %copy-done.7, f32[16,256]{1,0:T(8,128)S(1)} %copy-done.2, ...), kind=kLoop, calls=%fused_computation.8 | loop fusion | flops 8316928 | bytes 4833280 | tf_op jit(solution)/shard_map/reduce_sum | solution.py:151
  96.6 3.1 %collective-permute-start.14 = (f32[16,256]{1,0:T(8,128)S(1)}, f32[16,256]{1,0:T(8,128)S(1)}, u32[]{:S(2)}, u32[]{:S(2)}) collective-permute-start(f32[16,256]{1,0:T(8,128)S(1)} %get-tuple-element.18), channel_id=1, source_target_pairs={{0,16},{16,0},{32,48},{48,32},{64,80},{80,64},{96,112},{112,96},{1... | collective-permute-start | bytes 49160 | tf_op jit(solution)/shard_map/ppermute | solution.py:21
  99.7 0.4 multiply_reduce_fusion.1
  100.1 1.9 %collective-permute-start.10 = (f32[16,128]{0,1:T(8,128)S(1)}, f32[16,128]{0,1:T(8,128)S(1)}, u32[]{:S(2)}, u32[]{:S(2)}) collective-permute-start(f32[16,128]{0,1:T(8,128)S(1)} %bitcast.61), channel_id=1, source_target_pairs={{0,1},{1,0},{2,3},{3,2},{4,5},{5,4},{6,7},{7,6},{8,9},{9,8},{10,11... | collective-permute-start | bytes 24584 | tf_op jit(solution)/shard_map/ppermute | solution.py:21
  102.1 0.0 collective-permute-done.14
  102.1 4.0 %collective-permute-start.15 = (f32[16,256]{1,0:T(8,128)S(1)}, f32[16,256]{1,0:T(8,128)S(1)}, u32[]{:S(2)}, u32[]{:S(2)}) collective-permute-start(f32[16,256]{1,0:T(8,128)S(1)} %add.106), channel_id=1, source_target_pairs={{0,32},{16,48},{32,0},{48,16},{64,96},{80,112},{96,64},{112,80},{1... | collective-permute-start | bytes 49160 | tf_op jit(solution)/shard_map/ppermute | solution.py:21
  106.1 0.2 collective-permute-done.10
  106.3 4.3 %collective-permute-start.11 = (f32[16,128]{0,1:T(8,128)S(1)}, f32[16,128]{0,1:T(8,128)S(1)}, u32[]{:S(2)}, u32[]{:S(2)}) collective-permute-start(f32[16,128]{0,1:T(8,128)S(1)} %bitcast_add_fusion), channel_id=1, source_target_pairs={{0,2},{1,3},{2,0},{3,1},{4,6},{5,7},{6,4},{7,5},{8,10},{9,11},{10,... | collective-permute-start | bytes 24584 | tf_op jit(solution)/shard_map/ppermute | solution.py:21
  110.6 1.9 %collective-permute-start.6 = (f32[16,128]{0,1:T(8,128)S(1)}, f32[16,128]{0,1:T(8,128)S(1)}, u32[]{:S(2)}, u32[]{:S(2)}) collective-permute-start(f32[16,128]{0,1:T(8,128)S(1)} %bitcast.60), channel_id=1, source_target_pairs={{0,1},{1,0},{2,3},{3,2},{4,5},{5,4},{6,7},{7,6},{8,9},{9,8},{10,11... | collective-permute-start | bytes 24584 | tf_op jit(solution)/shard_map/ppermute | solution.py:21
  112.6 1.4 collective-permute-done.11
  114.0 4.4 %collective-permute-start.12 = (f32[16,128]{0,1:T(8,128)S(1)}, f32[16,128]{0,1:T(8,128)S(1)}, u32[]{:S(2)}, u32[]{:S(2)}) collective-permute-start(f32[16,128]{0,1:T(8,128)S(1)} %add.103), channel_id=1, source_target_pairs={{0,4},{1,5},{2,6},{3,7},{4,0},{5,1},{6,2},{7,3},{8,12},{9,13},{10,... | collective-permute-start | bytes 24584 | tf_op jit(solution)/shard_map/ppermute | solution.py:21
  118.4 0.0 collective-permute-done.15
  118.4 6.2 %collective-permute-start.16 = (f32[16,256]{1,0:T(8,128)S(1)}, f32[16,256]{1,0:T(8,128)S(1)}, u32[]{:S(2)}, u32[]{:S(2)}) collective-permute-start(f32[16,256]{1,0:T(8,128)S(1)} %add.107), channel_id=1, source_target_pairs={{0,64},{16,80},{32,96},{48,112},{64,0},{80,16},{96,32},{112,48},{1... | collective-permute-start | bytes 49160 | tf_op jit(solution)/shard_map/ppermute | solution.py:21
  124.6 4.2 %collective-permute-start.7 = (f32[16,128]{0,1:T(8,128)S(1)}, f32[16,128]{0,1:T(8,128)S(1)}, u32[]{:S(2)}, u32[]{:S(2)}) collective-permute-start(f32[16,128]{0,1:T(8,128)S(1)} %bitcast_add_fusion.1), channel_id=1, source_target_pairs={{0,2},{1,3},{2,0},{3,1},{4,6},{5,7},{6,4},{7,5},{8,10},{9,11},{10,... | collective-permute-start | bytes 24584 | tf_op jit(solution)/shard_map/ppermute | solution.py:21
  128.9 8.9 %collective-permute-start.17 = (f32[16,256]{1,0:T(8,128)S(1)}, f32[16,256]{1,0:T(8,128)S(1)}, u32[]{:S(2)}, u32[]{:S(2)}) collective-permute-start(f32[16,256]{1,0:T(8,128)S(1)} %add.108), channel_id=1, source_target_pairs={{0,128},{16,144},{32,160},{48,176},{64,192},{80,208},{96,224},{112... | collective-permute-start | bytes 49160 | tf_op jit(solution)/shard_map/ppermute | solution.py:21
  137.9 1.9 %collective-permute-start.13 = (f32[16,128]{0,1:T(8,128)S(1)}, f32[16,128]{0,1:T(8,128)S(1)}, u32[]{:S(2)}, u32[]{:S(2)}) collective-permute-start(f32[16,128]{0,1:T(8,128)S(1)} %add.104), channel_id=1, source_target_pairs={{0,8},{1,9},{2,10},{3,11},{4,12},{5,13},{6,14},{7,15},{8,0},{9,1},... | collective-permute-start | bytes 24584 | tf_op jit(solution)/shard_map/ppermute | solution.py:21
  139.8 3.9 %collective-permute-start.8 = (f32[16,128]{0,1:T(8,128)S(1)}, f32[16,128]{0,1:T(8,128)S(1)}, u32[]{:S(2)}, u32[]{:S(2)}) collective-permute-start(f32[16,128]{0,1:T(8,128)S(1)} %add.99), channel_id=1, source_target_pairs={{0,4},{1,5},{2,6},{3,7},{4,0},{5,1},{6,2},{7,3},{8,12},{9,13},{10,... | collective-permute-start | bytes 24584 | tf_op jit(solution)/shard_map/ppermute | solution.py:21
  143.8 1.8 collective-permute-done.13
  145.6 0.7 copy.34
  146.2 5.2 %collective-permute-start.9 = (f32[16,128]{0,1:T(8,128)S(1)}, f32[16,128]{0,1:T(8,128)S(1)}, u32[]{:S(2)}, u32[]{:S(2)}) collective-permute-start(f32[16,128]{0,1:T(8,128)S(1)} %add.100), channel_id=1, source_target_pairs={{0,8},{1,9},{2,10},{3,11},{4,12},{5,13},{6,14},{7,15},{8,0},{9,1},... | collective-permute-start | bytes 24584 | tf_op jit(solution)/shard_map/ppermute | solution.py:21
  151.5 3.2 %collective-permute-start.18 = (f32[16,256]{1,0:T(8,128)S(1)}, f32[16,256]{1,0:T(8,128)S(1)}, u32[]{:S(2)}, u32[]{:S(2)}) collective-permute-start(f32[16,256]{1,0:T(8,128)S(1)} %add.109), channel_id=1, source_target_pairs={{0,256},{16,272},{32,288},{48,304},{64,320},{80,336},{96,352},{112... | collective-permute-start | bytes 49160 | tf_op jit(solution)/shard_map/ppermute | solution.py:21
  154.7 0.7 fusion.23
  155.3 0.7 copy.33
  156.0 9.9 %collective-permute-done.18 = f32[16,256]{1,0:T(8,128)S(1)} collective-permute-done((f32[16,256]{1,0:T(8,128)S(1)}, f32[16,256]{1,0:T(8,128)S(1)}, u32[]{:S(2)}, u32[]{:S(2)}) %collective-permute-start.18) | collective-permute-done | bytes 16416 | tf_op jit(solution)/shard_map/ppermute | solution.py:21
  165.9 0.6 add.110
  166.5 6.8 %fusion.7 = bf16[1,224,4096]{2,1,0:T(8,128)(2,1)} fusion(bf16[1,1024,4096]{2,1,0:T(8,128)(2,1)} %all-gather.2.cloned.1.call-done, bf16[1,1024,224]{1,2,0:T(8,128)(2,1)S(1)} %copy-done.12), kind=kOutput, calls=%fused_computation.5 | convolution fusion | flops 1879965696 | bytes 10682368 | tf_op jit(solution)/shard_map/lrf,lrd->lfd/dot_general | solution.py:159
  173.4 3.4 %fusion.16 = bf16[1,1024,224]{1,2,0:T(8,128)(2,1)} fusion(bf16[1,224,4096]{2,1,0:T(8,128)(2,1)S(1)} %copy-done, bf16[1,1024,4096]{2,1,0:T(8,128)(2,1)S(1)} %copy-done.11), kind=kOutput, calls=%fused_computation.16 | convolution fusion | flops 1879277568 | bytes 10682368 | tf_op jit(solution)/shard_map/lrd,lfd->lrf/dot_general | solution.py:162
  (60 shorter events, 0.4 us)
Async XLA Ops:
  7.2 166.2 %copy-start = (bf16[1,224,4096]{2,1,0:T(8,128)(2,1)S(1)}, bf16[1,224,4096]{2,1,0:T(8,128)(2,1)}, u32[]{:S(2)}) copy-start(bf16[1,224,4096]{2,1,0:T(8,128)(2,1)} %param.26) | copy-start | bytes 5505028
  7.2 19.9 %copy-start.8 = (f32[16,128]{1,0:T(8,128)S(1)}, f32[16,128]{1,0:T(8,128)}, u32[]{:S(2)}) copy-start(f32[16,128]{1,0:T(8,128)} %param.17) | copy-start | bytes 24580
  7.2 20.0 %copy-start.3 = (bf16[128,256]{1,0:T(8,128)(2,1)S(1)}, bf16[128,256]{1,0:T(8,128)(2,1)}, u32[]{:S(2)}) copy-start(bf16[128,256]{1,0:T(8,128)(2,1)} %param.22) | copy-start | bytes 196612
  7.2 20.0 %copy-start.9 = (f32[16,128]{1,0:T(8,128)S(1)}, f32[16,128]{1,0:T(8,128)}, u32[]{:S(2)}) copy-start(f32[16,128]{1,0:T(8,128)} %param.18) | copy-start | bytes 24580
  7.2 20.1 %copy-start.4 = (bf16[128,256]{1,0:T(8,128)(2,1)S(1)}, bf16[128,256]{1,0:T(8,128)(2,1)}, u32[]{:S(2)}) copy-start(bf16[128,256]{1,0:T(8,128)(2,1)} %param.14) | copy-start | bytes 196612
  7.2 20.1 %copy-start.5 = (bf16[128,256]{1,0:T(8,128)(2,1)S(1)}, bf16[128,256]{1,0:T(8,128)(2,1)}, u32[]{:S(2)}) copy-start(bf16[128,256]{1,0:T(8,128)(2,1)} %param.15) | copy-start | bytes 196612
  7.2 159.3 %all-gather.2.cloned.1.call-start = ((), (), s32[]{:S(2)}) async-start(), calls=%async_computation.1 | async-start | bytes 8650752 | tf_op jit(solution)/shard_map/all_gather | solution.py:158
  11.0 18.0 %copy-start.2 = (f32[16,256]{1,0:T(8,128)S(1)}, f32[16,256]{1,0:T(8,128)}, u32[]{:S(2)}) copy-start(f32[16,256]{1,0:T(8,128)} %param.16) | copy-start | bytes 49156
  31.6 4.9 %copy-start.6 = (f32[16,256]{1,0:T(8,128)S(1)}, f32[16,256]{1,0:T(8,128)}, u32[]{:S(2)}) copy-start(f32[16,256]{1,0:T(8,128)} %param.21) | copy-start | bytes 49156
  37.3 3.1 %collective-permute-start = (f32[2,16,256]{2,1,0:T(8,128)S(1)}, f32[2,16,256]{2,1,0:T(8,128)S(1)}, u32[]{:S(2)}, u32[]{:S(2)}) collective-permute-start(f32[2,16,256]{2,1,0:T(8,128)S(1)} %pad_maximum_fusion.1), channel_id=1, source_target_pairs={{16,0},{32,16},{48,32},{64,48},{80,64},{96,80},{112,96},{128,112},... | collective-permute-start | bytes 98312 | tf_op jit(solution)/shard_map/ppermute | solution.py:13
  41.1 6.6 %collective-permute-start.1 = (f32[2,16,256]{2,1,0:T(8,128)S(1)}, f32[2,16,256]{2,1,0:T(8,128)S(1)}, u32[]{:S(2)}, u32[]{:S(2)}) collective-permute-start(f32[2,16,256]{2,1,0:T(8,128)S(1)} %maximum_select_fusion), channel_id=1, source_target_pairs={{32,0},{48,16},{64,32},{80,48},{96,64},{112,80},{128,96},{144,112}... | collective-permute-start | bytes 98312 | tf_op jit(solution)/shard_map/ppermute | solution.py:13
  47.7 7.2 %collective-permute-start.2 = (f32[2,16,256]{2,1,0:T(8,128)S(1)}, f32[2,16,256]{2,1,0:T(8,128)S(1)}, u32[]{:S(2)}, u32[]{:S(2)}) collective-permute-start(f32[2,16,256]{2,1,0:T(8,128)S(1)} %maximum_select_fusion.1), channel_id=1, source_target_pairs={{64,0},{80,16},{96,32},{112,48},{128,64},{144,80},{160,96},{176,11... | collective-permute-start | bytes 98312 | tf_op jit(solution)/shard_map/ppermute | solution.py:13
  54.9 10.8 %collective-permute-start.3 = (f32[2,16,256]{2,1,0:T(8,128)S(1)}, f32[2,16,256]{2,1,0:T(8,128)S(1)}, u32[]{:S(2)}, u32[]{:S(2)}) collective-permute-start(f32[2,16,256]{2,1,0:T(8,128)S(1)} %maximum_select_fusion.2), channel_id=1, source_target_pairs={{128,0},{144,16},{160,32},{176,48},{192,64},{208,80},{224,96},{240... | collective-permute-start | bytes 98312 | tf_op jit(solution)/shard_map/ppermute | solution.py:13
  65.7 17.6 %collective-permute-start.4 = (f32[2,16,256]{2,1,0:T(8,128)S(1)}, f32[2,16,256]{2,1,0:T(8,128)S(1)}, u32[]{:S(2)}, u32[]{:S(2)}) collective-permute-start(f32[2,16,256]{2,1,0:T(8,128)S(1)} %maximum_select_fusion.3), channel_id=1, source_target_pairs={{256,0},{272,16},{288,32},{304,48},{320,64},{336,80},{352,96},{368... | collective-permute-start | bytes 98312 | tf_op jit(solution)/shard_map/ppermute | solution.py:13
  83.3 4.4 %collective-permute-start.5 = (f32[16,256]{1,0:T(8,128)S(1)}, f32[16,256]{1,0:T(8,128)S(1)}, u32[]{:S(2)}, u32[]{:S(2)}) collective-permute-start(f32[16,256]{1,0:T(8,128)S(1)} %fusion.26), channel_id=1, source_target_pairs={{16,0},{32,16},{48,32},{64,48},{80,64},{96,80},{112,96},{128,112},... | collective-permute-start | bytes 49160 | tf_op jit(solution)/shard_map/ppermute | solution.py:13
  88.3 4.0 %copy-start.7 = (f32[1,16,256]{2,1,0:T(8,128)S(1)}, f32[1,16,256]{2,1,0:T(8,128)}, u32[]{:S(2)}) copy-start(f32[1,16,256]{2,1,0:T(8,128)} %param.20) | copy-start | bytes 49156
  92.3 7.4 %copy-start.1 = (f32[128,16,256]{2,1,0:T(8,128)S(1)}, f32[128,16,256]{2,1,0:T(8,128)}, u32[]{:S(2)}) copy-start(f32[128,16,256]{2,1,0:T(8,128)} %get-tuple-element.10) | copy-start | bytes 6291460
  96.6 58.1 %copy-start.10 = (f32[256]{0:T(256)S(1)}, f32[256]{0:T(256)}, u32[]{:S(2)}) copy-start(f32[256]{0:T(256)} %param.19) | copy-start | bytes 3076
  96.6 69.9 %copy-start.12 = (bf16[1,1024,224]{1,2,0:T(8,128)(2,1)S(1)}, bf16[1,1024,224]{1,2,0:T(8,128)(2,1)}, u32[]{:S(2)}) copy-start(bf16[1,1024,224]{1,2,0:T(8,128)(2,1)} %param.27) | copy-start | bytes 1376260
  96.6 5.5 %collective-permute-start.14 = (f32[16,256]{1,0:T(8,128)S(1)}, f32[16,256]{1,0:T(8,128)S(1)}, u32[]{:S(2)}, u32[]{:S(2)}) collective-permute-start(f32[16,256]{1,0:T(8,128)S(1)} %get-tuple-element.18), channel_id=1, source_target_pairs={{0,16},{16,0},{32,48},{48,32},{64,80},{80,64},{96,112},{112,96},{1... | collective-permute-start | bytes 49160 | tf_op jit(solution)/shard_map/ppermute | solution.py:21
  100.1 6.2 %collective-permute-start.10 = (f32[16,128]{0,1:T(8,128)S(1)}, f32[16,128]{0,1:T(8,128)S(1)}, u32[]{:S(2)}, u32[]{:S(2)}) collective-permute-start(f32[16,128]{0,1:T(8,128)S(1)} %bitcast.61), channel_id=1, source_target_pairs={{0,1},{1,0},{2,3},{3,2},{4,5},{5,4},{6,7},{7,6},{8,9},{9,8},{10,11... | collective-permute-start | bytes 24584 | tf_op jit(solution)/shard_map/ppermute | solution.py:21
  102.1 16.3 %collective-permute-start.15 = (f32[16,256]{1,0:T(8,128)S(1)}, f32[16,256]{1,0:T(8,128)S(1)}, u32[]{:S(2)}, u32[]{:S(2)}) collective-permute-start(f32[16,256]{1,0:T(8,128)S(1)} %add.106), channel_id=1, source_target_pairs={{0,32},{16,48},{32,0},{48,16},{64,96},{80,112},{96,64},{112,80},{1... | collective-permute-start | bytes 49160 | tf_op jit(solution)/shard_map/ppermute | solution.py:21
  106.3 7.7 %collective-permute-start.11 = (f32[16,128]{0,1:T(8,128)S(1)}, f32[16,128]{0,1:T(8,128)S(1)}, u32[]{:S(2)}, u32[]{:S(2)}) collective-permute-start(f32[16,128]{0,1:T(8,128)S(1)} %bitcast_add_fusion), channel_id=1, source_target_pairs={{0,2},{1,3},{2,0},{3,1},{4,6},{5,7},{6,4},{7,5},{8,10},{9,11},{10,... | collective-permute-start | bytes 24584 | tf_op jit(solution)/shard_map/ppermute | solution.py:21
  110.6 14.0 %collective-permute-start.6 = (f32[16,128]{0,1:T(8,128)S(1)}, f32[16,128]{0,1:T(8,128)S(1)}, u32[]{:S(2)}, u32[]{:S(2)}) collective-permute-start(f32[16,128]{0,1:T(8,128)S(1)} %bitcast.60), channel_id=1, source_target_pairs={{0,1},{1,0},{2,3},{3,2},{4,5},{5,4},{6,7},{7,6},{8,9},{9,8},{10,11... | collective-permute-start | bytes 24584 | tf_op jit(solution)/shard_map/ppermute | solution.py:21
  114.0 23.9 %collective-permute-start.12 = (f32[16,128]{0,1:T(8,128)S(1)}, f32[16,128]{0,1:T(8,128)S(1)}, u32[]{:S(2)}, u32[]{:S(2)}) collective-permute-start(f32[16,128]{0,1:T(8,128)S(1)} %add.103), channel_id=1, source_target_pairs={{0,4},{1,5},{2,6},{3,7},{4,0},{5,1},{6,2},{7,3},{8,12},{9,13},{10,... | collective-permute-start | bytes 24584 | tf_op jit(solution)/shard_map/ppermute | solution.py:21
  118.4 10.5 %collective-permute-start.16 = (f32[16,256]{1,0:T(8,128)S(1)}, f32[16,256]{1,0:T(8,128)S(1)}, u32[]{:S(2)}, u32[]{:S(2)}) collective-permute-start(f32[16,256]{1,0:T(8,128)S(1)} %add.107), channel_id=1, source_target_pairs={{0,64},{16,80},{32,96},{48,112},{64,0},{80,16},{96,32},{112,48},{1... | collective-permute-start | bytes 49160 | tf_op jit(solution)/shard_map/ppermute | solution.py:21
  124.6 15.2 %collective-permute-start.7 = (f32[16,128]{0,1:T(8,128)S(1)}, f32[16,128]{0,1:T(8,128)S(1)}, u32[]{:S(2)}, u32[]{:S(2)}) collective-permute-start(f32[16,128]{0,1:T(8,128)S(1)} %bitcast_add_fusion.1), channel_id=1, source_target_pairs={{0,2},{1,3},{2,0},{3,1},{4,6},{5,7},{6,4},{7,5},{8,10},{9,11},{10,... | collective-permute-start | bytes 24584 | tf_op jit(solution)/shard_map/ppermute | solution.py:21
  128.9 22.5 %collective-permute-start.17 = (f32[16,256]{1,0:T(8,128)S(1)}, f32[16,256]{1,0:T(8,128)S(1)}, u32[]{:S(2)}, u32[]{:S(2)}) collective-permute-start(f32[16,256]{1,0:T(8,128)S(1)} %add.108), channel_id=1, source_target_pairs={{0,128},{16,144},{32,160},{48,176},{64,192},{80,208},{96,224},{112... | collective-permute-start | bytes 49160 | tf_op jit(solution)/shard_map/ppermute | solution.py:21
  137.9 7.7 %collective-permute-start.13 = (f32[16,128]{0,1:T(8,128)S(1)}, f32[16,128]{0,1:T(8,128)S(1)}, u32[]{:S(2)}, u32[]{:S(2)}) collective-permute-start(f32[16,128]{0,1:T(8,128)S(1)} %add.104), channel_id=1, source_target_pairs={{0,8},{1,9},{2,10},{3,11},{4,12},{5,13},{6,14},{7,15},{8,0},{9,1},... | collective-permute-start | bytes 24584 | tf_op jit(solution)/shard_map/ppermute | solution.py:21
  139.8 6.4 %collective-permute-start.8 = (f32[16,128]{0,1:T(8,128)S(1)}, f32[16,128]{0,1:T(8,128)S(1)}, u32[]{:S(2)}, u32[]{:S(2)}) collective-permute-start(f32[16,128]{0,1:T(8,128)S(1)} %add.99), channel_id=1, source_target_pairs={{0,4},{1,5},{2,6},{3,7},{4,0},{5,1},{6,2},{7,3},{8,12},{9,13},{10,... | collective-permute-start | bytes 24584 | tf_op jit(solution)/shard_map/ppermute | solution.py:21
  146.2 9.1 %collective-permute-start.9 = (f32[16,128]{0,1:T(8,128)S(1)}, f32[16,128]{0,1:T(8,128)S(1)}, u32[]{:S(2)}, u32[]{:S(2)}) collective-permute-start(f32[16,128]{0,1:T(8,128)S(1)} %add.100), channel_id=1, source_target_pairs={{0,8},{1,9},{2,10},{3,11},{4,12},{5,13},{6,14},{7,15},{8,0},{9,1},... | collective-permute-start | bytes 24584 | tf_op jit(solution)/shard_map/ppermute | solution.py:21
  151.5 14.5 %collective-permute-start.18 = (f32[16,256]{1,0:T(8,128)S(1)}, f32[16,256]{1,0:T(8,128)S(1)}, u32[]{:S(2)}, u32[]{:S(2)}) collective-permute-start(f32[16,256]{1,0:T(8,128)S(1)} %add.109), channel_id=1, source_target_pairs={{0,256},{16,272},{32,288},{48,304},{64,320},{80,336},{96,352},{112... | collective-permute-start | bytes 49160 | tf_op jit(solution)/shard_map/ppermute | solution.py:21
  166.5 6.8 %copy-start.11 = (bf16[1,1024,4096]{2,1,0:T(8,128)(2,1)S(1)}, bf16[1,1024,4096]{2,1,0:T(8,128)(2,1)}, u32[]{:S(2)}) copy-start(bf16[1,1024,4096]{2,1,0:T(8,128)(2,1)} %all-gather.2.cloned.1.call-done) | copy-start | bytes 25165828
Sparse Core Ops, SparseCore 0:
  27.2 84.6 all-gather.1
where the time goes:
time: 185 us; the launch traced here: 184 us
  starting transfers between devices  61.1 us (33%)
  waiting for transfers between devices  52 us (28%)
  blocking collectives  15.2 us (8%)
  between operations  14.6 us (8%)
  other arithmetic  12.7 us (7%)
  matrix products  10.6 us (6%)
  Pallas kernels  8.88 us (5%)
  local copies, waits for them, and re-layouts  8.57 us (5%)
    ppermute x13, starting transfers between devices, butterfly_sum(): lax.ppermute(part, axis, pairs)  53.3 us
    ppermute x6, waiting for transfers between devices, shifted_from(): lax.ppermute(value, axis, [(source, source - distance) for source in rang...  38.7 us
    all_to_all x1, blocking collectives, body(): lax.all_to_all(buffer, 'exp', split_axis=0, concat_axis=1, tiled=True)  15.2 us
    ppermute x13, waiting for transfers between devices, butterfly_sum(): lax.ppermute(part, axis, pairs)  13.3 us
    ppermute x6, starting transfers between devices, shifted_from(): lax.ppermute(value, axis, [(source, source - distance) for source in rang...  7.75 us
    dot_general x1, matrix products, body(): jnp.einsum('lrf,lrd->lfd', hidden_saved, all_rows, preferred_element_type...  6.83 us
    pallas_call x1, Pallas kernels, local_scans(): pl.pallas_call(local_scans_kernel, out_shape=(jax.ShapeDtypeStruct(decays...  4.92 us
    reduce_sum x1, other arithmetic, body(): jnp.sum(adjoint * (-steps[:, None, :] * decays * before), axis=0)  4.27 us
  transfers between devices with their start and end apart: 20, of which 9 were waited for; matrix products, arithmetic and copies ran while one was open for 9% of the time, Pallas kernels for 5%

commit v1 on v0

--- a/solution.py
+++ b/solution.py
@@ -1,3 +1,5 @@
+import functools
+
 import jax
 import jax.numpy as jnp
 from jax import lax
@@ -13,16 +15,6 @@
     return lax.ppermute(value, axis, [(source, source - distance) for source in range(distance, count)])
 
 
-def butterfly_sum(value, axis):
-    count = lax.axis_size(axis)
-    distance = 1
-    while distance < count:
-        pairs = [(source, source ^ distance) for source in range(count)]
-        value = jax.tree.map(lambda part: part + lax.ppermute(part, axis, pairs), value)
-        distance *= 2
-    return value
-
-
 def local_scans_kernel(decay_ref, drive_ref, source_ref, first_ref, states_ref, seed_ref):
     count = decay_ref.shape[0]
 
@@ -73,6 +65,51 @@
             flops=2 * decays.size, bytes_accessed=12 * decays.size, transcendentals=0
         ),
     )(decays, sources, entering)
+
+
+def exchange_kernel(axis, count, same, x_ref, out_ref, land, send_sems, recv_sems):
+    me = lax.axis_index(axis)
+    barrier = pltpu.get_barrier_semaphore()
+    for k in range(1, count):
+        pl.semaphore_signal(
+            barrier,
+            1,
+            device_id={axis: lax.rem(me + k, count)},
+            device_id_type=pl.DeviceIdType.MESH,
+        )
+    pl.semaphore_wait(barrier, count - 1)
+    copies = []
+    for k in range(1, count):
+        peer = lax.rem(me + k, count)
+        copy = pltpu.make_async_remote_copy(
+            src_ref=x_ref if same else x_ref.at[peer],
+            dst_ref=land.at[me],
+            send_sem=send_sems.at[k],
+            recv_sem=recv_sems.at[k],
+            device_id={axis: peer},
+            device_id_type=pl.DeviceIdType.MESH,
+        )
+        copy.start()
+        copies.append(copy)
+    land[me] = x_ref[...] if same else x_ref[me]
+    for copy in copies:
+        copy.wait()
+    out_ref[...] = land[...]
+
+
+def exchange(x, axis, same, collective_id):
+    count = lax.axis_size(axis)
+    block = x.shape if same else x.shape[1:]
+    return pl.pallas_call(
+        functools.partial(exchange_kernel, axis, count, same),
+        out_shape=jax.ShapeDtypeStruct((count,) + block, x.dtype),
+        scratch_shapes=[
+            pltpu.VMEM((count,) + block, x.dtype),
+            pltpu.SemaphoreType.DMA((count,)),
+            pltpu.SemaphoreType.DMA((count,)),
+        ],
+        compiler_params=pltpu.CompilerParams(collective_id=collective_id, has_side_effects=True),
+    )(x)
 
 
 def slot_buffer(moe_grad, route, gate_prob, capacity):
@@ -149,8 +186,12 @@
     ).astype(jnp.bfloat16)
     in_cols = jnp.sum(adjoint * (steps * inputs)[:, None, :], axis=2)
     rate_local = jnp.sum(adjoint * (-steps[:, None, :] * decays * before), axis=0)
-    in_proj_grad, out_proj_grad = butterfly_sum((in_cols.T, out_cols.T), "exp")
-    decay_grad = butterfly_sum(rate_local, "ctx")
+    col_sums = jnp.sum(exchange(jnp.stack([in_cols.T, out_cols.T]), "exp", True, 1), axis=0)
+    in_proj_grad, out_proj_grad = col_sums[0], col_sums[1]
+    ctx_count = lax.axis_size("ctx")
+    rate_parts = rate_local.reshape(ctx_count, 1, rate_local.size // ctx_count)
+    rate_chunk = jnp.sum(exchange(rate_parts, "ctx", False, 2), axis=0)
+    decay_grad = exchange(rate_chunk, "ctx", True, 3).reshape(rate_local.shape)
     slot_total = hidden_saved.shape[1]
     capacity = slot_total // (lax.axis_size("ctx") * lax.axis_size("exp"))
     buffer = slot_buffer(moe_grad, route, gate_prob, capacity)

time: 185 us -> 171 us (0.924)
  the two profiles are of different devices: /device:TPU:2 before, /device:TPU:1 now
where the time goes in v1:
time: 171 us; the launch traced here: 170 us
  Pallas kernels  54.4 us (32%)
  waiting for transfers between devices  34.2 us (20%)
  other arithmetic  17.9 us (10%)
  starting transfers between devices  15.6 us (9%)
  blocking collectives  14.8 us (9%)
  between operations  14.4 us (8%)
  matrix products  10.6 us (6%)
  local copies, waits for them, and re-layouts  8.09 us (5%)
    pallas_call x3, Pallas kernels, exchange(): pl.pallas_call(functools.partial(exchange_kernel, axis, count, same), out...  45.5 us
    ppermute x6, waiting for transfers between devices, shifted_from(): lax.ppermute(value, axis, [(source, source - distance) for source in rang...  34.2 us
    ppermute x6, starting transfers between devices, shifted_from(): lax.ppermute(value, axis, [(source, source - distance) for source in rang...  15.6 us
    all_to_all x1, blocking collectives, body(): lax.all_to_all(buffer, 'exp', split_axis=0, concat_axis=1, tiled=True)  14.8 us
    dot_general x1, matrix products, body(): jnp.einsum('lrf,lrd->lfd', hidden_saved, all_rows, preferred_element_type...  6.83 us
    pallas_call x1, Pallas kernels, local_scans(): pl.pallas_call(local_scans_kernel, out_shape=(jax.ShapeDtypeStruct(decays...  4.85 us
    reduce_sum x1, other arithmetic, body(): jnp.sum(adjoint * (-steps[:, None, :] * decays * before), axis=0)  4.16 us
    pallas_call x1, Pallas kernels, adjoint_scan(): pl.pallas_call(adjoint_scan_kernel, out_shape=jax.ShapeDtypeStruct(decays...  3.99 us
  transfers between devices with their start and end apart: 7, of which 5 were waited for; matrix products, arithmetic and copies ran while one was open for 13% of the time, Pallas kernels for 32%

profile of v1, /device:TPU:1, one launch (start us, length us, event | category | flops | bytes accessed | tf_op | source)
XLA Modules:
  0.0 169.9 jit_solution(12886387759044188035)
XLA Ops:
  7.2 0.0 copy-start
  7.2 0.0 copy-start.8
  7.2 0.0 copy-start.3
  7.2 0.0 copy-start.9
  7.2 0.0 copy-start.4
  7.2 0.0 all-gather.2.cloned.1.call-start
  7.3 0.9 copy.33
  8.2 0.1 reshape.71
  8.2 0.1 fusion.33
  8.4 0.2 select_reduce_fusion
  8.5 0.9 mul.225
  9.5 0.2 mul.226
  9.7 0.8 copy.34
  10.4 0.1 mul.223
  10.5 0.3 convolution_convert_fusion
  10.9 0.2 reshape.72
  11.0 0.0 copy-start.2
  11.1 14.8 %all_to_all.12 = bf16[16,2,4096]{2,1,0:T(2,128)(2,1)S(1)} all-to-all(bf16[16,2,4096]{2,1,0:T(2,128)(2,1)S(1)} %reshape.72), channel_id=1, replica_groups=mesh['ctx'=32,'exp'=16] {'exp'}, dimensions={0} | all-to-all | bytes 524288 | tf_op jit(solution)/shard_map/all_to_all | solution.py:198
  25.8 0.8 all_to_all.10
  26.6 0.0 all-gather.2.cloned.1.call-update
  26.6 0.1 copy.29
  26.8 0.1 copy.30
  26.9 1.7 %broadcast_multiply_fusion.1.source_ref = f32[128,16,256]{2,1,0:T(8,128)} fusion(f32[128,256]{1,0:T(8,128)S(1)} %convert_element_type.45, f32[128,16]{1,0:T(8,128)S(1)} %copy.30), kind=kLoop, calls=%fused_computation.18 | loop fusion | flops 524288 | bytes 2236416 | tf_op jit(solution)/shard_map/mul | solution.py:160
  28.7 2.5 %multiply_exponential_fusion = (f32[128,16,256]{2,1,0:T(8,128)}, f32[128,16,256]{2,1,0:T(8,128)}) fusion(f32[16,256]{1,0:T(8,128)S(1)} %copy-done.2, f32[128,256]{1,0:T(8,128)S(1)} %get-tuple-element.25, f32[128,16]{1,0:T(8,128)S(1)} %copy.29, f32[128,256]{1,0:T(8,128)S(1)} %get-tuple-element.24), kind=kLoop, calls=%fused_computation.13 | loop fusion | flops 1048576 | bytes 4481024 | tf_op jit(solution)/shard_map/exp | solution.py:158
  31.2 4.9 %shard_map.189 = (f32[128,16,256]{2,1,0:T(8,128)}, f32[16,256]{1,0:T(8,128)}) custom-call(f32[128,16,256]{2,1,0:T(8,128)} %get-tuple-element.32.decay_ref, f32[128,16,256]{2,1,0:T(8,128)} %get-tuple-element.33.drive_ref, f32[128,16,256]{2,1,0:T(8,128)} %broadcast_multiply_fusion.1.source_ref, f32[16,256]{1,0:T(8,128)} %bitcast.67), custom_call_target="tpu_custom_call" | custom-call | flops 2097152 | bytes 8388608 | tf_op jit(solution)/shard_map/pallas_call | solution.py:36
  36.0 0.7 select_bitcast_fusion
  36.8 5.1 %collective-permute-start = (f32[2,16,256]{2,1,0:T(8,128)S(1)}, f32[2,16,256]{2,1,0:T(8,128)S(1)}, u32[]{:S(2)}, u32[]{:S(2)}) collective-permute-start(f32[2,16,256]{2,1,0:T(8,128)S(1)} %pad_maximum_fusion.1), channel_id=1, source_target_pairs={{16,0},{32,16},{48,32},{64,48},{80,64},{96,80},{112,96},{128,112},... | collective-permute-start | bytes 98312 | tf_op jit(solution)/shard_map/ppermute | solution.py:15
  41.9 2.0 %collective-permute-done = f32[2,16,256]{2,1,0:T(8,128)S(1)} collective-permute-done((f32[2,16,256]{2,1,0:T(8,128)S(1)}, f32[2,16,256]{2,1,0:T(8,128)S(1)}, u32[]{:S(2)}, u32[]{:S(2)}) %collective-permute-start) | collective-permute-done | bytes 32800 | tf_op jit(solution)/shard_map/ppermute | solution.py:15
  43.9 0.7 fusion.32
  44.7 1.3 collective-permute-start.1
  46.0 4.6 %collective-permute-done.1 = f32[2,16,256]{2,1,0:T(8,128)S(1)} collective-permute-done((f32[2,16,256]{2,1,0:T(8,128)S(1)}, f32[2,16,256]{2,1,0:T(8,128)S(1)}, u32[]{:S(2)}, u32[]{:S(2)}) %collective-permute-start.1) | collective-permute-done | bytes 32800 | tf_op jit(solution)/shard_map/ppermute | solution.py:15
  50.6 1.3 collective-permute-start.2
  51.9 5.5 %collective-permute-done.2 = f32[2,16,256]{2,1,0:T(8,128)S(1)} collective-permute-done((f32[2,16,256]{2,1,0:T(8,128)S(1)}, f32[2,16,256]{2,1,0:T(8,128)S(1)}, u32[]{:S(2)}, u32[]{:S(2)}) %collective-permute-start.2) | collective-permute-done | bytes 32800 | tf_op jit(solution)/shard_map/ppermute | solution.py:15
  57.4 1.3 collective-permute-start.3
  58.7 9.6 %collective-permute-done.3 = f32[2,16,256]{2,1,0:T(8,128)S(1)} collective-permute-done((f32[2,16,256]{2,1,0:T(8,128)S(1)}, f32[2,16,256]{2,1,0:T(8,128)S(1)}, u32[]{:S(2)}, u32[]{:S(2)}) %collective-permute-start.3) | collective-permute-done | bytes 32800 | tf_op jit(solution)/shard_map/ppermute | solution.py:15
  68.3 1.3 collective-permute-start.4
  69.6 0.0 copy-start.1
  69.6 12.5 %collective-permute-done.4 = f32[2,16,256]{2,1,0:T(8,128)S(1)} collective-permute-done((f32[2,16,256]{2,1,0:T(8,128)S(1)}, f32[2,16,256]{2,1,0:T(8,128)S(1)}, u32[]{:S(2)}, u32[]{:S(2)}) %collective-permute-start.4) | collective-permute-done | bytes 32800 | tf_op jit(solution)/shard_map/ppermute | solution.py:15
  82.2 5.3 %collective-permute-start.5 = (f32[16,256]{1,0:T(8,128)S(1)}, f32[16,256]{1,0:T(8,128)S(1)}, u32[]{:S(2)}, u32[]{:S(2)}) collective-permute-start(f32[16,256]{1,0:T(8,128)S(1)} %fusion.26), channel_id=1, source_target_pairs={{16,0},{32,16},{48,32},{64,48},{80,64},{96,80},{112,96},{128,112},... | collective-permute-start | bytes 49160 | tf_op jit(solution)/shard_map/ppermute | solution.py:15
  87.5 2.0 %multiply_reduce_fusion.1 = f32[128,16]{1,0:T(8,128)S(1)} fusion(f32[128,16,256]{2,1,0:T(8,128)} %get-tuple-element.10, f32[128,256]{1,0:T(8,128)S(1)} %convert_element_type.45), kind=kLoop, calls=%fused_computation.9 | loop fusion | flops 1046528 | bytes 2236416 | tf_op jit(solution)/shard_map/reduce_sum | solution.py:163
  89.5 0.0 copy-done.1
  89.5 1.5 slice.89
  91.0 0.1 copy.32
  91.1 0.0 collective-permute-done.5
  91.1 0.6 broadcast_select_fusion.entering_ref
  91.7 4.0 %shard_map.190 = f32[128,16,256]{2,1,0:T(8,128)} custom-call(f32[128,16,256]{2,1,0:T(8,128)} %get-tuple-element.32.decay_ref, f32[128,16,256]{2,1,0:T(8,128)} %broadcast_multiply_fusion.1.source_ref, f32[16,256]{1,0:T(8,128)} %broadcast_select_fusion.entering_ref), custom_call_target="tpu_custom_call" | custom-call | flops 1048576 | bytes 6291456 | tf_op jit(solution)/shard_map/pallas_call | solution.py:61
  95.7 4.2 %multiply_reduce_fusion = (f32[16,256]{1,0:T(8,128)S(1)}, bf16[128,256]{1,0:T(8,128)(2,1)}, f32[128,256]{1,0:T(8,128)S(1)}, f32[128,16]{1,0:T(8,128)S(1)}) fusion(f32[128,16,256]{2,1,0:T(8,128)} %shard_map.190, f32[127,16,256]{2,1,0:T(8,128)} %slice.89, f32[1,16,256]{2,1,0:T(8,128)S(1)} %copy-done.7, f32[16,256]{1,0:T(8,128)S(1)} %copy-done.2, ...), kind=kLoop, calls=%fused_computation.8 | loop fusion | flops 8316928 | bytes 4833280 | tf_op jit(solution)/shard_map/reduce_sum | solution.py:188
  99.9 0.6 pad_maximum_fusion.3.x_ref
  100.6 10.6 %shard_map.191 = f32[16,2,16,128]{3,2,1,0:T(8,128)} custom-call(f32[2,16,128]{2,1,0:T(8,128)} %pad_maximum_fusion.3.x_ref), custom_call_target="tpu_custom_call" | custom-call | tf_op jit(solution)/shard_map/pallas_call | solution.py:103
  111.2 0.6 reshape.69.x_ref
  111.8 19.8 %shard_map.192 = f32[32,1,128]{2,1,0:T(1,128)} custom-call(f32[32,1,128]{2,1,0:T(1,128)} %reshape.69.x_ref), custom_call_target="tpu_custom_call" | custom-call | tf_op jit(solution)/shard_map/pallas_call | solution.py:103
  131.6 1.0 reduce_sum.88
  132.6 1.3 reduce_sum.90
  133.9 15.1 %shard_map.193 = f32[32,1,128]{2,1,0:T(1,128)} custom-call(f32[1,128]{1,0:T(1,128)} %bitcast.72), custom_call_target="tpu_custom_call" | custom-call | tf_op jit(solution)/shard_map/pallas_call | solution.py:103
  149.0 0.5 broadcast.29
  149.5 1.4 reduce.4
  150.9 0.6 reshape.70
  151.5 0.6 slice_bitcast_fusion.2
  152.1 0.0 copy-done.10
  152.1 0.7 fusion.23
  152.8 0.0 copy-done.12
  152.8 6.8 %fusion.7 = bf16[1,224,4096]{2,1,0:T(8,128)(2,1)} fusion(bf16[1,1024,4096]{2,1,0:T(8,128)(2,1)} %all-gather.2.cloned.1.call-done, bf16[1,1024,224]{1,2,0:T(8,128)(2,1)S(1)} %copy-done.12), kind=kOutput, calls=%fused_computation.5 | convolution fusion | flops 1879965696 | bytes 10682368 | tf_op jit(solution)/shard_map/lrf,lrd->lfd/dot_general | solution.py:200
  159.6 0.0 copy-done.11
  159.6 3.4 %fusion.16 = bf16[1,1024,224]{1,2,0:T(8,128)(2,1)} fusion(bf16[1,224,4096]{2,1,0:T(8,128)(2,1)S(1)} %copy-done, bf16[1,1024,4096]{2,1,0:T(8,128)(2,1)S(1)} %copy-done.11), kind=kOutput, calls=%fused_computation.16 | convolution fusion | flops 1879277568 | bytes 10682368 | tf_op jit(solution)/shard_map/lrd,lfd->lrf/dot_general | solution.py:203
  (32 shorter events, 0.3 us)
Async XLA Ops:
  7.2 152.5 %copy-start = (bf16[1,224,4096]{2,1,0:T(8,128)(2,1)S(1)}, bf16[1,224,4096]{2,1,0:T(8,128)(2,1)}, u32[]{:S(2)}) copy-start(bf16[1,224,4096]{2,1,0:T(8,128)(2,1)} %param.26) | copy-start | bytes 5505028
  7.2 19.5 %copy-start.8 = (f32[16,128]{1,0:T(8,128)S(1)}, f32[16,128]{1,0:T(8,128)}, u32[]{:S(2)}) copy-start(f32[16,128]{1,0:T(8,128)} %param.17) | copy-start | bytes 24580
  7.2 19.6 %copy-start.3 = (bf16[128,256]{1,0:T(8,128)(2,1)S(1)}, bf16[128,256]{1,0:T(8,128)(2,1)}, u32[]{:S(2)}) copy-start(bf16[128,256]{1,0:T(8,128)(2,1)} %param.22) | copy-start | bytes 196612
  7.2 19.6 %copy-start.9 = (f32[16,128]{1,0:T(8,128)S(1)}, f32[16,128]{1,0:T(8,128)}, u32[]{:S(2)}) copy-start(f32[16,128]{1,0:T(8,128)} %param.18) | copy-start | bytes 24580
  7.2 19.7 %copy-start.4 = (bf16[128,256]{1,0:T(8,128)(2,1)S(1)}, bf16[128,256]{1,0:T(8,128)(2,1)}, u32[]{:S(2)}) copy-start(bf16[128,256]{1,0:T(8,128)(2,1)} %param.14) | copy-start | bytes 196612
  7.2 19.7 %copy-start.5 = (bf16[128,256]{1,0:T(8,128)(2,1)S(1)}, bf16[128,256]{1,0:T(8,128)(2,1)}, u32[]{:S(2)}) copy-start(bf16[128,256]{1,0:T(8,128)(2,1)} %param.15) | copy-start | bytes 196612
  7.2 145.6 %all-gather.2.cloned.1.call-start = ((), (), s32[]{:S(2)}) async-start(), calls=%async_computation.1 | async-start | bytes 8650752 | tf_op jit(solution)/shard_map/all_gather | solution.py:199
  11.0 17.6 %copy-start.2 = (f32[16,256]{1,0:T(8,128)S(1)}, f32[16,256]{1,0:T(8,128)}, u32[]{:S(2)}) copy-start(f32[16,256]{1,0:T(8,128)} %param.16) | copy-start | bytes 49156
  31.2 4.9 %copy-start.6 = (f32[16,256]{1,0:T(8,128)S(1)}, f32[16,256]{1,0:T(8,128)}, u32[]{:S(2)}) copy-start(f32[16,256]{1,0:T(8,128)} %param.21) | copy-start | bytes 49156
  36.8 7.1 %collective-permute-start = (f32[2,16,256]{2,1,0:T(8,128)S(1)}, f32[2,16,256]{2,1,0:T(8,128)S(1)}, u32[]{:S(2)}, u32[]{:S(2)}) collective-permute-start(f32[2,16,256]{2,1,0:T(8,128)S(1)} %pad_maximum_fusion.1), channel_id=1, source_target_pairs={{16,0},{32,16},{48,32},{64,48},{80,64},{96,80},{112,96},{128,112},... | collective-permute-start | bytes 98312 | tf_op jit(solution)/shard_map/ppermute | solution.py:15
  44.7 5.9 %collective-permute-start.1 = (f32[2,16,256]{2,1,0:T(8,128)S(1)}, f32[2,16,256]{2,1,0:T(8,128)S(1)}, u32[]{:S(2)}, u32[]{:S(2)}) collective-permute-start(f32[2,16,256]{2,1,0:T(8,128)S(1)} %maximum_select_fusion), channel_id=1, source_target_pairs={{32,0},{48,16},{64,32},{80,48},{96,64},{112,80},{128,96},{144,112}... | collective-permute-start | bytes 98312 | tf_op jit(solution)/shard_map/ppermute | solution.py:15
  50.6 6.8 %collective-permute-start.2 = (f32[2,16,256]{2,1,0:T(8,128)S(1)}, f32[2,16,256]{2,1,0:T(8,128)S(1)}, u32[]{:S(2)}, u32[]{:S(2)}) collective-permute-start(f32[2,16,256]{2,1,0:T(8,128)S(1)} %maximum_select_fusion.1), channel_id=1, source_target_pairs={{64,0},{80,16},{96,32},{112,48},{128,64},{144,80},{160,96},{176,11... | collective-permute-start | bytes 98312 | tf_op jit(solution)/shard_map/ppermute | solution.py:15
  57.4 10.9 %collective-permute-start.3 = (f32[2,16,256]{2,1,0:T(8,128)S(1)}, f32[2,16,256]{2,1,0:T(8,128)S(1)}, u32[]{:S(2)}, u32[]{:S(2)}) collective-permute-start(f32[2,16,256]{2,1,0:T(8,128)S(1)} %maximum_select_fusion.2), channel_id=1, source_target_pairs={{128,0},{144,16},{160,32},{176,48},{192,64},{208,80},{224,96},{240... | collective-permute-start | bytes 98312 | tf_op jit(solution)/shard_map/ppermute | solution.py:15
  68.3 13.9 %collective-permute-start.4 = (f32[2,16,256]{2,1,0:T(8,128)S(1)}, f32[2,16,256]{2,1,0:T(8,128)S(1)}, u32[]{:S(2)}, u32[]{:S(2)}) collective-permute-start(f32[2,16,256]{2,1,0:T(8,128)S(1)} %maximum_select_fusion.3), channel_id=1, source_target_pairs={{256,0},{272,16},{288,32},{304,48},{320,64},{336,80},{352,96},{368... | collective-permute-start | bytes 98312 | tf_op jit(solution)/shard_map/ppermute | solution.py:15
  69.6 19.9 %copy-start.1 = (f32[128,16,256]{2,1,0:T(8,128)S(1)}, f32[128,16,256]{2,1,0:T(8,128)}, u32[]{:S(2)}) copy-start(f32[128,16,256]{2,1,0:T(8,128)} %get-tuple-element.10) | copy-start | bytes 6291460
  82.2 8.9 %collective-permute-start.5 = (f32[16,256]{1,0:T(8,128)S(1)}, f32[16,256]{1,0:T(8,128)S(1)}, u32[]{:S(2)}, u32[]{:S(2)}) collective-permute-start(f32[16,256]{1,0:T(8,128)S(1)} %fusion.26), channel_id=1, source_target_pairs={{16,0},{32,16},{48,32},{64,48},{80,64},{96,80},{112,96},{128,112},... | collective-permute-start | bytes 49160 | tf_op jit(solution)/shard_map/ppermute | solution.py:15
  91.7 4.0 %copy-start.7 = (f32[1,16,256]{2,1,0:T(8,128)S(1)}, f32[1,16,256]{2,1,0:T(8,128)}, u32[]{:S(2)}) copy-start(f32[1,16,256]{2,1,0:T(8,128)} %param.20) | copy-start | bytes 49156
  95.7 56.4 %copy-start.10 = (f32[256]{0:T(256)S(1)}, f32[256]{0:T(256)}, u32[]{:S(2)}) copy-start(f32[256]{0:T(256)} %param.19) | copy-start | bytes 3076
  95.7 57.1 %copy-start.12 = (bf16[1,1024,224]{1,2,0:T(8,128)(2,1)S(1)}, bf16[1,1024,224]{1,2,0:T(8,128)(2,1)}, u32[]{:S(2)}) copy-start(bf16[1,1024,224]{1,2,0:T(8,128)(2,1)} %param.27) | copy-start | bytes 1376260
  152.8 6.8 %copy-start.11 = (bf16[1,1024,4096]{2,1,0:T(8,128)(2,1)S(1)}, bf16[1,1024,4096]{2,1,0:T(8,128)(2,1)}, u32[]{:S(2)}) copy-start(bf16[1,1024,4096]{2,1,0:T(8,128)(2,1)} %all-gather.2.cloned.1.call-done) | copy-start | bytes 25165828
Sparse Core Ops, SparseCore 0:
  26.8 85.6 all-gather.1

commit v2 on v1

--- a/solution.py
+++ b/solution.py
@@ -8,11 +8,6 @@
 from jax.sharding import PartitionSpec as P
 
 EXPERTS = 16
-
-
-def shifted_from(value, axis, distance):
-    count = lax.axis_size(axis)
-    return lax.ppermute(value, axis, [(source, source - distance) for source in range(distance, count)])
 
 
 def local_scans_kernel(decay_ref, drive_ref, source_ref, first_ref, states_ref, seed_ref):
@@ -105,6 +100,62 @@
         out_shape=jax.ShapeDtypeStruct((count,) + block, x.dtype),
         scratch_shapes=[
             pltpu.VMEM((count,) + block, x.dtype),
+            pltpu.SemaphoreType.DMA((count,)),
+            pltpu.SemaphoreType.DMA((count,)),
+        ],
+        compiler_params=pltpu.CompilerParams(collective_id=collective_id, has_side_effects=True),
+    )(x)
+
+
+def relay_kernel(axis, count, x_ref, out_ref, land, send_sems, recv_sems):
+    me = lax.axis_index(axis)
+    land[...] = jnp.zeros_like(land)
+    barrier = pltpu.get_barrier_semaphore()
+    for k in range(1, count):
+        pl.semaphore_signal(
+            barrier,
+            1,
+            device_id={axis: lax.rem(me + k, count)},
+            device_id_type=pl.DeviceIdType.MESH,
+        )
+    pl.semaphore_wait(barrier, count - 1)
+    copies = []
+    for k in range(1, count):
+        copy = pltpu.make_async_remote_copy(
+            src_ref=x_ref,
+            dst_ref=land.at[me],
+            send_sem=send_sems.at[k],
+            recv_sem=recv_sems.at[k],
+            device_id={axis: lax.rem(me - k + count, count)},
+            device_id_type=pl.DeviceIdType.MESH,
+        )
+        copies.append(copy)
+
+        @pl.when(me >= k)
+        def _():
+            copy.start()
+
+    land[me] = x_ref[...]
+    for k, copy in enumerate(copies, start=1):
+
+        @pl.when(me >= k)
+        def _():
+            copy.wait_send()
+
+        @pl.when(me + k < count)
+        def _():
+            copy.wait_recv()
+
+    out_ref[...] = land[...]
+
+
+def relay_exchange(x, axis, collective_id):
+    count = lax.axis_size(axis)
+    return pl.pallas_call(
+        functools.partial(relay_kernel, axis, count),
+        out_shape=jax.ShapeDtypeStruct((count,) + x.shape, x.dtype),
+        scratch_shapes=[
+            pltpu.VMEM((count,) + x.shape, x.dtype),
             pltpu.SemaphoreType.DMA((count,)),
             pltpu.SemaphoreType.DMA((count,)),
         ],
@@ -161,21 +212,21 @@
     states, seed = local_scans(decays, driving, sources, first_state)
     before = jnp.concatenate([first_state[None], states[:-1]], axis=0)
     out_cols = jnp.sum(states * grads[:, None, :], axis=2)
-    shrink = jnp.exp(-decay_rate * jnp.sum(steps, axis=0)[None])
+    step_totals = jnp.sum(steps, axis=0)
+    shrink = jnp.exp(-decay_rate * step_totals[None])
     position = lax.axis_index("ctx")
     count = lax.axis_size("ctx")
     is_last = position == count - 1
-    pair = jnp.stack(
-        [jnp.where(is_last, 0.0, shrink), jnp.where(is_last, shrink * end_grad + seed, seed)]
-    )
-    distance = 1
-    while distance < count:
-        later = shifted_from(pair, "ctx", distance)
-        present = position + distance < count
-        composed = jnp.stack([pair[0] * later[0], pair[0] * later[1] + pair[1]])
-        pair = jnp.where(present, composed, pair)
-        distance *= 2
-    entering = jnp.where(is_last, end_grad, shifted_from(pair[1], "ctx", 1))
+    outgoing = jnp.where(is_last, shrink * end_grad + seed, seed)
+    gathered = relay_exchange(
+        jnp.concatenate([outgoing, step_totals[None]], axis=0), "ctx", 4
+    )
+    running = gathered[count - 1, :-1]
+    for later in range(count - 2, 0, -1):
+        block_shrink = jnp.exp(-decay_rate * gathered[later, -1][None])
+        composed = block_shrink * running + gathered[later, :-1]
+        running = jnp.where(later > position, composed, running)
+    entering = jnp.where(is_last, end_grad, running)
     adjoint = adjoint_scan(decays, sources, entering)
     input_grad = (
         steps * jnp.sum(bmats[:, :, None] * adjoint, axis=1) + skip_gain[None] * grads

time: 171 us -> 183 us (1.070)
  Pallas kernels: 54.4 us -> 115 us
  waiting for transfers between devices: 34.2 us -> 0.02 us
  starting transfers between devices: 15.6 us -> 0.04 us
    pallas_call x0 -> x1, Pallas kernels: none -> 60.1 us  [relay_exchange(): pl.pallas_call(functools.partial(relay_kernel, axis, count), out_shape=ja...]
    ppermute x6 -> x0, waiting for transfers between devices: 34.2 us -> none  [shifted_from(): lax.ppermute(value, axis, [(source, source - distance) for source in rang...]
    ppermute x6 -> x0, starting transfers between devices: 15.6 us -> none  [shifted_from(): lax.ppermute(value, axis, [(source, source - distance) for source in rang...]
  transfers between devices with their start and end apart: 7 -> 1, of which waited for: 5 -> 0; matrix products, arithmetic and copies ran while one was open for 13% -> 13% of each run, Pallas kernels for 32% -> 63%
where the time goes in v2:
time: 183 us; the launch traced here: 182 us
  Pallas kernels  115 us (63%)
  other arithmetic  17.9 us (10%)
  blocking collectives  14.8 us (8%)
  between operations  14.3 us (8%)
  matrix products  10.6 us (6%)
  local copies, waits for them, and re-layouts  9.83 us (5%)
    pallas_call x1, Pallas kernels, relay_exchange(): pl.pallas_call(functools.partial(relay_kernel, axis, count), out_shape=ja...  60.1 us
    pallas_call x3, Pallas kernels, exchange(): pl.pallas_call(functools.partial(exchange_kernel, axis, count, same), out...  45.7 us
    all_to_all x1, blocking collectives, body(): lax.all_to_all(buffer, 'exp', split_axis=0, concat_axis=1, tiled=True)  14.8 us
    dot_general x1, matrix products, body(): jnp.einsum('lrf,lrd->lfd', hidden_saved, all_rows, preferred_element_type...  6.83 us
    pallas_call x1, Pallas kernels, local_scans(): pl.pallas_call(local_scans_kernel, out_shape=(jax.ShapeDtypeStruct(decays...  4.92 us
    reduce_sum x1, other arithmetic, body(): jnp.sum(adjoint * (-steps[:, None, :] * decays * before), axis=0)  4.13 us
    pallas_call x1, Pallas kernels, adjoint_scan(): pl.pallas_call(adjoint_scan_kernel, out_shape=jax.ShapeDtypeStruct(decays...  3.99 us
  transfers between devices with their start and end apart: 1, of which 0 were waited for; matrix products, arithmetic and copies ran while one was open for 13% of the time, Pallas kernels for 63%

profile of v2, /device:TPU:1, one launch (start us, length us, event | category | flops | bytes accessed | tf_op | source)
XLA Modules:
  0.0 182.1 jit_solution(13354842737548673604)
XLA Ops:
  7.2 0.0 copy-start
  7.2 0.0 copy-start.8
  7.2 0.0 copy-start.3
  7.2 0.0 copy-start.9
  7.2 0.0 copy-start.4
  7.2 0.0 copy-start.5
  7.2 0.0 all-gather.2.cloned.1.call-start
  7.3 0.9 copy.33
  8.2 0.1 reshape.101
  8.2 0.1 fusion.56
  8.4 0.2 select_reduce_fusion
  8.5 0.9 mul.687
  9.5 0.2 mul.688
  9.7 0.8 copy.34
  10.4 0.1 mul.685
  10.5 0.3 convolution_convert_fusion
  10.9 0.2 reshape.102
  11.0 14.8 %all_to_all.12 = bf16[16,2,4096]{2,1,0:T(2,128)(2,1)S(1)} all-to-all(bf16[16,2,4096]{2,1,0:T(2,128)(2,1)S(1)} %reshape.102), channel_id=1, replica_groups=mesh['ctx'=32,'exp'=16] {'exp'}, dimensions={0} | all-to-all | bytes 524288 | tf_op jit(solution)/shard_map/all_to_all | solution.py:249
  25.8 0.0 copy-start.2
  25.8 0.8 all_to_all.10
  26.6 0.0 all-gather.2.cloned.1.call-update
  26.6 0.0 copy-done.8
  26.6 0.1 copy.29
  26.7 0.0 copy-done.3
  26.8 0.0 copy-done.9
  26.8 0.1 copy.30
  26.9 0.0 copy-done.4
  26.9 0.0 copy-done.5
  27.0 1.6 broadcast_multiply_fusion.1.source_ref
  28.6 0.0 copy-done.2
  28.6 2.5 %multiply_exponential_fusion = (f32[128,16,256]{2,1,0:T(8,128)}, f32[128,16,256]{2,1,0:T(8,128)}) fusion(f32[16,256]{1,0:T(8,128)S(1)} %copy-done.2, f32[128,256]{1,0:T(8,128)S(1)} %get-tuple-element.47, f32[128,16]{1,0:T(8,128)S(1)} %copy.29, f32[128,256]{1,0:T(8,128)S(1)} %get-tuple-element.45), kind=kLoop, calls=%fused_computation.13 | loop fusion | flops 1048576 | bytes 4481024 | tf_op jit(solution)/shard_map/exp | solution.py:209
  31.1 0.0 copy-start.7
  31.1 4.9 %shard_map.189 = (f32[128,16,256]{2,1,0:T(8,128)}, f32[16,256]{1,0:T(8,128)}) custom-call(f32[128,16,256]{2,1,0:T(8,128)} %get-tuple-element.50.decay_ref, f32[128,16,256]{2,1,0:T(8,128)} %get-tuple-element.51.drive_ref, f32[128,16,256]{2,1,0:T(8,128)} %broadcast_multiply_fusion.1.source_ref, f32[16,256]{1,0:T(8,128)} %bitcast.261), custom_call_target="tpu_custom_call" | custom-call | flops 2097152 | bytes 8388608 | tf_op jit(solution)/shard_map/pallas_call | solution.py:31
  36.0 0.0 copy-done.7
  36.0 0.7 add_select_fusion
  36.8 0.6 pad_maximum_fusion.1.x_ref
  37.4 60.1 %shard_map.190 = f32[32,17,256]{2,1,0:T(8,128)} custom-call(f32[17,256]{1,0:T(8,128)} %pad_maximum_fusion.1.x_ref), custom_call_target="tpu_custom_call" | custom-call | tf_op jit(solution)/shard_map/pallas_call | solution.py:154
  97.5 0.0 copy-start.1
  97.5 3.2 %slice.253 = f32[127,16,256]{2,1,0:T(8,128)} slice(f32[128,16,256]{2,1,0:T(8,128)} %get-tuple-element.10), slice={[0:127], [0:16], [0:256]} | slice | bytes 4161536 | tf_op jit(solution)/shard_map/slice | solution.py:213
  100.7 0.0 copy-done.1
  100.8 0.8 fusion.26.entering_ref
  101.6 4.0 %shard_map.191 = f32[128,16,256]{2,1,0:T(8,128)} custom-call(f32[128,16,256]{2,1,0:T(8,128)} %get-tuple-element.50.decay_ref, f32[128,16,256]{2,1,0:T(8,128)} %broadcast_multiply_fusion.1.source_ref, f32[16,256]{1,0:T(8,128)} %fusion.26.entering_ref), custom_call_target="tpu_custom_call" | custom-call | flops 1048576 | bytes 6291456 | tf_op jit(solution)/shard_map/pallas_call | solution.py:56
  105.6 0.0 copy-done.6
  105.6 4.1 %multiply_reduce_fusion = (f32[16,256]{1,0:T(8,128)S(1)}, bf16[128,256]{1,0:T(8,128)(2,1)}, f32[128,256]{1,0:T(8,128)S(1)}, f32[128,16]{1,0:T(8,128)S(1)}) fusion(f32[128,16,256]{2,1,0:T(8,128)} %shard_map.191, f32[127,16,256]{2,1,0:T(8,128)} %slice.253, f32[1,16,256]{2,1,0:T(8,128)S(1)} %copy-done.6, f32[16,256]{1,0:T(8,128)S(1)} %copy-done.2, ...), kind=kLoop, calls=%fused_computation.8 | loop fusion | flops 8316928 | bytes 4833280 | tf_op jit(solution)/shard_map/reduce_sum | solution.py:239
  109.8 2.1 %multiply_reduce_fusion.1 = f32[128,16]{1,0:T(8,128)S(1)} fusion(f32[128,16,256]{2,1,0:T(8,128)} %get-tuple-element.10, f32[128,256]{1,0:T(8,128)S(1)} %convert_element_type.45), kind=kLoop, calls=%fused_computation.9 | loop fusion | flops 1046528 | bytes 2236416 | tf_op jit(solution)/shard_map/reduce_sum | solution.py:214
  111.9 0.1 copy.32
  111.9 0.6 pad_maximum_fusion.2.x_ref
  112.6 9.9 %shard_map.192 = f32[16,2,16,128]{3,2,1,0:T(8,128)} custom-call(f32[2,16,128]{2,1,0:T(8,128)} %pad_maximum_fusion.2.x_ref), custom_call_target="tpu_custom_call" | custom-call | tf_op jit(solution)/shard_map/pallas_call | solution.py:98
  122.4 0.6 reshape.99.x_ref
  123.1 20.7 %shard_map.193 = f32[32,1,128]{2,1,0:T(1,128)} custom-call(f32[32,1,128]{2,1,0:T(1,128)} %reshape.99.x_ref), custom_call_target="tpu_custom_call" | custom-call | tf_op jit(solution)/shard_map/pallas_call | solution.py:98
  143.8 1.0 reduce_sum.88
  144.8 1.3 reduce_sum.90
  146.1 15.2 %shard_map.194 = f32[32,1,128]{2,1,0:T(1,128)} custom-call(f32[1,128]{1,0:T(1,128)} %bitcast.297), custom_call_target="tpu_custom_call" | custom-call | tf_op jit(solution)/shard_map/pallas_call | solution.py:98
  161.2 0.5 broadcast.29
  161.7 1.4 reduce.4
  163.1 0.6 reshape.100
  163.8 0.6 slice_bitcast_fusion
  164.4 0.0 copy-done.10
  164.4 0.7 fusion.23
  165.0 0.0 copy-done.12
  165.0 6.8 %fusion.7 = bf16[1,224,4096]{2,1,0:T(8,128)(2,1)} fusion(bf16[1,1024,4096]{2,1,0:T(8,128)(2,1)} %all-gather.2.cloned.1.call-done, bf16[1,1024,224]{1,2,0:T(8,128)(2,1)S(1)} %copy-done.12), kind=kOutput, calls=%fused_computation.5 | convolution fusion | flops 1879965696 | bytes 10682368 | tf_op jit(solution)/shard_map/lrf,lrd->lfd/dot_general | solution.py:251
  171.9 0.0 copy-done
  171.9 0.0 copy-done.11
  171.9 3.4 %fusion.16 = bf16[1,1024,224]{1,2,0:T(8,128)(2,1)} fusion(bf16[1,224,4096]{2,1,0:T(8,128)(2,1)S(1)} %copy-done, bf16[1,1024,4096]{2,1,0:T(8,128)(2,1)S(1)} %copy-done.11), kind=kOutput, calls=%fused_computation.16 | convolution fusion | flops 1879277568 | bytes 10682368 | tf_op jit(solution)/shard_map/lrd,lfd->lrf/dot_general | solution.py:254
  (13 shorter events, 0.2 us)
Async XLA Ops:
  7.2 164.7 %copy-start = (bf16[1,224,4096]{2,1,0:T(8,128)(2,1)S(1)}, bf16[1,224,4096]{2,1,0:T(8,128)(2,1)}, u32[]{:S(2)}) copy-start(bf16[1,224,4096]{2,1,0:T(8,128)(2,1)} %param.26) | copy-start | bytes 5505028
  7.2 19.4 %copy-start.8 = (f32[16,128]{1,0:T(8,128)S(1)}, f32[16,128]{1,0:T(8,128)}, u32[]{:S(2)}) copy-start(f32[16,128]{1,0:T(8,128)} %param.17) | copy-start | bytes 24580
  7.2 19.5 %copy-start.3 = (bf16[128,256]{1,0:T(8,128)(2,1)S(1)}, bf16[128,256]{1,0:T(8,128)(2,1)}, u32[]{:S(2)}) copy-start(bf16[128,256]{1,0:T(8,128)(2,1)} %param.22) | copy-start | bytes 196612
  7.2 19.6 %copy-start.9 = (f32[16,128]{1,0:T(8,128)S(1)}, f32[16,128]{1,0:T(8,128)}, u32[]{:S(2)}) copy-start(f32[16,128]{1,0:T(8,128)} %param.18) | copy-start | bytes 24580
  7.2 19.7 %copy-start.4 = (bf16[128,256]{1,0:T(8,128)(2,1)S(1)}, bf16[128,256]{1,0:T(8,128)(2,1)}, u32[]{:S(2)}) copy-start(bf16[128,256]{1,0:T(8,128)(2,1)} %param.14) | copy-start | bytes 196612
  7.2 19.7 %copy-start.5 = (bf16[128,256]{1,0:T(8,128)(2,1)S(1)}, bf16[128,256]{1,0:T(8,128)(2,1)}, u32[]{:S(2)}) copy-start(bf16[128,256]{1,0:T(8,128)(2,1)} %param.15) | copy-start | bytes 196612
  7.2 157.8 %all-gather.2.cloned.1.call-start = ((), (), s32[]{:S(2)}) async-start(), calls=%async_computation.1 | async-start | bytes 8650752 | tf_op jit(solution)/shard_map/all_gather | solution.py:250
  25.8 2.8 %copy-start.2 = (f32[16,256]{1,0:T(8,128)S(1)}, f32[16,256]{1,0:T(8,128)}, u32[]{:S(2)}) copy-start(f32[16,256]{1,0:T(8,128)} %param.16) | copy-start | bytes 49156
  31.1 4.9 %copy-start.7 = (f32[16,256]{1,0:T(8,128)S(1)}, f32[16,256]{1,0:T(8,128)}, u32[]{:S(2)}) copy-start(f32[16,256]{1,0:T(8,128)} %param.21) | copy-start | bytes 49156
  97.5 3.3 %copy-start.1 = (f32[32,17,256]{2,1,0:T(8,128)S(1)}, f32[32,17,256]{2,1,0:T(8,128)}, u32[]{:S(2)}) copy-start(f32[32,17,256]{2,1,0:T(8,128)} %shard_map.190) | copy-start | bytes 1671172
  101.6 4.0 %copy-start.6 = (f32[1,16,256]{2,1,0:T(8,128)S(1)}, f32[1,16,256]{2,1,0:T(8,128)}, u32[]{:S(2)}) copy-start(f32[1,16,256]{2,1,0:T(8,128)} %param.20) | copy-start | bytes 49156
  109.7 54.6 %copy-start.10 = (f32[256]{0:T(256)S(1)}, f32[256]{0:T(256)}, u32[]{:S(2)}) copy-start(f32[256]{0:T(256)} %param.19) | copy-start | bytes 3076
  109.7 55.3 %copy-start.12 = (bf16[1,1024,224]{1,2,0:T(8,128)(2,1)S(1)}, bf16[1,1024,224]{1,2,0:T(8,128)(2,1)}, u32[]{:S(2)}) copy-start(bf16[1,1024,224]{1,2,0:T(8,128)(2,1)} %param.27) | copy-start | bytes 1376260
  165.0 6.8 %copy-start.11 = (bf16[1,1024,4096]{2,1,0:T(8,128)(2,1)S(1)}, bf16[1,1024,4096]{2,1,0:T(8,128)(2,1)}, u32[]{:S(2)}) copy-start(bf16[1,1024,4096]{2,1,0:T(8,128)(2,1)} %all-gather.2.cloned.1.call-done) | copy-start | bytes 25165828
Sparse Core Ops, SparseCore 0:
  26.7 113.2 all-gather.1

commit v3 on v1

--- a/solution.py
+++ b/solution.py
@@ -1,4 +1,5 @@
 import functools
+import math
 
 import jax
 import jax.numpy as jnp
@@ -10,8 +11,31 @@
 EXPERTS = 16
 
 
+CTX = ("z", "core")
+
+
+def axis_count(axes):
+    return math.prod(lax.axis_size(name) for name in axes)
+
+
+def axis_position(axes):
+    flat = 0
+    for name in axes:
+        flat = flat * lax.axis_size(name) + lax.axis_index(name)
+    return flat
+
+
+def device_at(axes, flat):
+    place = {}
+    for name in reversed(axes):
+        size = lax.axis_size(name)
+        place[name] = lax.rem(flat, size)
+        flat = flat // size
+    return place
+
+
 def shifted_from(value, axis, distance):
-    count = lax.axis_size(axis)
+    count = axis_count(axis)
     return lax.ppermute(value, axis, [(source, source - distance) for source in range(distance, count)])
 
 
@@ -68,13 +92,13 @@
 
 
 def exchange_kernel(axis, count, same, x_ref, out_ref, land, send_sems, recv_sems):
-    me = lax.axis_index(axis)
+    me = axis_position(axis)
     barrier = pltpu.get_barrier_semaphore()
     for k in range(1, count):
         pl.semaphore_signal(
             barrier,
             1,
-            device_id={axis: lax.rem(me + k, count)},
+            device_id=device_at(axis, lax.rem(me + k, count)),
             device_id_type=pl.DeviceIdType.MESH,
         )
     pl.semaphore_wait(barrier, count - 1)
@@ -86,7 +110,7 @@
             dst_ref=land.at[me],
             send_sem=send_sems.at[k],
             recv_sem=recv_sems.at[k],
-            device_id={axis: peer},
+            device_id=device_at(axis, peer),
             device_id_type=pl.DeviceIdType.MESH,
         )
         copy.start()
@@ -98,7 +122,7 @@
 
 
 def exchange(x, axis, same, collective_id):
-    count = lax.axis_size(axis)
+    count = axis_count(axis)
     block = x.shape if same else x.shape[1:]
     return pl.pallas_call(
         functools.partial(exchange_kernel, axis, count, same),
@@ -162,20 +186,20 @@
     before = jnp.concatenate([first_state[None], states[:-1]], axis=0)
     out_cols = jnp.sum(states * grads[:, None, :], axis=2)
     shrink = jnp.exp(-decay_rate * jnp.sum(steps, axis=0)[None])
-    position = lax.axis_index("ctx")
-    count = lax.axis_size("ctx")
+    position = axis_position(CTX)
+    count = axis_count(CTX)
     is_last = position == count - 1
     pair = jnp.stack(
         [jnp.where(is_last, 0.0, shrink), jnp.where(is_last, shrink * end_grad + seed, seed)]
     )
     distance = 1
     while distance < count:
-        later = shifted_from(pair, "ctx", distance)
+        later = shifted_from(pair, CTX, distance)
         present = position + distance < count
         composed = jnp.stack([pair[0] * later[0], pair[0] * later[1] + pair[1]])
         pair = jnp.where(present, composed, pair)
         distance *= 2
-    entering = jnp.where(is_last, end_grad, shifted_from(pair[1], "ctx", 1))
+    entering = jnp.where(is_last, end_grad, shifted_from(pair[1], CTX, 1))
     adjoint = adjoint_scan(decays, sources, entering)
     input_grad = (
         steps * jnp.sum(bmats[:, :, None] * adjoint, axis=1) + skip_gain[None] * grads
@@ -186,56 +210,71 @@
     ).astype(jnp.bfloat16)
     in_cols = jnp.sum(adjoint * (steps * inputs)[:, None, :], axis=2)
     rate_local = jnp.sum(adjoint * (-steps[:, None, :] * decays * before), axis=0)
-    col_sums = jnp.sum(exchange(jnp.stack([in_cols.T, out_cols.T]), "exp", True, 1), axis=0)
+    col_sums = jnp.sum(exchange(jnp.stack([in_cols.T, out_cols.T]), ("exp",), True, 1), axis=0)
     in_proj_grad, out_proj_grad = col_sums[0], col_sums[1]
-    ctx_count = lax.axis_size("ctx")
+    ctx_count = axis_count(CTX)
     rate_parts = rate_local.reshape(ctx_count, 1, rate_local.size // ctx_count)
-    rate_chunk = jnp.sum(exchange(rate_parts, "ctx", False, 2), axis=0)
-    decay_grad = exchange(rate_chunk, "ctx", True, 3).reshape(rate_local.shape)
+    rate_chunk = jnp.sum(exchange(rate_parts, CTX, False, 2), axis=0)
+    decay_grad = exchange(rate_chunk, CTX, True, 3).reshape(rate_local.shape)
     slot_total = hidden_saved.shape[1]
-    capacity = slot_total // (lax.axis_size("ctx") * lax.axis_size("exp"))
+    capacity = slot_total // (axis_count(CTX) * lax.axis_size("exp"))
     buffer = slot_buffer(moe_grad, route, gate_prob, capacity)
     received_rows = lax.all_to_all(buffer, "exp", split_axis=0, concat_axis=1, tiled=True)
-    all_rows = lax.all_gather(received_rows, "ctx", axis=1, tiled=True)
+    plane_rows = lax.all_gather(received_rows, "z", axis=1, tiled=True)
+    all_rows = lax.all_gather(plane_rows, "core", axis=1, tiled=True)
+    planes, cores = lax.axis_size("z"), lax.axis_size("core")
+    grouped = (1, planes, cores, received_rows.shape[1], hidden_saved.shape[2])
+    saved_by_core = (
+        hidden_saved.reshape(grouped).transpose(0, 2, 1, 3, 4).reshape(hidden_saved.shape)
+    )
     weight_total = jnp.einsum(
-        "lrf,lrd->lfd", hidden_saved, all_rows, preferred_element_type=jnp.float32
-    )
-    hidden_grad = jnp.einsum(
+        "lrf,lrd->lfd", saved_by_core, all_rows, preferred_element_type=jnp.float32
+    )
+    hidden_by_core = jnp.einsum(
         "lrd,lfd->lrf", all_rows, w_down, preferred_element_type=jnp.float32
     ).astype(jnp.bfloat16)
+    hidden_grad = (
+        hidden_by_core.reshape(1, cores, planes, received_rows.shape[1], hidden_saved.shape[2])
+        .transpose(0, 2, 1, 3, 4)
+        .reshape(hidden_saved.shape)
+    )
     down_grad = weight_total.astype(jnp.bfloat16)
     return (input_grad, step_grad, in_proj_grad, out_proj_grad, decay_grad, down_grad, hidden_grad)
 
 
 def solution(mesh):
     placed = (
-        P("ctx", "exp"),
-        P("ctx", "exp"),
+        P(CTX, "exp"),
+        P(CTX, "exp"),
         P(None, "exp"),
-        P(None, "ctx"),
-        P(None, "ctx"),
+        P(None, CTX),
+        P(None, CTX),
         P("exp"),
-        P("ctx", None, "exp"),
+        P(CTX, None, "exp"),
         P(None, "exp"),
-        P("ctx", "exp"),
-        P(("ctx", "exp"), None),
-        P(("ctx", "exp"), None),
-        P(("ctx", "exp"), None),
-        P("exp", "ctx", None),
-        P("exp", None, "ctx"),
+        P(CTX, "exp"),
+        P(CTX + ("exp",), None),
+        P(CTX + ("exp",), None),
+        P(CTX + ("exp",), None),
+        P("exp", CTX, None),
+        P("exp", None, CTX),
+    )
+    planes = mesh.shape["ctx"] // 2
+    split = jax.sharding.Mesh(
+        mesh.devices.reshape(planes, 2, mesh.shape["exp"]), CTX + ("exp",)
     )
     return jax.shard_map(
         body,
-        mesh=mesh,
+        mesh=split,
         in_specs=placed,
         out_specs=(
-            P("ctx", "exp"),
-            P("ctx", "exp"),
-            P(None, "ctx"),
-            P(None, "ctx"),
+            P(CTX, "exp"),
+            P(CTX, "exp"),
+            P(None, CTX),
+            P(None, CTX),
             P(None, "exp"),
-            P("exp", "ctx", None),
-            P("exp", None, "ctx"),
+            P("exp", CTX, None),
+            P("exp", None, CTX),
         ),
         check_vma=False,
     )

time: 171 us -> 251 us (1.47)
  waiting for transfers between devices: 34.2 us -> 103 us
  starting transfers between devices: 15.6 us -> 21.7 us
  local copies, waits for them, and re-layouts: 8.09 us -> 10.8 us
    all_gather x1 -> x2, waiting for transfers between devices: 0.01 us -> 72.5 us  [the longest x1 72.5 us: body(): plane_rows = lax.all_gather(received_rows, 'z', axis=1, tiled=True)]
    ppermute x6, starting transfers between devices: 15.6 us -> 21.6 us  [shifted_from(): lax.ppermute(value, axis, [(source, source - distance) for source in rang...]
    ppermute x6, waiting for transfers between devices: 34.2 us -> 30 us  [shifted_from(): lax.ppermute(value, axis, [(source, source - distance) for source in rang...]
    dot_general x1, matrix products: 3.4 us -> 6 us  [body(): jnp.einsum('lrd,lfd->lrf', all_rows, w_down, preferred_element_type=jnp.f...]
  transfers between devices with their start and end apart: 7 -> 8, of which waited for: 5 -> 6; matrix products, arithmetic and copies ran while one was open for 13% -> 9% of each run, Pallas kernels for 32% -> 22%
where the time goes in v3:
time: 251 us; the launch traced here: 250 us
  waiting for transfers between devices  103 us (41%)
  Pallas kernels  53.7 us (21%)
  starting transfers between devices  21.7 us (9%)
  other arithmetic  19 us (8%)
  blocking collectives  14.8 us (6%)
  between operations  14.4 us (6%)
  matrix products  13.1 us (5%)
  local copies, waits for them, and re-layouts  10.8 us (4%)
    all_gather x1, waiting for transfers between devices, body(): plane_rows = lax.all_gather(received_rows, 'z', axis=1, tiled=True)  72.5 us
    pallas_call x3, Pallas kernels, exchange(): pl.pallas_call(functools.partial(exchange_kernel, axis, count, same), out...  45 us
    ppermute x6, waiting for transfers between devices, shifted_from(): lax.ppermute(value, axis, [(source, source - distance) for source in rang...  30 us
    ppermute x6, starting transfers between devices, shifted_from(): lax.ppermute(value, axis, [(source, source - distance) for source in rang...  21.6 us
    all_to_all x1, blocking collectives, body(): lax.all_to_all(buffer, 'exp', split_axis=0, concat_axis=1, tiled=True)  14.8 us
    dot_general x1, matrix products, body(): jnp.einsum('lrf,lrd->lfd', saved_by_core, all_rows, preferred_element_typ...  6.73 us
    dot_general x1, matrix products, body(): jnp.einsum('lrd,lfd->lrf', all_rows, w_down, preferred_element_type=jnp.f...  6 us
  transfers between devices with their start and end apart: 8, of which 6 were waited for; matrix products, arithmetic and copies ran while one was open for 9% of the time, Pallas kernels for 22%

profile of v3, /device:TPU:1, one launch (start us, length us, event | category | flops | bytes accessed | tf_op | source)
XLA Modules:
  0.0 249.9 jit_solution(5979849984747361632)
XLA Ops:
  7.2 0.0 copy-start
  7.2 0.0 all-gather.3.cloned.1.call-start
  7.2 0.9 copy.39
  8.1 0.1 reshape.83
  8.2 0.1 fusion.27
  8.3 0.2 select_reduce_fusion
  8.5 0.9 mul.229
  9.4 0.2 mul.230
  9.6 0.8 copy.40
  10.4 0.1 mul.227
  10.5 0.3 convolution_convert_fusion
  10.8 0.2 reshape.84
  11.0 14.8 %all_to_all.12 = bf16[16,2,4096]{2,1,0:T(2,128)(2,1)S(1)} all-to-all(bf16[16,2,4096]{2,1,0:T(2,128)(2,1)S(1)} %reshape.84), channel_id=1, replica_groups=mesh['z'=16,'core'=2,'exp'=16] {'exp'}, dimensions={0} | all-to-all | bytes 524288 | tf_op jit(solution)/shard_map/all_to_all | solution.py:222
  25.7 0.8 all_to_all.10
  26.5 0.0 all-gather.3.cloned.1.call-update
  26.6 0.0 all-gather.5.cloned.1.call-start
  26.6 72.5 %all-gather.3.cloned.1.call-done = bf16[1,512,4096]{2,1,0:T(8,128)(2,1)} async-done(((bf16[1,32,4096]{2,1,0:T(8,128)(2,1)}), bf16[1,512,4096]{2,1,0:T(8,128)(2,1)}) %all-gather.3.cloned.1.call-update) | async-done | bytes 4194320 | tf_op jit(solution)/shard_map/all_gather | solution.py:223
  99.2 0.0 all-gather.5.cloned.1.call-update
  99.2 0.0 copy-start.3
  99.2 0.6 copy-done.10
  99.8 0.1 copy.35
  99.9 0.1 copy-done.4
  100.0 0.1 copy.36
  100.2 1.7 broadcast_multiply_fusion.1.source_ref
  101.9 2.5 multiply_exponential_fusion
  104.3 4.8 %shard_map.189 = (f32[128,16,256]{2,1,0:T(8,128)}, f32[16,256]{1,0:T(8,128)}) custom-call(f32[128,16,256]{2,1,0:T(8,128)} %get-tuple-element.46.decay_ref, f32[128,16,256]{2,1,0:T(8,128)} %get-tuple-element.47.drive_ref, f32[128,16,256]{2,1,0:T(8,128)} %broadcast_multiply_fusion.1.source_ref, f32[16,256]{1,0:T(8,128)} %bitcast.71), custom_call_target="tpu_custom_call" | custom-call | flops 2097152 | bytes 8388608 | tf_op jit(solution)/shard_map/pallas_call | solution.py:60
  109.1 0.7 select_bitcast_fusion
  109.9 11.5 %collective-permute-start = (f32[2,16,256]{2,1,0:T(8,128)S(1)}, f32[2,16,256]{2,1,0:T(8,128)S(1)}, u32[]{:S(2)}, u32[]{:S(2)}) collective-permute-start(f32[2,16,256]{2,1,0:T(8,128)S(1)} %pad_maximum_fusion.1), channel_id=1, source_target_pairs={{16,0},{32,16},{48,32},{64,48},{80,64},{96,80},{112,96},{128,112},... | collective-permute-start | bytes 98312 | tf_op jit(solution)/shard_map/ppermute | solution.py:39
  121.4 2.6 %collective-permute-done = f32[2,16,256]{2,1,0:T(8,128)S(1)} collective-permute-done((f32[2,16,256]{2,1,0:T(8,128)S(1)}, f32[2,16,256]{2,1,0:T(8,128)S(1)}, u32[]{:S(2)}, u32[]{:S(2)}) %collective-permute-start) | collective-permute-done | bytes 32800 | tf_op jit(solution)/shard_map/ppermute | solution.py:39
  123.9 0.7 fusion.26
  124.7 1.3 collective-permute-start.1
  126.0 3.4 %collective-permute-done.1 = f32[2,16,256]{2,1,0:T(8,128)S(1)} collective-permute-done((f32[2,16,256]{2,1,0:T(8,128)S(1)}, f32[2,16,256]{2,1,0:T(8,128)S(1)}, u32[]{:S(2)}, u32[]{:S(2)}) %collective-permute-start.1) | collective-permute-done | bytes 32800 | tf_op jit(solution)/shard_map/ppermute | solution.py:39
  129.4 1.3 collective-permute-start.2
  130.7 4.7 %collective-permute-done.2 = f32[2,16,256]{2,1,0:T(8,128)S(1)} collective-permute-done((f32[2,16,256]{2,1,0:T(8,128)S(1)}, f32[2,16,256]{2,1,0:T(8,128)S(1)}, u32[]{:S(2)}, u32[]{:S(2)}) %collective-permute-start.2) | collective-permute-done | bytes 32800 | tf_op jit(solution)/shard_map/ppermute | solution.py:39
  135.4 1.3 collective-permute-start.3
  136.7 7.3 %collective-permute-done.3 = f32[2,16,256]{2,1,0:T(8,128)S(1)} collective-permute-done((f32[2,16,256]{2,1,0:T(8,128)S(1)}, f32[2,16,256]{2,1,0:T(8,128)S(1)}, u32[]{:S(2)}, u32[]{:S(2)}) %collective-permute-start.3) | collective-permute-done | bytes 32800 | tf_op jit(solution)/shard_map/ppermute | solution.py:39
  144.0 1.3 collective-permute-start.4
  145.3 12.1 %collective-permute-done.4 = f32[2,16,256]{2,1,0:T(8,128)S(1)} collective-permute-done((f32[2,16,256]{2,1,0:T(8,128)S(1)}, f32[2,16,256]{2,1,0:T(8,128)S(1)}, u32[]{:S(2)}, u32[]{:S(2)}) %collective-permute-start.4) | collective-permute-done | bytes 32800 | tf_op jit(solution)/shard_map/ppermute | solution.py:39
  157.4 0.6 fusion.20
  158.0 5.0 %collective-permute-start.5 = (f32[16,256]{1,0:T(8,128)}, f32[16,256]{1,0:T(8,128)}, u32[]{:S(2)}, u32[]{:S(2)}) collective-permute-start(f32[16,256]{1,0:T(8,128)} %fusion.20), channel_id=1, source_target_pairs={{16,0},{32,16},{48,32},{64,48},{80,64},{96,80},{112,96},{128,112},... | collective-permute-start | bytes 49160 | tf_op jit(solution)/shard_map/ppermute | solution.py:39
  163.0 1.9 multiply_reduce_fusion.1
  164.9 0.0 copy-start.2
  164.9 1.5 slice.89
  166.4 0.7 copy.38
  167.1 0.2 copy.41
  167.4 1.3 broadcast_select_fusion.entering_ref
  168.7 3.9 %shard_map.190 = f32[128,16,256]{2,1,0:T(8,128)} custom-call(f32[128,16,256]{2,1,0:T(8,128)} %get-tuple-element.46.decay_ref, f32[128,16,256]{2,1,0:T(8,128)} %broadcast_multiply_fusion.1.source_ref, f32[16,256]{1,0:T(8,128)} %broadcast_select_fusion.entering_ref), custom_call_target="tpu_custom_call" | custom-call | flops 1048576 | bytes 6291456 | tf_op jit(solution)/shard_map/pallas_call | solution.py:85
  172.6 4.1 %multiply_reduce_fusion = (f32[16,256]{1,0:T(8,128)S(1)}, bf16[128,256]{1,0:T(8,128)(2,1)}, f32[128,256]{1,0:T(8,128)S(1)}, f32[128,16]{1,0:T(8,128)S(1)}) fusion(f32[128,16,256]{2,1,0:T(8,128)} %shard_map.190, f32[127,16,256]{2,1,0:T(8,128)} %slice.89, f32[1,16,256]{2,1,0:T(8,128)S(1)} %copy-done.8, f32[16,256]{1,0:T(8,128)S(1)} %copy-done.3, ...), kind=kLoop, calls=%fused_computation.8 | loop fusion | flops 8316928 | bytes 4833280 | tf_op jit(solution)/shard_map/reduce_sum | solution.py:212
  176.8 0.6 pad_maximum_fusion.3.x_ref
  177.4 12.1 %shard_map.191 = f32[16,2,16,128]{3,2,1,0:T(8,128)} custom-call(f32[2,16,128]{2,1,0:T(8,128)} %pad_maximum_fusion.3.x_ref), custom_call_target="tpu_custom_call" | custom-call | tf_op jit(solution)/shard_map/pallas_call | solution.py:127
  189.5 0.6 reshape.81.x_ref
  190.1 17.7 %shard_map.192 = f32[32,1,128]{2,1,0:T(1,128)} custom-call(f32[32,1,128]{2,1,0:T(1,128)} %reshape.81.x_ref), custom_call_target="tpu_custom_call" | custom-call | tf_op jit(solution)/shard_map/pallas_call | solution.py:127
  207.9 1.0 reduce_sum.88
  208.8 1.3 reduce_sum.90
  210.1 15.2 %shard_map.193 = f32[32,1,128]{2,1,0:T(1,128)} custom-call(f32[1,128]{1,0:T(1,128)} %bitcast.76), custom_call_target="tpu_custom_call" | custom-call | tf_op jit(solution)/shard_map/pallas_call | solution.py:127
  225.3 0.5 broadcast.29
  225.8 1.4 reduce.4
  227.2 0.6 reshape.82
  227.8 0.6 slice_bitcast_fusion.2
  228.4 0.7 fusion.17
  229.1 6.0 %fusion.11 = bf16[1024,224]{0,1:T(8,128)(2,1)S(1)} fusion(bf16[1,224,4096]{2,1,0:T(8,128)(2,1)S(1)} %copy-done, bf16[1,1024,4096]{2,1,0:T(8,128)(2,1)} %all-gather.5.cloned.1.call-done), kind=kOutput, calls=%fused_computation.15 | convolution fusion | flops 1879277568 | bytes 10682368 | tf_op jit(solution)/shard_map/lrd,lfd->lrf/dot_general | solution.py:233
  235.1 0.2 copy.43
  235.3 1.0 copy.45
  236.3 6.7 %fusion.7 = bf16[1,224,4096]{2,1,0:T(8,128)(2,1)} fusion(bf16[1024,224]{1,0:T(8,128)(2,1)S(1)} %bitcast.70, bf16[1,1024,4096]{2,1,0:T(8,128)(2,1)} %all-gather.5.cloned.1.call-done), kind=kOutput, calls=%fused_computation.5 | convolution fusion | flops 1879965696 | bytes 10682368 | tf_op jit(solution)/shard_map/lrf,lrd->lfd/dot_general | solution.py:230
  (40 shorter events, 0.3 us)
Async XLA Ops:
  7.2 221.9 %copy-start = (bf16[1,224,4096]{2,1,0:T(8,128)(2,1)S(1)}, bf16[1,224,4096]{2,1,0:T(8,128)(2,1)}, u32[]{:S(2)}) copy-start(bf16[1,224,4096]{2,1,0:T(8,128)(2,1)} %param.26) | copy-start | bytes 5505028
  7.2 92.0 %all-gather.3.cloned.1.call-start = ((), (), s32[]{:S(2)}) async-start(), calls=%async_computation.1 | async-start | bytes 4456448 | tf_op jit(solution)/shard_map/all_gather | solution.py:223
  26.6 202.5 %all-gather.5.cloned.1.call-start = ((), (), s32[]{:S(2)}) async-start(), calls=%async_computation.2 | async-start | bytes 12582912 | tf_op jit(solution)/shard_map/all_gather | solution.py:224
  99.1 0.7 copy-start.10
  99.1 0.9 copy-start.4
  99.1 0.9 copy-start.11
  99.1 1.0 copy-start.5
  99.1 1.0 copy-start.6
  99.2 2.7 %copy-start.3 = (f32[16,256]{1,0:T(8,128)S(1)}, f32[16,256]{1,0:T(8,128)}, u32[]{:S(2)}) copy-start(f32[16,256]{1,0:T(8,128)} %param.16) | copy-start | bytes 49156
  104.3 4.8 %copy-start.7 = (f32[16,256]{1,0:T(8,128)S(1)}, f32[16,256]{1,0:T(8,128)}, u32[]{:S(2)}) copy-start(f32[16,256]{1,0:T(8,128)} %param.21) | copy-start | bytes 49156
  109.9 14.1 %collective-permute-start = (f32[2,16,256]{2,1,0:T(8,128)S(1)}, f32[2,16,256]{2,1,0:T(8,128)S(1)}, u32[]{:S(2)}, u32[]{:S(2)}) collective-permute-start(f32[2,16,256]{2,1,0:T(8,128)S(1)} %pad_maximum_fusion.1), channel_id=1, source_target_pairs={{16,0},{32,16},{48,32},{64,48},{80,64},{96,80},{112,96},{128,112},... | collective-permute-start | bytes 98312 | tf_op jit(solution)/shard_map/ppermute | solution.py:39
  124.7 4.7 %collective-permute-start.1 = (f32[2,16,256]{2,1,0:T(8,128)S(1)}, f32[2,16,256]{2,1,0:T(8,128)S(1)}, u32[]{:S(2)}, u32[]{:S(2)}) collective-permute-start(f32[2,16,256]{2,1,0:T(8,128)S(1)} %maximum_select_fusion), channel_id=1, source_target_pairs={{32,0},{48,16},{64,32},{80,48},{96,64},{112,80},{128,96},{144,112}... | collective-permute-start | bytes 98312 | tf_op jit(solution)/shard_map/ppermute | solution.py:39
  129.4 6.0 %collective-permute-start.2 = (f32[2,16,256]{2,1,0:T(8,128)S(1)}, f32[2,16,256]{2,1,0:T(8,128)S(1)}, u32[]{:S(2)}, u32[]{:S(2)}) collective-permute-start(f32[2,16,256]{2,1,0:T(8,128)S(1)} %maximum_select_fusion.1), channel_id=1, source_target_pairs={{64,0},{80,16},{96,32},{112,48},{128,64},{144,80},{160,96},{176,11... | collective-permute-start | bytes 98312 | tf_op jit(solution)/shard_map/ppermute | solution.py:39
  135.4 8.6 %collective-permute-start.3 = (f32[2,16,256]{2,1,0:T(8,128)S(1)}, f32[2,16,256]{2,1,0:T(8,128)S(1)}, u32[]{:S(2)}, u32[]{:S(2)}) collective-permute-start(f32[2,16,256]{2,1,0:T(8,128)S(1)} %maximum_select_fusion.2), channel_id=1, source_target_pairs={{128,0},{144,16},{160,32},{176,48},{192,64},{208,80},{224,96},{240... | collective-permute-start | bytes 98312 | tf_op jit(solution)/shard_map/ppermute | solution.py:39
  144.0 13.4 %collective-permute-start.4 = (f32[2,16,256]{2,1,0:T(8,128)S(1)}, f32[2,16,256]{2,1,0:T(8,128)S(1)}, u32[]{:S(2)}, u32[]{:S(2)}) collective-permute-start(f32[2,16,256]{2,1,0:T(8,128)S(1)} %maximum_select_fusion.3), channel_id=1, source_target_pairs={{256,0},{272,16},{288,32},{304,48},{320,64},{336,80},{352,96},{368... | collective-permute-start | bytes 98312 | tf_op jit(solution)/shard_map/ppermute | solution.py:39
  145.3 19.6 %copy-start.1 = (f32[128,16,256]{2,1,0:T(8,128)S(1)}, f32[128,16,256]{2,1,0:T(8,128)}, u32[]{:S(2)}) copy-start(f32[128,16,256]{2,1,0:T(8,128)} %get-tuple-element.10) | copy-start | bytes 6291460
  158.0 9.3 %collective-permute-start.5 = (f32[16,256]{1,0:T(8,128)}, f32[16,256]{1,0:T(8,128)}, u32[]{:S(2)}, u32[]{:S(2)}) collective-permute-start(f32[16,256]{1,0:T(8,128)} %fusion.20), channel_id=1, source_target_pairs={{16,0},{32,16},{48,32},{64,48},{80,64},{96,80},{112,96},{128,112},... | collective-permute-start | bytes 49160 | tf_op jit(solution)/shard_map/ppermute | solution.py:39
  164.9 2.2 copy-start.2
  168.7 3.9 %copy-start.8 = (f32[1,16,256]{2,1,0:T(8,128)S(1)}, f32[1,16,256]{2,1,0:T(8,128)}, u32[]{:S(2)}) copy-start(f32[1,16,256]{2,1,0:T(8,128)} %param.20) | copy-start | bytes 49156
  172.6 4.1 %copy-start.9 = (f32[128,16]{0,1:T(8,128)S(1)}, f32[128,16]{0,1:T(8,128)}, u32[]{:S(2)}) copy-start(f32[128,16]{0,1:T(8,128)} %copy.38) | copy-start | bytes 24580
  172.6 55.8 %copy-start.12 = (f32[256]{0:T(256)S(1)}, f32[256]{0:T(256)}, u32[]{:S(2)}) copy-start(f32[256]{0:T(256)} %param.19) | copy-start | bytes 3076
Sparse Core Ops, SparseCore 0:
  26.7 72.4 all-gather.2
  101.2 37.1 all-gather.4

commit v4 on v1

--- a/solution.py
+++ b/solution.py
@@ -8,11 +8,6 @@
 from jax.sharding import PartitionSpec as P
 
 EXPERTS = 16
-
-
-def shifted_from(value, axis, distance):
-    count = lax.axis_size(axis)
-    return lax.ppermute(value, axis, [(source, source - distance) for source in range(distance, count)])
 
 
 def local_scans_kernel(decay_ref, drive_ref, source_ref, first_ref, states_ref, seed_ref):
@@ -110,6 +105,77 @@
         ],
         compiler_params=pltpu.CompilerParams(collective_id=collective_id, has_side_effects=True),
     )(x)
+
+
+def relay_kernel(axis, count, pair_ref, out_ref, held, land, send_sems, recv_sems):
+    me = lax.axis_index(axis)
+    distances = []
+    while 1 << len(distances) < count:
+        distances.append(1 << len(distances))
+    land[...] = jnp.zeros_like(land)
+    barrier = pltpu.get_barrier_semaphore()
+    expected = 0
+    for d in distances:
+
+        @pl.when(me >= d)
+        def _():
+            pl.semaphore_signal(barrier, 1, device_id={axis: me - d}, device_id_type=pl.DeviceIdType.MESH)
+
+        @pl.when(me + d < count)
+        def _():
+            pl.semaphore_signal(barrier, 1, device_id={axis: me + d}, device_id_type=pl.DeviceIdType.MESH)
+
+        expected = expected + (me >= d).astype(jnp.int32) + (me + d < count).astype(jnp.int32)
+    pl.semaphore_wait(barrier, expected)
+    rounds = distances + [1]
+    for r, d in enumerate(rounds):
+        last_round = r == len(rounds) - 1
+        source = pair_ref if r == 0 else held.at[r - 1]
+        copy = pltpu.make_async_remote_copy(
+            src_ref=source,
+            dst_ref=land.at[r],
+            send_sem=send_sems.at[r],
+            recv_sem=recv_sems.at[r],
+            device_id={axis: lax.rem(me - d + count, count)},
+            device_id_type=pl.DeviceIdType.MESH,
+        )
+
+        @pl.when(me >= d)
+        def _():
+            copy.start()
+
+        if not last_round:
+            held[r] = source[...]
+
+        @pl.when(me + d < count)
+        def _():
+            copy.wait_recv()
+            if not last_round:
+                shrink, seed = source[0], source[1]
+                held[r, 0] = shrink * land[r, 0]
+                held[r, 1] = shrink * land[r, 1] + seed
+
+        @pl.when(me >= d)
+        def _():
+            copy.wait_send()
+
+    out_ref[...] = land[len(rounds) - 1, 1]
+
+
+def relay(pair, axis, collective_id):
+    count = lax.axis_size(axis)
+    rounds = max(1, (count - 1).bit_length()) + 1
+    return pl.pallas_call(
+        functools.partial(relay_kernel, axis, count),
+        out_shape=jax.ShapeDtypeStruct(pair.shape[1:], pair.dtype),
+        scratch_shapes=[
+            pltpu.VMEM((rounds - 1,) + pair.shape, pair.dtype),
+            pltpu.VMEM((rounds,) + pair.shape, pair.dtype),
+            pltpu.SemaphoreType.DMA((rounds,)),
+            pltpu.SemaphoreType.DMA((rounds,)),
+        ],
+        compiler_params=pltpu.CompilerParams(collective_id=collective_id, has_side_effects=True),
+    )(pair)
 
 
 def slot_buffer(moe_grad, route, gate_prob, capacity):
@@ -168,14 +234,7 @@
     pair = jnp.stack(
         [jnp.where(is_last, 0.0, shrink), jnp.where(is_last, shrink * end_grad + seed, seed)]
     )
-    distance = 1
-    while distance < count:
-        later = shifted_from(pair, "ctx", distance)
-        present = position + distance < count
-        composed = jnp.stack([pair[0] * later[0], pair[0] * later[1] + pair[1]])
-        pair = jnp.where(present, composed, pair)
-        distance *= 2
-    entering = jnp.where(is_last, end_grad, shifted_from(pair[1], "ctx", 1))
+    entering = jnp.where(is_last, end_grad, relay(pair, "ctx", 4))
     adjoint = adjoint_scan(decays, sources, entering)
     input_grad = (
         steps * jnp.sum(bmats[:, :, None] * adjoint, axis=1) + skip_gain[None] * grads

time: 171 us -> 160 us (0.936)
  Pallas kernels: 54.4 us -> 91.8 us
  waiting for transfers between devices: 34.2 us -> 0.02 us
  starting transfers between devices: 15.6 us -> 0.04 us
    pallas_call x0 -> x1, Pallas kernels: none -> 43.7 us  [relay(): pl.pallas_call(functools.partial(relay_kernel, axis, count), out_shape=ja...]
    ppermute x6 -> x0, waiting for transfers between devices: 34.2 us -> none  [shifted_from(): lax.ppermute(value, axis, [(source, source - distance) for source in rang...]
    ppermute x6 -> x0, starting transfers between devices: 15.6 us -> none  [shifted_from(): lax.ppermute(value, axis, [(source, source - distance) for source in rang...]
    pallas_call x3, Pallas kernels: 45.5 us -> 39.2 us  [exchange(): pl.pallas_call(functools.partial(exchange_kernel, axis, count, same), out...]
  transfers between devices with their start and end apart: 7 -> 1, of which waited for: 5 -> 0; matrix products, arithmetic and copies ran while one was open for 13% -> 15% of each run, Pallas kernels for 32% -> 58%
where the time goes in v4:
time: 160 us; the launch traced here: 159 us
  Pallas kernels  91.8 us (57%)
  other arithmetic  17.7 us (11%)
  blocking collectives  14.8 us (9%)
  between operations  14.2 us (9%)
  matrix products  10.6 us (7%)
  local copies, waits for them, and re-layouts  9.74 us (6%)
    pallas_call x1, Pallas kernels, relay(): pl.pallas_call(functools.partial(relay_kernel, axis, count), out_shape=ja...  43.7 us
    pallas_call x3, Pallas kernels, exchange(): pl.pallas_call(functools.partial(exchange_kernel, axis, count, same), out...  39.2 us
    all_to_all x1, blocking collectives, body(): lax.all_to_all(buffer, 'exp', split_axis=0, concat_axis=1, tiled=True)  14.8 us
    dot_general x1, matrix products, body(): jnp.einsum('lrf,lrd->lfd', hidden_saved, all_rows, preferred_element_type...  6.83 us
    pallas_call x1, Pallas kernels, local_scans(): pl.pallas_call(local_scans_kernel, out_shape=(jax.ShapeDtypeStruct(decays...  4.92 us
    reduce_sum x1, other arithmetic, body(): jnp.sum(adjoint * (-steps[:, None, :] * decays * before), axis=0)  4.22 us
    pallas_call x1, Pallas kernels, adjoint_scan(): pl.pallas_call(adjoint_scan_kernel, out_shape=jax.ShapeDtypeStruct(decays...  3.95 us
    dot_general x1, matrix products, body(): jnp.einsum('lrd,lfd->lrf', all_rows, w_down, preferred_element_type=jnp.f...  3.42 us
  transfers between devices with their start and end apart: 1, of which 0 were waited for; matrix products, arithmetic and copies ran while one was open for 15% of the time, Pallas kernels for 58%

profile of v4, /device:TPU:1, one launch (start us, length us, event | category | flops | bytes accessed | tf_op | source)
XLA Modules:
  0.0 158.8 jit_solution(5597126626645400487)
XLA Ops:
  7.2 0.0 copy-start
  7.2 0.0 copy-start.8
  7.2 0.0 copy-start.1
  7.2 0.0 copy-start.9
  7.2 0.0 copy-start.2
  7.2 0.0 copy-start.3
  7.2 0.0 all-gather.2.cloned.1.call-start
  7.3 0.9 copy.33
  8.2 0.1 reshape.71
  8.2 0.1 fusion.26
  8.4 0.2 select_reduce_fusion
  8.5 0.9 mul.177
  9.5 0.2 mul.178
  9.7 0.8 copy.34
  10.4 0.1 mul.175
  10.5 0.3 convolution_convert_fusion
  10.9 0.2 reshape.72
  11.0 14.8 %all_to_all.12 = bf16[16,2,4096]{2,1,0:T(2,128)(2,1)S(1)} all-to-all(bf16[16,2,4096]{2,1,0:T(2,128)(2,1)S(1)} %reshape.72), channel_id=1, replica_groups=mesh['ctx'=32,'exp'=16] {'exp'}, dimensions={0} | all-to-all | bytes 524288 | tf_op jit(solution)/shard_map/all_to_all | solution.py:257
  25.8 0.0 copy-start.4
  25.8 0.8 all_to_all.10
  26.6 0.0 all-gather.2.cloned.1.call-update
  26.6 0.0 copy-done.8
  26.6 0.1 copy.29
  26.7 0.0 copy-done.1
  26.8 0.0 copy-done.9
  26.8 0.1 copy.30
  26.9 0.0 copy-done.2
  26.9 0.0 copy-done.3
  27.0 1.6 %broadcast_multiply_fusion.1.source_ref = f32[128,16,256]{2,1,0:T(8,128)} fusion(f32[128,256]{1,0:T(8,128)S(1)} %convert_element_type.45, f32[128,16]{1,0:T(8,128)S(1)} %copy.30), kind=kLoop, calls=%fused_computation.18 | loop fusion | flops 524288 | bytes 2236416 | tf_op jit(solution)/shard_map/mul | solution.py:226
  28.6 0.0 copy-done.4
  28.6 2.5 %multiply_exponential_fusion = (f32[128,16,256]{2,1,0:T(8,128)}, f32[128,16,256]{2,1,0:T(8,128)}) fusion(f32[16,256]{1,0:T(8,128)S(1)} %copy-done.4, f32[128,256]{1,0:T(8,128)S(1)} %get-tuple-element.17, f32[128,16]{1,0:T(8,128)S(1)} %copy.29, f32[128,256]{1,0:T(8,128)S(1)} %get-tuple-element.16), kind=kLoop, calls=%fused_computation.13 | loop fusion | flops 1048576 | bytes 4481024 | tf_op jit(solution)/shard_map/exp | solution.py:224
  31.1 0.0 copy-start.7
  31.1 4.9 %shard_map.189 = (f32[128,16,256]{2,1,0:T(8,128)}, f32[16,256]{1,0:T(8,128)}) custom-call(f32[128,16,256]{2,1,0:T(8,128)} %get-tuple-element.22.decay_ref, f32[128,16,256]{2,1,0:T(8,128)} %get-tuple-element.23.drive_ref, f32[128,16,256]{2,1,0:T(8,128)} %broadcast_multiply_fusion.1.source_ref, f32[16,256]{1,0:T(8,128)} %bitcast.47), custom_call_target="tpu_custom_call" | custom-call | flops 2097152 | bytes 8388608 | tf_op jit(solution)/shard_map/pallas_call | solution.py:31
  36.0 0.0 copy-done.7
  36.0 0.7 select_bitcast_fusion
  36.8 0.6 pad_maximum_fusion.1.pair_ref
  37.4 43.7 %shard_map.190 = f32[16,256]{1,0:T(8,128)} custom-call(f32[2,16,256]{2,1,0:T(8,128)} %pad_maximum_fusion.1.pair_ref), custom_call_target="tpu_custom_call" | custom-call | tf_op jit(solution)/shard_map/pallas_call | solution.py:168
  81.1 0.0 copy-start.6
  81.1 3.1 %slice.9 = f32[127,16,256]{2,1,0:T(8,128)} slice(f32[128,16,256]{2,1,0:T(8,128)} %get-tuple-element.10), slice={[0:127], [0:16], [0:256]} | slice | bytes 4161536 | tf_op jit(solution)/shard_map/slice | solution.py:228
  84.3 0.0 copy-done.6
  84.3 0.6 broadcast_select_fusion.entering_ref
  84.9 4.0 %shard_map.191 = f32[128,16,256]{2,1,0:T(8,128)} custom-call(f32[128,16,256]{2,1,0:T(8,128)} %get-tuple-element.22.decay_ref, f32[128,16,256]{2,1,0:T(8,128)} %broadcast_multiply_fusion.1.source_ref, f32[16,256]{1,0:T(8,128)} %broadcast_select_fusion.entering_ref), custom_call_target="tpu_custom_call" | custom-call | flops 1048576 | bytes 6291456 | tf_op jit(solution)/shard_map/pallas_call | solution.py:56
  88.8 0.0 copy-done.5
  88.8 4.2 %multiply_reduce_fusion = (f32[16,256]{1,0:T(8,128)S(1)}, bf16[128,256]{1,0:T(8,128)(2,1)}, f32[128,256]{1,0:T(8,128)S(1)}, f32[128,16]{1,0:T(8,128)S(1)}) fusion(f32[128,16,256]{2,1,0:T(8,128)} %shard_map.191, f32[127,16,256]{2,1,0:T(8,128)} %slice.9, f32[1,16,256]{2,1,0:T(8,128)S(1)} %copy-done.5, f32[16,256]{1,0:T(8,128)S(1)} %copy-done.4, ...), kind=kLoop, calls=%fused_computation.8 | loop fusion | flops 8316928 | bytes 4833280 | tf_op jit(solution)/shard_map/reduce_sum | solution.py:247
  93.1 2.0 %multiply_reduce_fusion.1 = f32[128,16]{1,0:T(8,128)S(1)} fusion(f32[128,16,256]{2,1,0:T(8,128)} %get-tuple-element.10, f32[128,256]{1,0:T(8,128)S(1)} %convert_element_type.45), kind=kLoop, calls=%fused_computation.9 | loop fusion | flops 1046528 | bytes 2236416 | tf_op jit(solution)/shard_map/reduce_sum | solution.py:229
  95.2 0.1 copy.32
  95.2 0.6 pad_maximum_fusion.2.x_ref
  95.9 9.6 %shard_map.192 = f32[16,2,16,128]{3,2,1,0:T(8,128)} custom-call(f32[2,16,128]{2,1,0:T(8,128)} %pad_maximum_fusion.2.x_ref), custom_call_target="tpu_custom_call" | custom-call | tf_op jit(solution)/shard_map/pallas_call | solution.py:98
  105.5 0.6 reshape.69.x_ref
  106.1 14.6 %shard_map.193 = f32[32,1,128]{2,1,0:T(1,128)} custom-call(f32[32,1,128]{2,1,0:T(1,128)} %reshape.69.x_ref), custom_call_target="tpu_custom_call" | custom-call | tf_op jit(solution)/shard_map/pallas_call | solution.py:98
  120.7 1.0 reduce_sum.88
  121.7 1.3 reduce_sum.90
  123.0 15.0 %shard_map.194 = f32[32,1,128]{2,1,0:T(1,128)} custom-call(f32[1,128]{1,0:T(1,128)} %bitcast.52), custom_call_target="tpu_custom_call" | custom-call | tf_op jit(solution)/shard_map/pallas_call | solution.py:98
  137.9 0.5 broadcast.29
  138.4 1.4 reduce.4
  139.8 0.6 reshape.70
  140.5 0.6 slice_bitcast_fusion
  141.1 0.0 copy-done.10
  141.1 0.7 fusion.23
  141.7 0.0 copy-done.12
  141.7 6.8 %fusion.7 = bf16[1,224,4096]{2,1,0:T(8,128)(2,1)} fusion(bf16[1,1024,4096]{2,1,0:T(8,128)(2,1)} %all-gather.2.cloned.1.call-done, bf16[1,1024,224]{1,2,0:T(8,128)(2,1)S(1)} %copy-done.12), kind=kOutput, calls=%fused_computation.5 | convolution fusion | flops 1879965696 | bytes 10682368 | tf_op jit(solution)/shard_map/lrf,lrd->lfd/dot_general | solution.py:259
  148.6 0.0 copy-done
  148.6 0.0 copy-done.11
  148.6 3.4 %fusion.16 = bf16[1,1024,224]{1,2,0:T(8,128)(2,1)} fusion(bf16[1,224,4096]{2,1,0:T(8,128)(2,1)S(1)} %copy-done, bf16[1,1024,4096]{2,1,0:T(8,128)(2,1)S(1)} %copy-done.11), kind=kOutput, calls=%fused_computation.16 | convolution fusion | flops 1879277568 | bytes 10682368 | tf_op jit(solution)/shard_map/lrd,lfd->lrf/dot_general | solution.py:262
  (11 shorter events, 0.2 us)
Async XLA Ops:
  7.2 141.4 %copy-start = (bf16[1,224,4096]{2,1,0:T(8,128)(2,1)S(1)}, bf16[1,224,4096]{2,1,0:T(8,128)(2,1)}, u32[]{:S(2)}) copy-start(bf16[1,224,4096]{2,1,0:T(8,128)(2,1)} %param.26) | copy-start | bytes 5505028
  7.2 19.4 %copy-start.8 = (f32[16,128]{1,0:T(8,128)S(1)}, f32[16,128]{1,0:T(8,128)}, u32[]{:S(2)}) copy-start(f32[16,128]{1,0:T(8,128)} %param.17) | copy-start | bytes 24580
  7.2 19.5 %copy-start.1 = (bf16[128,256]{1,0:T(8,128)(2,1)S(1)}, bf16[128,256]{1,0:T(8,128)(2,1)}, u32[]{:S(2)}) copy-start(bf16[128,256]{1,0:T(8,128)(2,1)} %param.22) | copy-start | bytes 196612
  7.2 19.6 %copy-start.9 = (f32[16,128]{1,0:T(8,128)S(1)}, f32[16,128]{1,0:T(8,128)}, u32[]{:S(2)}) copy-start(f32[16,128]{1,0:T(8,128)} %param.18) | copy-start | bytes 24580
  7.2 19.7 %copy-start.2 = (bf16[128,256]{1,0:T(8,128)(2,1)S(1)}, bf16[128,256]{1,0:T(8,128)(2,1)}, u32[]{:S(2)}) copy-start(bf16[128,256]{1,0:T(8,128)(2,1)} %param.14) | copy-start | bytes 196612
  7.2 19.7 %copy-start.3 = (bf16[128,256]{1,0:T(8,128)(2,1)S(1)}, bf16[128,256]{1,0:T(8,128)(2,1)}, u32[]{:S(2)}) copy-start(bf16[128,256]{1,0:T(8,128)(2,1)} %param.15) | copy-start | bytes 196612
  7.2 134.5 %all-gather.2.cloned.1.call-start = ((), (), s32[]{:S(2)}) async-start(), calls=%async_computation.1 | async-start | bytes 8650752 | tf_op jit(solution)/shard_map/all_gather | solution.py:258
  25.8 2.8 %copy-start.4 = (f32[16,256]{1,0:T(8,128)S(1)}, f32[16,256]{1,0:T(8,128)}, u32[]{:S(2)}) copy-start(f32[16,256]{1,0:T(8,128)} %param.16) | copy-start | bytes 49156
  31.1 4.9 %copy-start.7 = (f32[16,256]{1,0:T(8,128)S(1)}, f32[16,256]{1,0:T(8,128)}, u32[]{:S(2)}) copy-start(f32[16,256]{1,0:T(8,128)} %param.21) | copy-start | bytes 49156
  81.1 3.2 %copy-start.6 = (f32[16,256]{1,0:T(8,128)S(1)}, f32[16,256]{1,0:T(8,128)}, u32[]{:S(2)}) copy-start(f32[16,256]{1,0:T(8,128)} %shard_map.190) | copy-start | bytes 49156
  84.9 4.0 %copy-start.5 = (f32[1,16,256]{2,1,0:T(8,128)S(1)}, f32[1,16,256]{2,1,0:T(8,128)}, u32[]{:S(2)}) copy-start(f32[1,16,256]{2,1,0:T(8,128)} %param.20) | copy-start | bytes 49156
  93.1 48.0 %copy-start.10 = (f32[256]{0:T(256)S(1)}, f32[256]{0:T(256)}, u32[]{:S(2)}) copy-start(f32[256]{0:T(256)} %param.19) | copy-start | bytes 3076
  93.1 48.7 %copy-start.12 = (bf16[1,1024,224]{1,2,0:T(8,128)(2,1)S(1)}, bf16[1,1024,224]{1,2,0:T(8,128)(2,1)}, u32[]{:S(2)}) copy-start(bf16[1,1024,224]{1,2,0:T(8,128)(2,1)} %param.27) | copy-start | bytes 1376260
  141.7 6.8 %copy-start.11 = (bf16[1,1024,4096]{2,1,0:T(8,128)(2,1)S(1)}, bf16[1,1024,4096]{2,1,0:T(8,128)(2,1)}, u32[]{:S(2)}) copy-start(bf16[1,1024,4096]{2,1,0:T(8,128)(2,1)} %all-gather.2.cloned.1.call-done) | copy-start | bytes 25165828
Sparse Core Ops, SparseCore 0:
  26.7 87.4 all-gather.1

commit v5 on v4

--- a/solution.py
+++ b/solution.py
@@ -60,51 +60,6 @@
             flops=2 * decays.size, bytes_accessed=12 * decays.size, transcendentals=0
         ),
     )(decays, sources, entering)
-
-
-def exchange_kernel(axis, count, same, x_ref, out_ref, land, send_sems, recv_sems):
-    me = lax.axis_index(axis)
-    barrier = pltpu.get_barrier_semaphore()
-    for k in range(1, count):
-        pl.semaphore_signal(
-            barrier,
-            1,
-            device_id={axis: lax.rem(me + k, count)},
-            device_id_type=pl.DeviceIdType.MESH,
-        )
-    pl.semaphore_wait(barrier, count - 1)
-    copies = []
-    for k in range(1, count):
-        peer = lax.rem(me + k, count)
-        copy = pltpu.make_async_remote_copy(
-            src_ref=x_ref if same else x_ref.at[peer],
-            dst_ref=land.at[me],
-            send_sem=send_sems.at[k],
-            recv_sem=recv_sems.at[k],
-            device_id={axis: peer},
-            device_id_type=pl.DeviceIdType.MESH,
-        )
-        copy.start()
-        copies.append(copy)
-    land[me] = x_ref[...] if same else x_ref[me]
-    for copy in copies:
-        copy.wait()
-    out_ref[...] = land[...]
-
-
-def exchange(x, axis, same, collective_id):
-    count = lax.axis_size(axis)
-    block = x.shape if same else x.shape[1:]
-    return pl.pallas_call(
-        functools.partial(exchange_kernel, axis, count, same),
-        out_shape=jax.ShapeDtypeStruct((count,) + block, x.dtype),
-        scratch_shapes=[
-            pltpu.VMEM((count,) + block, x.dtype),
-            pltpu.SemaphoreType.DMA((count,)),
-            pltpu.SemaphoreType.DMA((count,)),
-        ],
-        compiler_params=pltpu.CompilerParams(collective_id=collective_id, has_side_effects=True),
-    )(x)
 
 
 def relay_kernel(axis, count, pair_ref, out_ref, held, land, send_sems, recv_sems):
@@ -176,6 +131,72 @@
         ],
         compiler_params=pltpu.CompilerParams(collective_id=collective_id, has_side_effects=True),
     )(pair)
+
+
+def reduce_kernel(cols_ref, parts_ref, cols_out, rate_out, cols_land, parts_land, chunk, chunk_land, sems):
+    me_e, me_c = lax.axis_index("exp"), lax.axis_index("ctx")
+    n_e, n_c = lax.axis_size("exp"), lax.axis_size("ctx")
+    mesh_id = pl.DeviceIdType.MESH
+    barrier = pltpu.get_barrier_semaphore()
+    for k in range(1, n_e):
+        pl.semaphore_signal(barrier, 1, device_id={"exp": lax.rem(me_e + k, n_e)}, device_id_type=mesh_id)
+    for k in range(1, n_c):
+        pl.semaphore_signal(barrier, 1, device_id={"ctx": lax.rem(me_c + k, n_c)}, device_id_type=mesh_id)
+    pl.semaphore_wait(barrier, n_e - 1 + n_c - 1)
+
+    def push(src, dst, axis, peer, slot):
+        copy = pltpu.make_async_remote_copy(
+            src_ref=src,
+            dst_ref=dst,
+            send_sem=sems.at[0, slot],
+            recv_sem=sems.at[1, slot],
+            device_id={axis: peer},
+            device_id_type=mesh_id,
+        )
+        copy.start()
+        return copy
+
+    scattered = [
+        push(parts_ref.at[lax.rem(me_c + k, n_c)], parts_land.at[me_c], "ctx", lax.rem(me_c + k, n_c), k)
+        for k in range(1, n_c)
+    ]
+    gathered = [
+        push(cols_ref, cols_land.at[me_e], "exp", lax.rem(me_e + k, n_e), 2 * n_c + k)
+        for k in range(1, n_e)
+    ]
+    parts_land[me_c] = parts_ref[me_c]
+    cols_land[me_e] = cols_ref[...]
+    for copy in scattered:
+        copy.wait()
+    chunk[...] = jnp.sum(parts_land[...], axis=0)
+    chunk_land[me_c] = chunk[...]
+    spread = [
+        push(chunk, chunk_land.at[me_c], "ctx", lax.rem(me_c + k, n_c), n_c + k)
+        for k in range(1, n_c)
+    ]
+    for copy in gathered + spread:
+        copy.wait()
+    cols_out[...] = cols_land[...]
+    rate_out[...] = chunk_land[...]
+
+
+def reduce_partials(cols, parts, collective_id):
+    n_e, n_c = lax.axis_size("exp"), lax.axis_size("ctx")
+    return pl.pallas_call(
+        reduce_kernel,
+        out_shape=(
+            jax.ShapeDtypeStruct((n_e,) + cols.shape, cols.dtype),
+            jax.ShapeDtypeStruct(parts.shape, parts.dtype),
+        ),
+        scratch_shapes=[
+            pltpu.VMEM((n_e,) + cols.shape, cols.dtype),
+            pltpu.VMEM(parts.shape, parts.dtype),
+            pltpu.VMEM(parts.shape[1:], parts.dtype),
+            pltpu.VMEM(parts.shape, parts.dtype),
+            pltpu.SemaphoreType.DMA((2, 2 * n_c + n_e)),
+        ],
+        compiler_params=pltpu.CompilerParams(collective_id=collective_id, has_side_effects=True),
+    )(cols, parts)
 
 
 def slot_buffer(moe_grad, route, gate_prob, capacity):
@@ -245,12 +266,12 @@
     ).astype(jnp.bfloat16)
     in_cols = jnp.sum(adjoint * (steps * inputs)[:, None, :], axis=2)
     rate_local = jnp.sum(adjoint * (-steps[:, None, :] * decays * before), axis=0)
-    col_sums = jnp.sum(exchange(jnp.stack([in_cols.T, out_cols.T]), "exp", True, 1), axis=0)
-    in_proj_grad, out_proj_grad = col_sums[0], col_sums[1]
     ctx_count = lax.axis_size("ctx")
     rate_parts = rate_local.reshape(ctx_count, 1, rate_local.size // ctx_count)
-    rate_chunk = jnp.sum(exchange(rate_parts, "ctx", False, 2), axis=0)
-    decay_grad = exchange(rate_chunk, "ctx", True, 3).reshape(rate_local.shape)
+    col_parts, rate_chunks = reduce_partials(jnp.stack([in_cols.T, out_cols.T]), rate_parts, 1)
+    col_sums = jnp.sum(col_parts, axis=0)
+    in_proj_grad, out_proj_grad = col_sums[0], col_sums[1]
+    decay_grad = rate_chunks.reshape(rate_local.shape)
     slot_total = hidden_saved.shape[1]
     capacity = slot_total // (lax.axis_size("ctx") * lax.axis_size("exp"))
     buffer = slot_buffer(moe_grad, route, gate_prob, capacity)

time: 160 us -> 138 us (0.86)
  Pallas kernels: 91.8 us -> 71.9 us
    pallas_call x3 -> x1, Pallas kernels: 39.2 us -> 19.3 us  [reduce_partials(): pl.pallas_call(reduce_kernel, out_shape=(jax.ShapeDtypeStruct((n_e,) + co...]
  transfers between devices with their start and end apart: 1 -> 1, of which waited for: 0 -> 0; matrix products, arithmetic and copies ran while one was open for 15% -> 16% of each run, Pallas kernels for 58% -> 52%
where the time goes in v5:
time: 138 us
  Pallas kernels  71.9 us (52%)
  other arithmetic  16.4 us (12%)
  blocking collectives  14.8 us (11%)
  between operations  14.2 us (10%)
  matrix products  10.6 us (8%)
  local copies, waits for them, and re-layouts  9.76 us (7%)
    pallas_call x1, Pallas kernels, relay(): pl.pallas_call(functools.partial(relay_kernel, axis, count), out_shape=ja...  43.7 us
    pallas_call x1, Pallas kernels, reduce_partials(): pl.pallas_call(reduce_kernel, out_shape=(jax.ShapeDtypeStruct((n_e,) + co...  19.3 us
    all_to_all x1, blocking collectives, body(): lax.all_to_all(buffer, 'exp', split_axis=0, concat_axis=1, tiled=True)  14.8 us
    dot_general x1, matrix products, body(): jnp.einsum('lrf,lrd->lfd', hidden_saved, all_rows, preferred_element_type...  6.83 us
    pallas_call x1, Pallas kernels, local_scans(): pl.pallas_call(local_scans_kernel, out_shape=(jax.ShapeDtypeStruct(decays...  4.92 us
    reduce_sum x1, other arithmetic, body(): jnp.sum(adjoint * (-steps[:, None, :] * decays * before), axis=0)  4.22 us
    pallas_call x1, Pallas kernels, adjoint_scan(): pl.pallas_call(adjoint_scan_kernel, out_shape=jax.ShapeDtypeStruct(decays...  3.95 us
    dot_general x1, matrix products, body(): jnp.einsum('lrd,lfd->lrf', all_rows, w_down, preferred_element_type=jnp.f...  3.41 us
  transfers between devices with their start and end apart: 1, of which 0 were waited for; matrix products, arithmetic and copies ran while one was open for 16% of the time, Pallas kernels for 52%

profile of v5, /device:TPU:1, one launch (start us, length us, event | category | flops | bytes accessed | tf_op | source)
XLA Modules:
  0.0 137.6 jit_solution(11745931455208662697)
XLA Ops:
  7.2 0.0 copy-start
  7.2 0.0 copy-start.8
  7.2 0.0 copy-start.1
  7.2 0.0 copy-start.9
  7.2 0.0 copy-start.2
  7.2 0.0 copy-start.3
  7.2 0.0 all-gather.2.cloned.1.call-start
  7.3 0.9 copy.33
  8.2 0.1 reshape.70
  8.2 0.1 fusion.26
  8.4 0.2 select_reduce_fusion
  8.5 0.9 mul.177
  9.5 0.2 mul.178
  9.7 0.8 copy.34
  10.4 0.1 mul.175
  10.5 0.3 convolution_convert_fusion
  10.9 0.2 reshape.71
  11.0 14.8 %all_to_all.12 = bf16[16,2,4096]{2,1,0:T(2,128)(2,1)S(1)} all-to-all(bf16[16,2,4096]{2,1,0:T(2,128)(2,1)S(1)} %reshape.71), channel_id=1, replica_groups=mesh['ctx'=32,'exp'=16] {'exp'}, dimensions={0} | all-to-all | bytes 524288 | tf_op jit(solution)/shard_map/all_to_all | solution.py:278
  25.8 0.0 copy-start.4
  25.8 0.8 all_to_all.10
  26.6 0.0 all-gather.2.cloned.1.call-update
  26.6 0.0 copy-done.8
  26.6 0.1 copy.29
  26.7 0.0 copy-done.1
  26.8 0.0 copy-done.9
  26.8 0.1 copy.30
  26.9 0.0 copy-done.2
  26.9 0.0 copy-done.3
  27.0 1.6 %broadcast_multiply_fusion.1.source_ref = f32[128,16,256]{2,1,0:T(8,128)} fusion(f32[128,256]{1,0:T(8,128)S(1)} %convert_element_type.45, f32[128,16]{1,0:T(8,128)S(1)} %copy.30), kind=kLoop, calls=%fused_computation.18 | loop fusion | flops 524288 | bytes 2236416 | tf_op jit(solution)/shard_map/mul | solution.py:247
  28.6 0.0 copy-done.4
  28.6 2.5 %multiply_exponential_fusion = (f32[128,16,256]{2,1,0:T(8,128)}, f32[128,16,256]{2,1,0:T(8,128)}) fusion(f32[16,256]{1,0:T(8,128)S(1)} %copy-done.4, f32[128,256]{1,0:T(8,128)S(1)} %get-tuple-element.21, f32[128,16]{1,0:T(8,128)S(1)} %copy.29, f32[128,256]{1,0:T(8,128)S(1)} %get-tuple-element.20), kind=kLoop, calls=%fused_computation.13 | loop fusion | flops 1048576 | bytes 4481024 | tf_op jit(solution)/shard_map/exp | solution.py:245
  31.1 0.0 copy-start.7
  31.1 4.9 %shard_map.189 = (f32[128,16,256]{2,1,0:T(8,128)}, f32[16,256]{1,0:T(8,128)}) custom-call(f32[128,16,256]{2,1,0:T(8,128)} %get-tuple-element.26.decay_ref, f32[128,16,256]{2,1,0:T(8,128)} %get-tuple-element.27.drive_ref, f32[128,16,256]{2,1,0:T(8,128)} %broadcast_multiply_fusion.1.source_ref, f32[16,256]{1,0:T(8,128)} %bitcast.46), custom_call_target="tpu_custom_call" | custom-call | flops 2097152 | bytes 8388608 | tf_op jit(solution)/shard_map/pallas_call | solution.py:31
  36.0 0.0 copy-done.7
  36.0 0.7 select_bitcast_fusion
  36.8 0.6 pad_maximum_fusion.1.pair_ref
  37.4 43.7 %shard_map.190 = f32[16,256]{1,0:T(8,128)} custom-call(f32[2,16,256]{2,1,0:T(8,128)} %pad_maximum_fusion.1.pair_ref), custom_call_target="tpu_custom_call" | custom-call | tf_op jit(solution)/shard_map/pallas_call | solution.py:123
  81.1 0.0 copy-start.6
  81.1 3.1 %slice.9 = f32[127,16,256]{2,1,0:T(8,128)} slice(f32[128,16,256]{2,1,0:T(8,128)} %get-tuple-element.12), slice={[0:127], [0:16], [0:256]} | slice | bytes 4161536 | tf_op jit(solution)/shard_map/slice | solution.py:249
  84.3 0.0 copy-done.6
  84.3 0.6 broadcast_select_fusion.entering_ref
  84.9 0.0 copy-start.5
  84.9 4.0 %shard_map.191 = f32[128,16,256]{2,1,0:T(8,128)} custom-call(f32[128,16,256]{2,1,0:T(8,128)} %get-tuple-element.26.decay_ref, f32[128,16,256]{2,1,0:T(8,128)} %broadcast_multiply_fusion.1.source_ref, f32[16,256]{1,0:T(8,128)} %broadcast_select_fusion.entering_ref), custom_call_target="tpu_custom_call" | custom-call | flops 1048576 | bytes 6291456 | tf_op jit(solution)/shard_map/pallas_call | solution.py:56
  88.8 0.0 copy-done.5
  88.8 4.2 %multiply_reduce_fusion = (f32[16,256]{1,0:T(8,128)S(1)}, bf16[128,256]{1,0:T(8,128)(2,1)}, f32[128,256]{1,0:T(8,128)S(1)}, f32[128,16]{1,0:T(8,128)S(1)}) fusion(f32[128,16,256]{2,1,0:T(8,128)} %shard_map.191, f32[127,16,256]{2,1,0:T(8,128)} %slice.9, f32[1,16,256]{2,1,0:T(8,128)S(1)} %copy-done.5, f32[16,256]{1,0:T(8,128)S(1)} %copy-done.4, ...), kind=kLoop, calls=%fused_computation.8 | loop fusion | flops 8316928 | bytes 4833280 | tf_op jit(solution)/shard_map/reduce_sum | solution.py:268
  93.1 0.0 copy-start.10
  93.1 0.0 copy-start.12
  93.1 2.0 %multiply_reduce_fusion.1 = f32[128,16]{1,0:T(8,128)S(1)} fusion(f32[128,16,256]{2,1,0:T(8,128)} %get-tuple-element.12, f32[128,256]{1,0:T(8,128)S(1)} %convert_element_type.45), kind=kLoop, calls=%fused_computation.9 | loop fusion | flops 1046528 | bytes 2236416 | tf_op jit(solution)/shard_map/reduce_sum | solution.py:250
  95.2 0.1 copy.32
  95.2 0.6 reshape.68.parts_ref
  95.9 0.6 pad_maximum_fusion.2.cols_ref
  96.5 19.3 %shard_map.192 = (f32[16,2,16,128]{3,2,1,0:T(8,128)}, f32[32,1,128]{2,1,0:T(1,128)}) custom-call(f32[2,16,128]{2,1,0:T(8,128)} %pad_maximum_fusion.2.cols_ref, f32[32,1,128]{2,1,0:T(1,128)} %reshape.68.parts_ref), custom_call_target="tpu_custom_call" | custom-call | tf_op jit(solution)/shard_map/pallas_call | solution.py:185
  115.8 0.5 broadcast.29
  116.3 1.4 %reduce.3 = f32[32,128]{1,0:T(8,128)S(1)} reduce(f32[32,1,128]{2,1,0:T(1,128)} %get-tuple-element.14, f32[]{:T(128)} %broadcast.29), dimensions={1}, to_apply=%get-tuple-element.14.reduce_sub_computation.3 | reduce | bytes 32772 | tf_op jit(solution)/shard_map/pallas_call | solution.py:185
  117.7 0.6 reshape.69
  118.3 1.0 reduce_sum.78
  119.3 0.6 slice_bitcast_fusion
  119.9 0.0 copy-done.10
  119.9 0.7 fusion.23
  120.5 0.0 copy-done.12
  120.6 6.8 %fusion.7 = bf16[1,224,4096]{2,1,0:T(8,128)(2,1)} fusion(bf16[1,1024,4096]{2,1,0:T(8,128)(2,1)} %all-gather.2.cloned.1.call-done, bf16[1,1024,224]{1,2,0:T(8,128)(2,1)S(1)} %copy-done.12), kind=kOutput, calls=%fused_computation.5 | convolution fusion | flops 1879965696 | bytes 10682368 | tf_op jit(solution)/shard_map/lrf,lrd->lfd/dot_general | solution.py:280
  127.4 0.0 copy-done
  127.4 0.0 copy-done.11
  127.4 3.4 %fusion.16 = bf16[1,1024,224]{1,2,0:T(8,128)(2,1)} fusion(bf16[1,224,4096]{2,1,0:T(8,128)(2,1)S(1)} %copy-done, bf16[1,1024,4096]{2,1,0:T(8,128)(2,1)S(1)} %copy-done.11), kind=kOutput, calls=%fused_computation.16 | convolution fusion | flops 1879277568 | bytes 10682368 | tf_op jit(solution)/shard_map/lrd,lfd->lrf/dot_general | solution.py:283
  (8 shorter events, 0.2 us)
Async XLA Ops:
  7.2 120.2 %copy-start = (bf16[1,224,4096]{2,1,0:T(8,128)(2,1)S(1)}, bf16[1,224,4096]{2,1,0:T(8,128)(2,1)}, u32[]{:S(2)}) copy-start(bf16[1,224,4096]{2,1,0:T(8,128)(2,1)} %param.26) | copy-start | bytes 5505028
  7.2 19.4 %copy-start.8 = (f32[16,128]{1,0:T(8,128)S(1)}, f32[16,128]{1,0:T(8,128)}, u32[]{:S(2)}) copy-start(f32[16,128]{1,0:T(8,128)} %param.17) | copy-start | bytes 24580
  7.2 19.5 %copy-start.1 = (bf16[128,256]{1,0:T(8,128)(2,1)S(1)}, bf16[128,256]{1,0:T(8,128)(2,1)}, u32[]{:S(2)}) copy-start(bf16[128,256]{1,0:T(8,128)(2,1)} %param.22) | copy-start | bytes 196612
  7.2 19.6 %copy-start.9 = (f32[16,128]{1,0:T(8,128)S(1)}, f32[16,128]{1,0:T(8,128)}, u32[]{:S(2)}) copy-start(f32[16,128]{1,0:T(8,128)} %param.18) | copy-start | bytes 24580
  7.2 19.7 %copy-start.2 = (bf16[128,256]{1,0:T(8,128)(2,1)S(1)}, bf16[128,256]{1,0:T(8,128)(2,1)}, u32[]{:S(2)}) copy-start(bf16[128,256]{1,0:T(8,128)(2,1)} %param.14) | copy-start | bytes 196612
  7.2 19.7 %copy-start.3 = (bf16[128,256]{1,0:T(8,128)(2,1)S(1)}, bf16[128,256]{1,0:T(8,128)(2,1)}, u32[]{:S(2)}) copy-start(bf16[128,256]{1,0:T(8,128)(2,1)} %param.15) | copy-start | bytes 196612
  7.2 113.3 %all-gather.2.cloned.1.call-start = ((), (), s32[]{:S(2)}) async-start(), calls=%async_computation.1 | async-start | bytes 8650752 | tf_op jit(solution)/shard_map/all_gather | solution.py:279
  25.8 2.8 %copy-start.4 = (f32[16,256]{1,0:T(8,128)S(1)}, f32[16,256]{1,0:T(8,128)}, u32[]{:S(2)}) copy-start(f32[16,256]{1,0:T(8,128)} %param.16) | copy-start | bytes 49156
  31.1 4.9 %copy-start.7 = (f32[16,256]{1,0:T(8,128)S(1)}, f32[16,256]{1,0:T(8,128)}, u32[]{:S(2)}) copy-start(f32[16,256]{1,0:T(8,128)} %param.21) | copy-start | bytes 49156
  81.1 3.2 %copy-start.6 = (f32[16,256]{1,0:T(8,128)S(1)}, f32[16,256]{1,0:T(8,128)}, u32[]{:S(2)}) copy-start(f32[16,256]{1,0:T(8,128)} %shard_map.190) | copy-start | bytes 49156
  84.9 4.0 %copy-start.5 = (f32[1,16,256]{2,1,0:T(8,128)S(1)}, f32[1,16,256]{2,1,0:T(8,128)}, u32[]{:S(2)}) copy-start(f32[1,16,256]{2,1,0:T(8,128)} %param.20) | copy-start | bytes 49156
  93.1 26.8 %copy-start.10 = (f32[256]{0:T(256)S(1)}, f32[256]{0:T(256)}, u32[]{:S(2)}) copy-start(f32[256]{0:T(256)} %param.19) | copy-start | bytes 3076
  93.1 27.5 %copy-start.12 = (bf16[1,1024,224]{1,2,0:T(8,128)(2,1)S(1)}, bf16[1,1024,224]{1,2,0:T(8,128)(2,1)}, u32[]{:S(2)}) copy-start(bf16[1,1024,224]{1,2,0:T(8,128)(2,1)} %param.27) | copy-start | bytes 1376260
  120.5 6.8 %copy-start.11 = (bf16[1,1024,4096]{2,1,0:T(8,128)(2,1)S(1)}, bf16[1,1024,4096]{2,1,0:T(8,128)(2,1)}, u32[]{:S(2)}) copy-start(bf16[1,1024,4096]{2,1,0:T(8,128)(2,1)} %all-gather.2.cloned.1.call-done) | copy-start | bytes 25165828
Sparse Core Ops, SparseCore 0:
  26.7 87.7 all-gather.1

commit v6 on v5

--- a/solution.py
+++ b/solution.py
@@ -62,72 +62,104 @@
     )(decays, sources, entering)
 
 
-def relay_kernel(axis, count, pair_ref, out_ref, held, land, send_sems, recv_sems):
+def relay_kernel(axis, count, radix, pair_ref, out_ref, held, land, send_sems, recv_sems):
     me = lax.axis_index(axis)
-    distances = []
-    while 1 << len(distances) < count:
-        distances.append(1 << len(distances))
+    mesh_id = pl.DeviceIdType.MESH
+    distances = [1]
+    while distances[-1] * radix < count:
+        distances.append(distances[-1] * radix)
+    offsets = sorted({d * m for d in distances for m in range(1, radix)})
     land[...] = jnp.zeros_like(land)
     barrier = pltpu.get_barrier_semaphore()
     expected = 0
-    for d in distances:
-
-        @pl.when(me >= d)
+    for o in offsets:
+
+        @pl.when(me >= o)
         def _():
-            pl.semaphore_signal(barrier, 1, device_id={axis: me - d}, device_id_type=pl.DeviceIdType.MESH)
-
-        @pl.when(me + d < count)
+            pl.semaphore_signal(barrier, 1, device_id={axis: me - o}, device_id_type=mesh_id)
+
+        @pl.when(me + o < count)
         def _():
-            pl.semaphore_signal(barrier, 1, device_id={axis: me + d}, device_id_type=pl.DeviceIdType.MESH)
-
-        expected = expected + (me >= d).astype(jnp.int32) + (me + d < count).astype(jnp.int32)
+            pl.semaphore_signal(barrier, 1, device_id={axis: me + o}, device_id_type=mesh_id)
+
+        expected = expected + (me >= o).astype(jnp.int32) + (me + o < count).astype(jnp.int32)
     pl.semaphore_wait(barrier, expected)
-    rounds = distances + [1]
-    for r, d in enumerate(rounds):
-        last_round = r == len(rounds) - 1
+    slot = 0
+    for r, d in enumerate(distances):
         source = pair_ref if r == 0 else held.at[r - 1]
-        copy = pltpu.make_async_remote_copy(
-            src_ref=source,
-            dst_ref=land.at[r],
-            send_sem=send_sems.at[r],
-            recv_sem=recv_sems.at[r],
-            device_id={axis: lax.rem(me - d + count, count)},
-            device_id_type=pl.DeviceIdType.MESH,
-        )
-
-        @pl.when(me >= d)
-        def _():
-            copy.start()
-
-        if not last_round:
-            held[r] = source[...]
-
-        @pl.when(me + d < count)
-        def _():
-            copy.wait_recv()
-            if not last_round:
-                shrink, seed = source[0], source[1]
-                held[r, 0] = shrink * land[r, 0]
-                held[r, 1] = shrink * land[r, 1] + seed
-
-        @pl.when(me >= d)
-        def _():
-            copy.wait_send()
-
-    out_ref[...] = land[len(rounds) - 1, 1]
-
-
-def relay(pair, axis, collective_id):
+        copies = []
+        for m in range(1, radix):
+            o = d * m
+            copy = pltpu.make_async_remote_copy(
+                src_ref=source,
+                dst_ref=land.at[slot],
+                send_sem=send_sems.at[slot],
+                recv_sem=recv_sems.at[slot],
+                device_id={axis: lax.rem(me - o + count, count)},
+                device_id_type=mesh_id,
+            )
+            copies.append((o, slot, copy))
+            slot += 1
+
+            @pl.when(me >= o)
+            def _():
+                copy.start()
+
+        held[r] = source[...]
+        for o, s, copy in copies:
+
+            @pl.when(me + o < count)
+            def _():
+                copy.wait_recv()
+                shrink, seed = held[r, 0], held[r, 1]
+                held[r, 0] = shrink * land[s, 0]
+                held[r, 1] = shrink * land[s, 1] + seed
+
+        for o, s, copy in copies:
+
+            @pl.when(me >= o)
+            def _():
+                copy.wait_send()
+
+    last = len(distances) - 1
+    shift = pltpu.make_async_remote_copy(
+        src_ref=held.at[last],
+        dst_ref=land.at[slot],
+        send_sem=send_sems.at[slot],
+        recv_sem=recv_sems.at[slot],
+        device_id={axis: lax.rem(me - 1 + count, count)},
+        device_id_type=mesh_id,
+    )
+
+    @pl.when(me >= 1)
+    def _():
+        shift.start()
+
+    @pl.when(me + 1 < count)
+    def _():
+        shift.wait_recv()
+
+    @pl.when(me >= 1)
+    def _():
+        shift.wait_send()
+
+    out_ref[...] = land[slot, 1]
+
+
+def relay(pair, axis, collective_id, radix=4):
     count = lax.axis_size(axis)
-    rounds = max(1, (count - 1).bit_length()) + 1
+    rounds = 1
+    while radix**rounds < count:
+        rounds += 1
+    slots = rounds * (radix - 1) + 1
     return pl.pallas_call(
-        functools.partial(relay_kernel, axis, count),
+        functools.partial(relay_kernel, axis, count, radix),
         out_shape=jax.ShapeDtypeStruct(pair.shape[1:], pair.dtype),
         scratch_shapes=[
-            pltpu.VMEM((rounds - 1,) + pair.shape, pair.dtype),
             pltpu.VMEM((rounds,) + pair.shape, pair.dtype),
-            pltpu.SemaphoreType.DMA((rounds,)),
-            pltpu.SemaphoreType.DMA((rounds,)),
+            pltpu.VMEM((slots,) + pair.shape, pair.dtype),
+            pltpu.SemaphoreType.DMA((slots,)),
+            pltpu.SemaphoreType.DMA((slots,)),
         ],
         compiler_params=pltpu.CompilerParams(collective_id=collective_id, has_side_effects=True),
     )(pair)

time: 138 us -> 140 us (1.014)
  Pallas kernels: 71.9 us -> 73.4 us
  transfers between devices with their start and end apart: 1 -> 1, of which waited for: 0 -> 0; matrix products, arithmetic and copies ran while one was open for 16% -> 16% of each run, Pallas kernels for 52% -> 53%
where the time goes in v6:
time: 140 us; the launch traced here: 139 us
  Pallas kernels  73.4 us (52%)
  other arithmetic  16.4 us (12%)
  blocking collectives  14.8 us (11%)
  between operations  14.2 us (10%)
  matrix products  10.6 us (8%)
  local copies, waits for them, and re-layouts  9.73 us (7%)
    pallas_call x1, Pallas kernels, relay(): pl.pallas_call(functools.partial(relay_kernel, axis, count, radix), out_s...  44.7 us
    pallas_call x1, Pallas kernels, reduce_partials(): pl.pallas_call(reduce_kernel, out_shape=(jax.ShapeDtypeStruct((n_e,) + co...  19.8 us
    all_to_all x1, blocking collectives, body(): lax.all_to_all(buffer, 'exp', split_axis=0, concat_axis=1, tiled=True)  14.8 us
    dot_general x1, matrix products, body(): jnp.einsum('lrf,lrd->lfd', hidden_saved, all_rows, preferred_element_type...  6.83 us
    pallas_call x1, Pallas kernels, local_scans(): pl.pallas_call(local_scans_kernel, out_shape=(jax.ShapeDtypeStruct(decays...  4.92 us
    reduce_sum x1, other arithmetic, body(): jnp.sum(adjoint * (-steps[:, None, :] * decays * before), axis=0)  4.18 us
    pallas_call x1, Pallas kernels, adjoint_scan(): pl.pallas_call(adjoint_scan_kernel, out_shape=jax.ShapeDtypeStruct(decays...  3.95 us
    dot_general x1, matrix products, body(): jnp.einsum('lrd,lfd->lrf', all_rows, w_down, preferred_element_type=jnp.f...  3.42 us
  transfers between devices with their start and end apart: 1, of which 0 were waited for; matrix products, arithmetic and copies ran while one was open for 16% of the time, Pallas kernels for 53%

profile of v6, /device:TPU:1, one launch (start us, length us, event | category | flops | bytes accessed | tf_op | source)
XLA Modules:
  0.0 139.1 jit_solution(1864413186419921148)
XLA Ops:
  7.2 0.0 copy-start
  7.2 0.0 copy-start.8
  7.2 0.0 copy-start.1
  7.2 0.0 copy-start.9
  7.2 0.0 copy-start.2
  7.2 0.0 copy-start.3
  7.2 0.0 all-gather.2.cloned.1.call-start
  7.3 0.9 copy.33
  8.2 0.1 reshape.70
  8.2 0.1 fusion.26
  8.4 0.2 select_reduce_fusion
  8.5 0.9 mul.177
  9.5 0.2 mul.178
  9.7 0.8 copy.34
  10.4 0.1 mul.175
  10.5 0.3 convolution_convert_fusion
  10.9 0.2 reshape.71
  11.0 14.8 %all_to_all.12 = bf16[16,2,4096]{2,1,0:T(2,128)(2,1)S(1)} all-to-all(bf16[16,2,4096]{2,1,0:T(2,128)(2,1)S(1)} %reshape.71), channel_id=1, replica_groups=mesh['ctx'=32,'exp'=16] {'exp'}, dimensions={0} | all-to-all | bytes 524288 | tf_op jit(solution)/shard_map/all_to_all | solution.py:310
  25.8 0.0 copy-start.4
  25.8 0.8 all_to_all.10
  26.6 0.0 all-gather.2.cloned.1.call-update
  26.6 0.0 copy-done.8
  26.6 0.1 copy.29
  26.7 0.0 copy-done.1
  26.8 0.0 copy-done.9
  26.8 0.1 copy.30
  26.9 0.0 copy-done.2
  26.9 0.0 copy-done.3
  27.0 1.6 %broadcast_multiply_fusion.1.source_ref = f32[128,16,256]{2,1,0:T(8,128)} fusion(f32[128,256]{1,0:T(8,128)S(1)} %convert_element_type.45, f32[128,16]{1,0:T(8,128)S(1)} %copy.30), kind=kLoop, calls=%fused_computation.18 | loop fusion | flops 524288 | bytes 2236416 | tf_op jit(solution)/shard_map/mul | solution.py:279
  28.6 0.0 copy-done.4
  28.6 2.5 %multiply_exponential_fusion = (f32[128,16,256]{2,1,0:T(8,128)}, f32[128,16,256]{2,1,0:T(8,128)}) fusion(f32[16,256]{1,0:T(8,128)S(1)} %copy-done.4, f32[128,256]{1,0:T(8,128)S(1)} %get-tuple-element.21, f32[128,16]{1,0:T(8,128)S(1)} %copy.29, f32[128,256]{1,0:T(8,128)S(1)} %get-tuple-element.20), kind=kLoop, calls=%fused_computation.13 | loop fusion | flops 1048576 | bytes 4481024 | tf_op jit(solution)/shard_map/exp | solution.py:277
  31.1 0.0 copy-start.7
  31.1 4.9 %shard_map.189 = (f32[128,16,256]{2,1,0:T(8,128)}, f32[16,256]{1,0:T(8,128)}) custom-call(f32[128,16,256]{2,1,0:T(8,128)} %get-tuple-element.26.decay_ref, f32[128,16,256]{2,1,0:T(8,128)} %get-tuple-element.27.drive_ref, f32[128,16,256]{2,1,0:T(8,128)} %broadcast_multiply_fusion.1.source_ref, f32[16,256]{1,0:T(8,128)} %bitcast.46), custom_call_target="tpu_custom_call" | custom-call | flops 2097152 | bytes 8388608 | tf_op jit(solution)/shard_map/pallas_call | solution.py:31
  36.0 0.0 copy-done.7
  36.0 0.7 select_bitcast_fusion
  36.8 0.6 pad_maximum_fusion.1.pair_ref
  37.4 44.7 %shard_map.190 = f32[16,256]{1,0:T(8,128)} custom-call(f32[2,16,256]{2,1,0:T(8,128)} %pad_maximum_fusion.1.pair_ref), custom_call_target="tpu_custom_call" | custom-call | tf_op jit(solution)/shard_map/pallas_call | solution.py:155
  82.1 0.0 copy-start.6
  82.1 3.1 %slice.9 = f32[127,16,256]{2,1,0:T(8,128)} slice(f32[128,16,256]{2,1,0:T(8,128)} %get-tuple-element.12), slice={[0:127], [0:16], [0:256]} | slice | bytes 4161536 | tf_op jit(solution)/shard_map/slice | solution.py:281
  85.2 0.0 copy-done.6
  85.2 0.6 broadcast_select_fusion.entering_ref
  85.8 0.0 copy-start.5
  85.8 3.9 %shard_map.191 = f32[128,16,256]{2,1,0:T(8,128)} custom-call(f32[128,16,256]{2,1,0:T(8,128)} %get-tuple-element.26.decay_ref, f32[128,16,256]{2,1,0:T(8,128)} %broadcast_multiply_fusion.1.source_ref, f32[16,256]{1,0:T(8,128)} %broadcast_select_fusion.entering_ref), custom_call_target="tpu_custom_call" | custom-call | flops 1048576 | bytes 6291456 | tf_op jit(solution)/shard_map/pallas_call | solution.py:56
  89.8 0.0 copy-done.5
  89.8 4.2 %multiply_reduce_fusion = (f32[16,256]{1,0:T(8,128)S(1)}, bf16[128,256]{1,0:T(8,128)(2,1)}, f32[128,256]{1,0:T(8,128)S(1)}, f32[128,16]{1,0:T(8,128)S(1)}) fusion(f32[128,16,256]{2,1,0:T(8,128)} %shard_map.191, f32[127,16,256]{2,1,0:T(8,128)} %slice.9, f32[1,16,256]{2,1,0:T(8,128)S(1)} %copy-done.5, f32[16,256]{1,0:T(8,128)S(1)} %copy-done.4, ...), kind=kLoop, calls=%fused_computation.8 | loop fusion | flops 8316928 | bytes 4833280 | tf_op jit(solution)/shard_map/reduce_sum | solution.py:300
  94.0 0.0 copy-start.10
  94.0 0.0 copy-start.12
  94.0 2.0 %multiply_reduce_fusion.1 = f32[128,16]{1,0:T(8,128)S(1)} fusion(f32[128,16,256]{2,1,0:T(8,128)} %get-tuple-element.12, f32[128,256]{1,0:T(8,128)S(1)} %convert_element_type.45), kind=kLoop, calls=%fused_computation.9 | loop fusion | flops 1046528 | bytes 2236416 | tf_op jit(solution)/shard_map/reduce_sum | solution.py:282
  96.1 0.1 copy.32
  96.1 0.6 reshape.68.parts_ref
  96.8 0.6 pad_maximum_fusion.2.cols_ref
  97.4 19.8 %shard_map.192 = (f32[16,2,16,128]{3,2,1,0:T(8,128)}, f32[32,1,128]{2,1,0:T(1,128)}) custom-call(f32[2,16,128]{2,1,0:T(8,128)} %pad_maximum_fusion.2.cols_ref, f32[32,1,128]{2,1,0:T(1,128)} %reshape.68.parts_ref), custom_call_target="tpu_custom_call" | custom-call | tf_op jit(solution)/shard_map/pallas_call | solution.py:217
  117.2 0.5 broadcast.29
  117.7 1.4 %reduce.3 = f32[32,128]{1,0:T(8,128)S(1)} reduce(f32[32,1,128]{2,1,0:T(1,128)} %get-tuple-element.14, f32[]{:T(128)} %broadcast.29), dimensions={1}, to_apply=%get-tuple-element.14.reduce_sub_computation.3 | reduce | bytes 32772 | tf_op jit(solution)/shard_map/pallas_call | solution.py:217
  119.1 0.6 reshape.69
  119.7 1.0 reduce_sum.78
  120.7 0.6 slice_bitcast_fusion
  121.3 0.0 copy-done.10
  121.3 0.7 fusion.23
  122.0 0.0 copy-done.12
  122.0 6.8 %fusion.7 = bf16[1,224,4096]{2,1,0:T(8,128)(2,1)} fusion(bf16[1,1024,4096]{2,1,0:T(8,128)(2,1)} %all-gather.2.cloned.1.call-done, bf16[1,1024,224]{1,2,0:T(8,128)(2,1)S(1)} %copy-done.12), kind=kOutput, calls=%fused_computation.5 | convolution fusion | flops 1879965696 | bytes 10682368 | tf_op jit(solution)/shard_map/lrf,lrd->lfd/dot_general | solution.py:312
  128.8 0.0 copy-done
  128.8 0.0 copy-done.11
  128.8 3.4 %fusion.16 = bf16[1,1024,224]{1,2,0:T(8,128)(2,1)} fusion(bf16[1,224,4096]{2,1,0:T(8,128)(2,1)S(1)} %copy-done, bf16[1,1024,4096]{2,1,0:T(8,128)(2,1)S(1)} %copy-done.11), kind=kOutput, calls=%fused_computation.16 | convolution fusion | flops 1879277568 | bytes 10682368 | tf_op jit(solution)/shard_map/lrd,lfd->lrf/dot_general | solution.py:315
  (8 shorter events, 0.2 us)
Async XLA Ops:
  7.2 121.6 %copy-start = (bf16[1,224,4096]{2,1,0:T(8,128)(2,1)S(1)}, bf16[1,224,4096]{2,1,0:T(8,128)(2,1)}, u32[]{:S(2)}) copy-start(bf16[1,224,4096]{2,1,0:T(8,128)(2,1)} %param.26) | copy-start | bytes 5505028
  7.2 19.4 %copy-start.8 = (f32[16,128]{1,0:T(8,128)S(1)}, f32[16,128]{1,0:T(8,128)}, u32[]{:S(2)}) copy-start(f32[16,128]{1,0:T(8,128)} %param.17) | copy-start | bytes 24580
  7.2 19.5 %copy-start.1 = (bf16[128,256]{1,0:T(8,128)(2,1)S(1)}, bf16[128,256]{1,0:T(8,128)(2,1)}, u32[]{:S(2)}) copy-start(bf16[128,256]{1,0:T(8,128)(2,1)} %param.22) | copy-start | bytes 196612
  7.2 19.6 %copy-start.9 = (f32[16,128]{1,0:T(8,128)S(1)}, f32[16,128]{1,0:T(8,128)}, u32[]{:S(2)}) copy-start(f32[16,128]{1,0:T(8,128)} %param.18) | copy-start | bytes 24580
  7.2 19.7 %copy-start.2 = (bf16[128,256]{1,0:T(8,128)(2,1)S(1)}, bf16[128,256]{1,0:T(8,128)(2,1)}, u32[]{:S(2)}) copy-start(bf16[128,256]{1,0:T(8,128)(2,1)} %param.14) | copy-start | bytes 196612
  7.2 19.7 %copy-start.3 = (bf16[128,256]{1,0:T(8,128)(2,1)S(1)}, bf16[128,256]{1,0:T(8,128)(2,1)}, u32[]{:S(2)}) copy-start(bf16[128,256]{1,0:T(8,128)(2,1)} %param.15) | copy-start | bytes 196612
  7.2 114.7 %all-gather.2.cloned.1.call-start = ((), (), s32[]{:S(2)}) async-start(), calls=%async_computation.1 | async-start | bytes 8650752 | tf_op jit(solution)/shard_map/all_gather | solution.py:311
  25.8 2.8 %copy-start.4 = (f32[16,256]{1,0:T(8,128)S(1)}, f32[16,256]{1,0:T(8,128)}, u32[]{:S(2)}) copy-start(f32[16,256]{1,0:T(8,128)} %param.16) | copy-start | bytes 49156
  31.1 4.9 %copy-start.7 = (f32[16,256]{1,0:T(8,128)S(1)}, f32[16,256]{1,0:T(8,128)}, u32[]{:S(2)}) copy-start(f32[16,256]{1,0:T(8,128)} %param.21) | copy-start | bytes 49156
  82.1 3.1 %copy-start.6 = (f32[16,256]{1,0:T(8,128)S(1)}, f32[16,256]{1,0:T(8,128)}, u32[]{:S(2)}) copy-start(f32[16,256]{1,0:T(8,128)} %shard_map.190) | copy-start | bytes 49156
  85.8 4.0 %copy-start.5 = (f32[1,16,256]{2,1,0:T(8,128)S(1)}, f32[1,16,256]{2,1,0:T(8,128)}, u32[]{:S(2)}) copy-start(f32[1,16,256]{2,1,0:T(8,128)} %param.20) | copy-start | bytes 49156
  94.0 27.3 %copy-start.10 = (f32[256]{0:T(256)S(1)}, f32[256]{0:T(256)}, u32[]{:S(2)}) copy-start(f32[256]{0:T(256)} %param.19) | copy-start | bytes 3076
  94.0 28.0 %copy-start.12 = (bf16[1,1024,224]{1,2,0:T(8,128)(2,1)S(1)}, bf16[1,1024,224]{1,2,0:T(8,128)(2,1)}, u32[]{:S(2)}) copy-start(bf16[1,1024,224]{1,2,0:T(8,128)(2,1)} %param.27) | copy-start | bytes 1376260
  122.0 6.8 %copy-start.11 = (bf16[1,1024,4096]{2,1,0:T(8,128)(2,1)S(1)}, bf16[1,1024,4096]{2,1,0:T(8,128)(2,1)}, u32[]{:S(2)}) copy-start(bf16[1,1024,4096]{2,1,0:T(8,128)(2,1)} %all-gather.2.cloned.1.call-done) | copy-start | bytes 25165828
Sparse Core Ops, SparseCore 0:
  26.7 94.5 all-gather.1

commit v7 on v6

--- a/solution.py
+++ b/solution.py
@@ -62,7 +62,9 @@
     )(decays, sources, entering)
 
 
-def relay_kernel(axis, count, radix, pair_ref, out_ref, held, land, send_sems, recv_sems):
+def relay_kernel(
+    axis, count, radix, pair_ref, rows_ref, out_ref, all_rows, held, land, send_sems, recv_sems, row_sems
+):
     me = lax.axis_index(axis)
     mesh_id = pl.DeviceIdType.MESH
     distances = [1]
@@ -71,19 +73,26 @@
     offsets = sorted({d * m for d in distances for m in range(1, radix)})
     land[...] = jnp.zeros_like(land)
     barrier = pltpu.get_barrier_semaphore()
-    expected = 0
-    for o in offsets:
-
-        @pl.when(me >= o)
-        def _():
-            pl.semaphore_signal(barrier, 1, device_id={axis: me - o}, device_id_type=mesh_id)
-
-        @pl.when(me + o < count)
-        def _():
-            pl.semaphore_signal(barrier, 1, device_id={axis: me + o}, device_id_type=mesh_id)
-
-        expected = expected + (me >= o).astype(jnp.int32) + (me + o < count).astype(jnp.int32)
-    pl.semaphore_wait(barrier, expected)
+    for k in range(1, count):
+        pl.semaphore_signal(
+            barrier, 1, device_id={axis: lax.rem(me + k, count)}, device_id_type=mesh_id
+        )
+    pl.semaphore_wait(barrier, count - 1)
+    block = rows_ref.shape[1]
+    row_copies = []
+    for k in range(1, count):
+        copy = pltpu.make_async_remote_copy(
+            src_ref=rows_ref,
+            dst_ref=all_rows.at[:, pl.ds(me * block, block)],
+            send_sem=row_sems.at[0, k],
+            recv_sem=row_sems.at[1, k],
+            device_id={axis: lax.rem(me + k, count)},
+            device_id_type=mesh_id,
+        )
+        copy.start()
+        row_copies.append(copy)
+    own = pltpu.make_async_copy(rows_ref, all_rows.at[:, pl.ds(me * block, block)], row_sems.at[0, 0])
+    own.start()
     slot = 0
     for r, d in enumerate(distances):
         source = pair_ref if r == 0 else held.at[r - 1]
@@ -144,9 +153,12 @@
         shift.wait_send()
 
     out_ref[...] = land[slot, 1]
-
-
-def relay(pair, axis, collective_id, radix=4):
+    own.wait()
+    for copy in row_copies:
+        copy.wait()
+
+
+def relay(pair, rows, axis, collective_id, radix=4):
     count = lax.axis_size(axis)
     rounds = 1
     while radix**rounds < count:
@@ -154,15 +166,21 @@
     slots = rounds * (radix - 1) + 1
     return pl.pallas_call(
         functools.partial(relay_kernel, axis, count, radix),
-        out_shape=jax.ShapeDtypeStruct(pair.shape[1:], pair.dtype),
+        out_shape=(
+            jax.ShapeDtypeStruct(pair.shape[1:], pair.dtype),
+            jax.ShapeDtypeStruct((rows.shape[0], count * rows.shape[1]) + rows.shape[2:], rows.dtype),
+        ),
+        in_specs=[pl.BlockSpec(memory_space=pltpu.VMEM), pl.BlockSpec(memory_space=pl.ANY)],
+        out_specs=(pl.BlockSpec(memory_space=pltpu.VMEM), pl.BlockSpec(memory_space=pl.ANY)),
         scratch_shapes=[
             pltpu.VMEM((rounds,) + pair.shape, pair.dtype),
             pltpu.VMEM((slots,) + pair.shape, pair.dtype),
             pltpu.SemaphoreType.DMA((slots,)),
             pltpu.SemaphoreType.DMA((slots,)),
+            pltpu.SemaphoreType.DMA((2, count)),
         ],
         compiler_params=pltpu.CompilerParams(collective_id=collective_id, has_side_effects=True),
-    )(pair)
+    )(pair, rows)
 
 
 def reduce_kernel(cols_ref, parts_ref, cols_out, rate_out, cols_land, parts_land, chunk, chunk_land, sems):
@@ -287,7 +305,12 @@
     pair = jnp.stack(
         [jnp.where(is_last, 0.0, shrink), jnp.where(is_last, shrink * end_grad + seed, seed)]
     )
-    entering = jnp.where(is_last, end_grad, relay(pair, "ctx", 4))
+    slot_total = hidden_saved.shape[1]
+    capacity = slot_total // (lax.axis_size("ctx") * lax.axis_size("exp"))
+    buffer = slot_buffer(moe_grad, route, gate_prob, capacity)
+    received_rows = lax.all_to_all(buffer, "exp", split_axis=0, concat_axis=1, tiled=True)
+    relayed, all_rows = relay(pair, received_rows, "ctx", 4)
+    entering = jnp.where(is_last, end_grad, relayed)
     adjoint = adjoint_scan(decays, sources, entering)
     input_grad = (
         steps * jnp.sum(bmats[:, :, None] * adjoint, axis=1) + skip_gain[None] * grads
@@ -304,11 +327,6 @@
     col_sums = jnp.sum(col_parts, axis=0)
     in_proj_grad, out_proj_grad = col_sums[0], col_sums[1]
     decay_grad = rate_chunks.reshape(rate_local.shape)
-    slot_total = hidden_saved.shape[1]
-    capacity = slot_total // (lax.axis_size("ctx") * lax.axis_size("exp"))
-    buffer = slot_buffer(moe_grad, route, gate_prob, capacity)
-    received_rows = lax.all_to_all(buffer, "exp", split_axis=0, concat_axis=1, tiled=True)
-    all_rows = lax.all_gather(received_rows, "ctx", axis=1, tiled=True)
     weight_total = jnp.einsum(
         "lrf,lrd->lfd", hidden_saved, all_rows, preferred_element_type=jnp.float32
     )

time: 140 us -> 481 us (3.44)
  Pallas kernels: 73.4 us -> 432 us
  blocking collectives: 14.8 us -> 0 us
  between operations: 14.2 us -> 0.83 us
  starting transfers between devices: 0.04 us -> 7.58 us
    pallas_call x1, Pallas kernels: 44.7 us -> 401 us  [relay(): pl.pallas_call(functools.partial(relay_kernel, axis, count, radix), out_s...]
    all_to_all x1 -> x0, blocking collectives: 14.8 us -> none  [body(): lax.all_to_all(buffer, 'exp', split_axis=0, concat_axis=1, tiled=True)]
    all_to_all x0 -> x1, starting transfers between devices: none -> 7.58 us  [body(): lax.all_to_all(buffer, 'exp', split_axis=0, concat_axis=1, tiled=True)]
  transfers between devices with their start and end apart: 1 -> 1, of which waited for: 0 -> 0; matrix products, arithmetic and copies ran while one was open for 16% -> 2% of each run, Pallas kernels for 53% -> 1%
where the time goes in v7:
time: 481 us; the launch traced here: 480 us
  Pallas kernels  432 us (90%)
  other arithmetic  16.5 us (3%)
  matrix products  13.8 us (3%)
  local copies, waits for them, and re-layouts  8.9 us (2%)
  starting transfers between devices  7.58 us (2%)
    pallas_call x1, Pallas kernels, relay(): pl.pallas_call(functools.partial(relay_kernel, axis, count, radix), out_s...  401 us
    pallas_call x1, Pallas kernels, reduce_partials(): pl.pallas_call(reduce_kernel, out_shape=(jax.ShapeDtypeStruct((n_e,) + co...  22.4 us
  transfers between devices with their start and end apart: 1, of which 0 were waited for; matrix products, arithmetic and copies ran while one was open for 2% of the time, Pallas kernels for 1%

profile of v7, /device:TPU:1, one launch (start us, length us, event | category | flops | bytes accessed | tf_op | source)
XLA Modules:
  0.0 480.0 jit_solution(1670429821656010277)
XLA Ops:
  0.6 0.0 copy-start
  0.6 0.0 copy-start.9
  0.7 0.0 copy-start.10
  0.7 0.0 copy-start.2
  0.7 0.0 copy-start.3
  0.7 0.0 copy-start.4
  0.7 0.9 copy.31
  1.6 0.1 reshape.68
  1.7 0.8 copy.32
  2.4 0.1 mul.161
  2.5 0.1 fusion.26
  2.6 0.2 select_reduce_fusion
  2.8 0.9 mul.163
  3.7 0.2 mul.164
  3.9 0.3 convolution_convert_fusion
  4.3 0.0 copy-start.5
  4.3 0.9 reshape.69
  5.2 7.6 %all-to-all-start = ((bf16[16,2,4096]{2,1,0:T(2,128)(2,1)}), bf16[16,2,4096]{2,1,0:T(2,128)(2,1)S(1)}, u32[]{:S(2)}, u32[]{:S(2)}) async-start(bf16[16,2,4096]{2,1,0:T(2,128)(2,1)} %reshape.69), calls=%async_computation | async-start | bytes 524288 | tf_op jit(solution)/shard_map/all_to_all | solution.py:311
  12.8 0.0 copy-done.9
  12.8 0.1 copy.29
  12.9 0.0 copy-done.10
  12.9 0.1 copy.30
  13.0 0.0 copy-done.2
  13.0 0.0 copy-done.3
  13.0 0.0 copy-done.4
  13.1 1.7 broadcast_multiply_fusion.1.source_ref
  14.8 0.0 copy-done.5
  14.8 2.5 multiply_exponential_fusion
  17.3 4.8 %shard_map.189 = (f32[128,16,256]{2,1,0:T(8,128)}, f32[16,256]{1,0:T(8,128)}) custom-call(f32[128,16,256]{2,1,0:T(8,128)} %get-tuple-element.30.decay_ref, f32[128,16,256]{2,1,0:T(8,128)} %get-tuple-element.31.drive_ref, f32[128,16,256]{2,1,0:T(8,128)} %broadcast_multiply_fusion.1.source_ref, f32[16,256]{1,0:T(8,128)} %bitcast.46), custom_call_target="tpu_custom_call" | custom-call | flops 2097152 | bytes 8388608 | tf_op jit(solution)/shard_map/pallas_call | solution.py:31
  22.1 0.0 copy-start.1
  22.1 2.1 multiply_reduce_fusion.1
  24.3 0.1 copy-done.1
  24.4 0.0 copy-start.7
  24.4 0.0 copy-start.8
  24.4 1.5 slice.9
  25.9 0.0 copy-done.7
  25.9 0.0 copy-done.8
  26.0 0.6 pad_maximum_fusion.1.pair_ref
  26.6 0.0 all-to-all-done
  26.6 0.8 all_to_all.10.rows_ref
  27.4 401.3 %shard_map.190 = (f32[16,256]{1,0:T(8,128)}, bf16[1,1024,4096]{2,1,0:T(8,128)(2,1)}) custom-call(f32[2,16,256]{2,1,0:T(8,128)} %pad_maximum_fusion.1.pair_ref, bf16[1,32,4096]{2,1,0:T(8,128)(2,1)} %all_to_all.10.rows_ref), custom_call_target="tpu_custom_call" | custom-call | tf_op jit(solution)/shard_map/pallas_call | solution.py:167
  428.7 1.3 broadcast_select_fusion.entering_ref
  430.0 0.0 copy-start.6
  430.0 3.9 shard_map.191
  434.0 0.0 copy-done.6
  434.0 4.1 multiply_reduce_fusion
  438.1 0.6 reshape.70.parts_ref
  438.7 0.6 pad_maximum_fusion.2.cols_ref
  439.4 22.4 %shard_map.192 = (f32[16,2,16,128]{3,2,1,0:T(8,128)}, f32[32,1,128]{2,1,0:T(1,128)}) custom-call(f32[2,16,128]{2,1,0:T(8,128)} %pad_maximum_fusion.2.cols_ref, f32[32,1,128]{2,1,0:T(1,128)} %reshape.70.parts_ref), custom_call_target="tpu_custom_call" | custom-call | tf_op jit(solution)/shard_map/pallas_call | solution.py:235
  461.7 1.0 reduce_sum.79
  462.7 0.6 slice_bitcast_fusion
  463.3 0.5 broadcast.29
  463.8 1.4 reduce.3
  465.2 0.6 reshape.71
  465.8 0.0 copy-done
  465.8 0.0 copy-start.12
  465.8 6.8 %fusion.16 = bf16[1,1024,224]{1,2,0:T(8,128)(2,1)} fusion(bf16[1,224,4096]{2,1,0:T(8,128)(2,1)S(1)} %copy-done, bf16[1,1024,4096]{2,1,0:T(8,128)(2,1)} %get-tuple-element.18), kind=kOutput, calls=%fused_computation.16 | convolution fusion | flops 1879277568 | bytes 10682368 | tf_op jit(solution)/shard_map/lrd,lfd->lrf/dot_general | solution.py:333
  472.7 0.0 copy-done.12
  472.7 0.0 copy-start.11
  472.7 6.7 %fusion.7 = bf16[1,224,4096]{2,1,0:T(8,128)(2,1)} fusion(bf16[1,1024,4096]{2,1,0:T(8,128)(2,1)} %get-tuple-element.18, bf16[1,1024,224]{1,2,0:T(8,128)(2,1)S(1)} %copy-done.12), kind=kOutput, calls=%fused_computation.5 | convolution fusion | flops 1879965696 | bytes 10682368 | tf_op jit(solution)/shard_map/lrf,lrd->lfd/dot_general | solution.py:330
  479.4 0.0 copy-done.11
  479.4 0.7 fusion.23
  (8 shorter events, 0.2 us)
Async XLA Ops:
  0.6 465.2 %copy-start = (bf16[1,224,4096]{2,1,0:T(8,128)(2,1)S(1)}, bf16[1,224,4096]{2,1,0:T(8,128)(2,1)}, u32[]{:S(2)}) copy-start(bf16[1,224,4096]{2,1,0:T(8,128)(2,1)} %param.26) | copy-start | bytes 5505028
  0.6 12.1 %copy-start.9 = (f32[16,128]{1,0:T(8,128)S(1)}, f32[16,128]{1,0:T(8,128)}, u32[]{:S(2)}) copy-start(f32[16,128]{1,0:T(8,128)} %param.17) | copy-start | bytes 24580
  0.7 12.2 %copy-start.10 = (f32[16,128]{1,0:T(8,128)S(1)}, f32[16,128]{1,0:T(8,128)}, u32[]{:S(2)}) copy-start(f32[16,128]{1,0:T(8,128)} %param.18) | copy-start | bytes 24580
  0.7 12.3 %copy-start.2 = (bf16[128,256]{1,0:T(8,128)(2,1)S(1)}, bf16[128,256]{1,0:T(8,128)(2,1)}, u32[]{:S(2)}) copy-start(bf16[128,256]{1,0:T(8,128)(2,1)} %param.22) | copy-start | bytes 196612
  0.7 12.3 %copy-start.3 = (bf16[128,256]{1,0:T(8,128)(2,1)S(1)}, bf16[128,256]{1,0:T(8,128)(2,1)}, u32[]{:S(2)}) copy-start(bf16[128,256]{1,0:T(8,128)(2,1)} %param.14) | copy-start | bytes 196612
  0.7 12.3 %copy-start.4 = (bf16[128,256]{1,0:T(8,128)(2,1)S(1)}, bf16[128,256]{1,0:T(8,128)(2,1)}, u32[]{:S(2)}) copy-start(bf16[128,256]{1,0:T(8,128)(2,1)} %param.15) | copy-start | bytes 196612
  4.3 10.6 %copy-start.5 = (f32[16,256]{1,0:T(8,128)S(1)}, f32[16,256]{1,0:T(8,128)}, u32[]{:S(2)}) copy-start(f32[16,256]{1,0:T(8,128)} %param.16) | copy-start | bytes 49156
  5.2 21.4 %all-to-all-start = ((bf16[16,2,4096]{2,1,0:T(2,128)(2,1)}), bf16[16,2,4096]{2,1,0:T(2,128)(2,1)S(1)}, u32[]{:S(2)}, u32[]{:S(2)}) async-start(bf16[16,2,4096]{2,1,0:T(2,128)(2,1)} %reshape.69), calls=%async_computation | async-start | bytes 524288 | tf_op jit(solution)/shard_map/all_to_all | solution.py:311
  22.1 2.2 copy-start.1
  24.4 1.6 copy-start.7
  24.4 1.6 copy-start.8
  430.0 3.9 copy-start.6
  465.8 6.8 %copy-start.12 = (bf16[1,1024,224]{1,2,0:T(8,128)(2,1)S(1)}, bf16[1,1024,224]{1,2,0:T(8,128)(2,1)}, u32[]{:S(2)}) copy-start(bf16[1,1024,224]{1,2,0:T(8,128)(2,1)} %param.27) | copy-start | bytes 1376260
  472.7 6.7 %copy-start.11 = (f32[256]{0:T(256)S(1)}, f32[256]{0:T(256)}, u32[]{:S(2)}) copy-start(f32[256]{0:T(256)} %param.19) | copy-start | bytes 3076

commit v8 on v5

--- a/solution.py
+++ b/solution.py
@@ -276,14 +276,26 @@
     capacity = slot_total // (lax.axis_size("ctx") * lax.axis_size("exp"))
     buffer = slot_buffer(moe_grad, route, gate_prob, capacity)
     received_rows = lax.all_to_all(buffer, "exp", split_axis=0, concat_axis=1, tiled=True)
-    all_rows = lax.all_gather(received_rows, "ctx", axis=1, tiled=True)
-    weight_total = jnp.einsum(
-        "lrf,lrd->lfd", hidden_saved, all_rows, preferred_element_type=jnp.float32
-    )
-    hidden_grad = jnp.einsum(
-        "lrd,lfd->lrf", all_rows, w_down, preferred_element_type=jnp.float32
+    half = received_rows.shape[2] // 2
+    row_halves = [
+        lax.all_gather(received_rows[:, :, :half], "ctx", axis=1, tiled=True),
+        lax.all_gather(received_rows[:, :, half:], "ctx", axis=1, tiled=True),
+    ]
+    down_grad = jnp.concatenate(
+        [
+            jnp.einsum("lrf,lrd->lfd", hidden_saved, rows, preferred_element_type=jnp.float32)
+            for rows in row_halves
+        ],
+        axis=2,
     ).astype(jnp.bfloat16)
-    down_grad = weight_total.astype(jnp.bfloat16)
+    hidden_grad = (
+        jnp.einsum(
+            "lrd,lfd->lrf", row_halves[0], w_down[:, :, :half], preferred_element_type=jnp.float32
+        )
+        + jnp.einsum(
+            "lrd,lfd->lrf", row_halves[1], w_down[:, :, half:], preferred_element_type=jnp.float32
+        )
+    ).astype(jnp.bfloat16)
     return (input_grad, step_grad, in_proj_grad, out_proj_grad, decay_grad, down_grad, hidden_grad)
 
 

time: 138 us -> 197 us (1.43)
  waiting for transfers between devices: 0.02 us -> 60.9 us
  Pallas kernels: 71.9 us -> 69.5 us
    all_gather x1 -> x2, waiting for transfers between devices: 0.01 us -> 60.2 us  [the longest x1 60.2 us: body(): lax.all_gather(received_rows[:, :, :half], 'ctx', axis=1, tiled=True)]
    unnamed x28 -> x32, local copies, waits for them, and re-layouts: 1.69 us -> 3.78 us
    dot_general x2 -> x4, matrix products: 10.2 us -> 10.4 us  [the longest x2 6.76 us: body(): jnp.einsum('lrf,lrd->lfd', hidden_saved, rows, preferred_element_type=jnp...]
  transfers between devices with their start and end apart: 1 -> 2, of which waited for: 0 -> 1; matrix products, arithmetic and copies ran while one was open for 16% -> 11% of each run, Pallas kernels for 52% -> 35%
where the time goes in v8:
time: 197 us
  Pallas kernels  69.5 us (35%)
  waiting for transfers between devices  60.9 us (31%)
  other arithmetic  15.8 us (8%)
  blocking collectives  14.8 us (8%)
  between operations  14.3 us (7%)
  matrix products  10.7 us (5%)
  local copies, waits for them, and re-layouts  10.6 us (5%)
    all_gather x1, waiting for transfers between devices, body(): lax.all_gather(received_rows[:, :, :half], 'ctx', axis=1, tiled=True)  60.2 us
    pallas_call x1, Pallas kernels, relay(): pl.pallas_call(functools.partial(relay_kernel, axis, count), out_shape=ja...  42 us
    pallas_call x1, Pallas kernels, reduce_partials(): pl.pallas_call(reduce_kernel, out_shape=(jax.ShapeDtypeStruct((n_e,) + co...  18.7 us
    all_to_all x1, blocking collectives, body(): lax.all_to_all(buffer, 'exp', split_axis=0, concat_axis=1, tiled=True)  14.8 us
    dot_general x2, matrix products, body(): jnp.einsum('lrf,lrd->lfd', hidden_saved, rows, preferred_element_type=jnp...  6.76 us
    pallas_call x1, Pallas kernels, local_scans(): pl.pallas_call(local_scans_kernel, out_shape=(jax.ShapeDtypeStruct(decays...  4.85 us
    pallas_call x1, Pallas kernels, adjoint_scan(): pl.pallas_call(adjoint_scan_kernel, out_shape=jax.ShapeDtypeStruct(decays...  3.98 us
  transfers between devices with their start and end apart: 2, of which 1 were waited for; matrix products, arithmetic and copies ran while one was open for 11% of the time, Pallas kernels for 35%

profile of v8, /device:TPU:1, one launch (start us, length us, event | category | flops | bytes accessed | tf_op | source)
XLA Modules:
  0.0 196.6 jit_solution(7360327598785657276)
XLA Ops:
  7.2 0.0 copy-start
  7.2 0.0 copy-start.9
  7.2 0.0 copy-start.10
  7.2 0.0 copy-start.2
  7.2 0.0 copy-start.3
  7.2 0.0 all-gather.5.cloned.1.call-start
  7.3 0.8 copy.33
  8.1 0.1 reshape.118
  8.2 0.8 copy.34
  8.9 0.1 mul.175
  9.0 0.1 fusion.39
  9.1 0.2 select_reduce_fusion
  9.3 0.0 copy-start.4
  9.3 1.0 mul.177
  10.3 0.2 mul.178
  10.5 0.3 convolution_convert_fusion
  10.8 0.2 reshape.119
  11.0 14.8 %all_to_all.12 = bf16[16,2,4096]{2,1,0:T(2,128)(2,1)S(1)} all-to-all(bf16[16,2,4096]{2,1,0:T(2,128)(2,1)S(1)} %reshape.119), channel_id=1, replica_groups=mesh['ctx'=32,'exp'=16] {'exp'}, dimensions={0} | all-to-all | bytes 524288 | tf_op jit(solution)/shard_map/all_to_all | solution.py:278
  25.7 0.1 all_to_all.10
  25.9 0.0 copy-start.5
  25.9 0.7 fusion.41
  26.6 0.0 all-gather.5.cloned.1.call-update
  26.6 0.0 all-gather.3.cloned.1.call-start
  26.7 0.7 all-gather.3.cloned.1.call-update
  27.4 0.0 copy-done.9
  27.4 0.1 copy.29
  27.5 0.0 copy-done.10
  27.5 0.1 copy.30
  27.6 0.0 copy-done.2
  27.6 0.0 copy-done.3
  27.6 0.0 copy-done.4
  27.7 1.7 broadcast_multiply_fusion.1.source_ref
  29.4 2.5 %multiply_exponential_fusion = (f32[128,16,256]{2,1,0:T(8,128)}, f32[128,16,256]{2,1,0:T(8,128)}) fusion(f32[16,256]{1,0:T(8,128)S(1)} %copy-done.5, f32[128,256]{1,0:T(8,128)S(1)} %get-tuple-element.23, f32[128,16]{1,0:T(8,128)S(1)} %copy.29, f32[128,256]{1,0:T(8,128)S(1)} %get-tuple-element.22), kind=kLoop, calls=%fused_computation.19 | loop fusion | flops 1048576 | bytes 4481024 | tf_op jit(solution)/shard_map/exp | solution.py:245
  31.9 4.8 %shard_map.189 = (f32[128,16,256]{2,1,0:T(8,128)}, f32[16,256]{1,0:T(8,128)}) custom-call(f32[128,16,256]{2,1,0:T(8,128)} %get-tuple-element.28.decay_ref, f32[128,16,256]{2,1,0:T(8,128)} %get-tuple-element.29.drive_ref, f32[128,16,256]{2,1,0:T(8,128)} %broadcast_multiply_fusion.1.source_ref, f32[16,256]{1,0:T(8,128)} %bitcast.62), custom_call_target="tpu_custom_call" | custom-call | flops 2097152 | bytes 8388608 | tf_op jit(solution)/shard_map/pallas_call | solution.py:31
  36.8 1.9 slice.21
  38.7 0.3 copy-done.1
  39.0 0.4 multiply_reduce_fusion.1
  39.4 0.1 copy.32
  39.5 0.3 copy-done.7
  39.7 0.0 copy-done.8
  39.8 0.6 pad_maximum_fusion.2.pair_ref
  40.4 42.0 %shard_map.190 = f32[16,256]{1,0:T(8,128)} custom-call(f32[2,16,256]{2,1,0:T(8,128)} %pad_maximum_fusion.2.pair_ref), custom_call_target="tpu_custom_call" | custom-call | tf_op jit(solution)/shard_map/pallas_call | solution.py:123
  82.3 1.3 broadcast_select_fusion.entering_ref
  83.7 4.0 %shard_map.191 = f32[128,16,256]{2,1,0:T(8,128)} custom-call(f32[128,16,256]{2,1,0:T(8,128)} %get-tuple-element.28.decay_ref, f32[128,16,256]{2,1,0:T(8,128)} %broadcast_multiply_fusion.1.source_ref, f32[16,256]{1,0:T(8,128)} %broadcast_select_fusion.entering_ref), custom_call_target="tpu_custom_call" | custom-call | flops 1048576 | bytes 6291456 | tf_op jit(solution)/shard_map/pallas_call | solution.py:56
  87.7 3.8 %multiply_reduce_fusion = (f32[16,256]{1,0:T(8,128)S(1)}, bf16[128,256]{1,0:T(8,128)(2,1)}, f32[128,256]{1,0:T(8,128)S(1)}, f32[128,16]{1,0:T(8,128)S(1)}) fusion(f32[128,16,256]{2,1,0:T(8,128)} %shard_map.191, f32[127,16,256]{2,1,0:T(8,128)S(1)} %slice.21, f32[1,16,256]{2,1,0:T(8,128)S(1)} %copy-done.6, f32[16,256]{1,0:T(8,128)S(1)} %copy-done.5, ...), kind=kLoop, calls=%fused_computation.14 | loop fusion | flops 8316928 | bytes 4833280 | tf_op jit(solution)/shard_map/reduce_sum | solution.py:268
  91.4 0.6 reshape.116.parts_ref
  92.1 0.6 pad_maximum_fusion.3.cols_ref
  92.7 18.7 %shard_map.192 = (f32[16,2,16,128]{3,2,1,0:T(8,128)}, f32[32,1,128]{2,1,0:T(1,128)}) custom-call(f32[2,16,128]{2,1,0:T(8,128)} %pad_maximum_fusion.3.cols_ref, f32[32,1,128]{2,1,0:T(1,128)} %reshape.116.parts_ref), custom_call_target="tpu_custom_call" | custom-call | tf_op jit(solution)/shard_map/pallas_call | solution.py:185
  111.5 0.5 broadcast.29
  112.0 1.4 reduce.3
  113.4 0.6 reshape.117
  114.0 1.0 reduce_sum.78
  115.0 0.6 slice_bitcast_fusion
  115.6 0.7 fusion.36
  116.3 3.3 %fusion.14 = bf16[1,224,2048]{2,1,0:T(8,128)(2,1)S(1)} fusion(bf16[1,1024,2048]{2,1,0:T(8,128)(2,1)} %all-gather.5.cloned.1.call-done, bf16[1,1024,224]{1,2,0:T(8,128)(2,1)S(1)} %copy-done), kind=kOutput, calls=%fused_computation.11 | convolution fusion | flops 939982848 | bytes 5570560 | tf_op jit(solution)/shard_map/lrf,lrd->lfd/dot_general | solution.py:286
  119.6 60.2 %all-gather.3.cloned.1.call-done = bf16[1,1024,2048]{2,1,0:T(8,128)(2,1)} async-done(((bf16[1,32,2048]{2,1,0:T(8,128)(2,1)}), bf16[1,1024,2048]{2,1,0:T(8,128)(2,1)}) %all-gather.3.cloned.1.call-update) | async-done | bytes 4194320 | tf_op jit(solution)/shard_map/all_gather | solution.py:281
  179.8 3.5 %fusion.17 = bf16[1,224,2048]{2,1,0:T(8,128)(2,1)S(1)} fusion(bf16[1,1024,2048]{2,1,0:T(8,128)(2,1)} %all-gather.3.cloned.1.call-done, bf16[1,1024,224]{1,2,0:T(8,128)(2,1)S(1)} %copy-done), kind=kOutput, calls=%fused_computation.12 | convolution fusion | flops 939982848 | bytes 5570560 | tf_op jit(solution)/shard_map/lrf,lrd->lfd/dot_general | solution.py:286
  183.2 0.0 copy-start.14
  183.2 1.4 pad_maximum_fusion.1
  184.6 0.0 copy-done.12
  184.6 0.8 copy-done.14
  185.4 1.4 fusion
  186.8 0.8 copy-done.13
  187.6 2.2 %fusion.26 = bf16[1,1024,224]{1,2,0:T(8,128)(2,1)} fusion(f32[1024,224]{0,1:T(8,128)S(1)} %fusion, bf16[1,1024,2048]{2,1,0:T(8,128)(2,1)S(1)} %copy-done.13, bf16[1,224,4096]{2,1,0:T(8,128)(2,1)S(1)} %copy-done.14), kind=kOutput, calls=%fused_computation.23 | convolution fusion | flops 939982848 | bytes 6488064 | tf_op jit(solution)/shard_map/lrd,lfd->lrf/dot_general | solution.py:292
  (19 shorter events, 0.2 us)
Async XLA Ops:
  7.2 109.1 %copy-start = (bf16[1,1024,224]{1,2,0:T(8,128)(2,1)S(1)}, bf16[1,1024,224]{1,2,0:T(8,128)(2,1)}, u32[]{:S(2)}) copy-start(bf16[1,1024,224]{1,2,0:T(8,128)(2,1)} %param.27) | copy-start | bytes 1376260
  7.2 20.2 %copy-start.9 = (f32[16,128]{1,0:T(8,128)S(1)}, f32[16,128]{1,0:T(8,128)}, u32[]{:S(2)}) copy-start(f32[16,128]{1,0:T(8,128)} %param.17) | copy-start | bytes 24580
  7.2 20.3 %copy-start.10 = (f32[16,128]{1,0:T(8,128)S(1)}, f32[16,128]{1,0:T(8,128)}, u32[]{:S(2)}) copy-start(f32[16,128]{1,0:T(8,128)} %param.18) | copy-start | bytes 24580
  7.2 20.4 %copy-start.2 = (bf16[128,256]{1,0:T(8,128)(2,1)S(1)}, bf16[128,256]{1,0:T(8,128)(2,1)}, u32[]{:S(2)}) copy-start(bf16[128,256]{1,0:T(8,128)(2,1)} %param.22) | copy-start | bytes 196612
  7.2 20.4 %copy-start.3 = (bf16[128,256]{1,0:T(8,128)(2,1)S(1)}, bf16[128,256]{1,0:T(8,128)(2,1)}, u32[]{:S(2)}) copy-start(bf16[128,256]{1,0:T(8,128)(2,1)} %param.14) | copy-start | bytes 196612
  7.2 109.0 %all-gather.5.cloned.1.call-start = ((), (), s32[]{:S(2)}) async-start(), calls=%async_computation.2 | async-start | bytes 4325376 | tf_op jit(solution)/shard_map/all_gather | solution.py:282
  9.3 18.3 %copy-start.4 = (bf16[128,256]{1,0:T(8,128)(2,1)S(1)}, bf16[128,256]{1,0:T(8,128)(2,1)}, u32[]{:S(2)}) copy-start(bf16[128,256]{1,0:T(8,128)(2,1)} %param.15) | copy-start | bytes 196612
  25.9 3.6 %copy-start.5 = (f32[16,256]{1,0:T(8,128)S(1)}, f32[16,256]{1,0:T(8,128)}, u32[]{:S(2)}) copy-start(f32[16,256]{1,0:T(8,128)} %param.16) | copy-start | bytes 49156
  26.6 153.2 %all-gather.3.cloned.1.call-start = ((), (), s32[]{:S(2)}) async-start(), calls=%async_computation.1 | async-start | bytes 4325376 | tf_op jit(solution)/shard_map/all_gather | solution.py:281
  36.8 2.2 %copy-start.1 = (f32[128,16,256]{2,1,0:T(8,128)S(1)}, f32[128,16,256]{2,1,0:T(8,128)}, u32[]{:S(2)}) copy-start(f32[128,16,256]{2,1,0:T(8,128)} %get-tuple-element.12) | copy-start | bytes 6291460
  39.0 0.7 copy-start.7
  39.0 0.7 copy-start.8
  83.7 4.0 %copy-start.6 = (f32[1,16,256]{2,1,0:T(8,128)S(1)}, f32[1,16,256]{2,1,0:T(8,128)}, u32[]{:S(2)}) copy-start(f32[1,16,256]{2,1,0:T(8,128)} %param.20) | copy-start | bytes 49156
  87.7 28.0 %copy-start.11 = (f32[256]{0:T(256)S(1)}, f32[256]{0:T(256)}, u32[]{:S(2)}) copy-start(f32[256]{0:T(256)} %param.19) | copy-start | bytes 3076
  179.8 4.8 %copy-start.12 = (bf16[1,1024,2048]{2,1,0:T(8,128)(2,1)S(1)}, bf16[1,1024,2048]{2,1,0:T(8,128)(2,1)}, u32[]{:S(2)}) copy-start(bf16[1,1024,2048]{2,1,0:T(8,128)(2,1)} %all-gather.5.cloned.1.call-done) | copy-start | bytes 12582916
  183.2 2.2 %copy-start.14 = (bf16[1,224,4096]{2,1,0:T(8,128)(2,1)S(1)}, bf16[1,224,4096]{2,1,0:T(8,128)(2,1)}, u32[]{:S(2)}) copy-start(bf16[1,224,4096]{2,1,0:T(8,128)(2,1)} %param.26) | copy-start | bytes 5505028
  185.4 2.2 %copy-start.13 = (bf16[1,1024,2048]{2,1,0:T(8,128)(2,1)S(1)}, bf16[1,1024,2048]{2,1,0:T(8,128)(2,1)}, u32[]{:S(2)}) copy-start(bf16[1,1024,2048]{2,1,0:T(8,128)(2,1)} %all-gather.3.cloned.1.call-done) | copy-start | bytes 12582916
Sparse Core Ops, SparseCore 0:
  26.7 80.6 all-gather.4
  110.2 69.5 all-gather.2

commit v9 on v5

--- a/solution.py
+++ b/solution.py
@@ -10,10 +10,11 @@
 EXPERTS = 16
 
 
-def local_scans_kernel(decay_ref, drive_ref, source_ref, first_ref, states_ref, seed_ref):
+def local_scans_kernel(decay_ref, drive_ref, source_ref, first_ref, states_ref, before_ref, seed_ref):
     count = decay_ref.shape[0]
 
     def forward(t, state):
+        before_ref[t] = state
         state = decay_ref[t] * state + drive_ref[t]
         states_ref[t] = state
         return state
@@ -32,10 +33,11 @@
         local_scans_kernel,
         out_shape=(
             jax.ShapeDtypeStruct(decays.shape, jnp.float32),
+            jax.ShapeDtypeStruct(decays.shape, jnp.float32),
             jax.ShapeDtypeStruct(first_state.shape, jnp.float32),
         ),
         cost_estimate=pl.CostEstimate(
-            flops=4 * decays.size, bytes_accessed=16 * decays.size, transcendentals=0
+            flops=4 * decays.size, bytes_accessed=20 * decays.size, transcendentals=0
         ),
     )(decays, driving, sources, first_state)
 
@@ -245,8 +247,7 @@
     decays = jnp.exp(-steps[:, None, :] * decay_rate[None])
     driving = (steps * inputs)[:, None, :] * bmats[:, :, None]
     sources = cmats[:, :, None] * grads[:, None, :]
-    states, seed = local_scans(decays, driving, sources, first_state)
-    before = jnp.concatenate([first_state[None], states[:-1]], axis=0)
+    states, before, seed = local_scans(decays, driving, sources, first_state)
     out_cols = jnp.sum(states * grads[:, None, :], axis=2)
     shrink = jnp.exp(-decay_rate * jnp.sum(steps, axis=0)[None])
     position = lax.axis_index("ctx")

time: 138 us -> 136 us (0.986)
  local copies, waits for them, and re-layouts: 9.76 us -> 6.61 us
    slice x1 -> x0, local copies, waits for them, and re-layouts: 3.15 us -> none  [body(): before = jnp.concatenate([first_state[None], states[:-1]], axis=0)]
  transfers between devices with their start and end apart: 1 -> 1, of which waited for: 0 -> 0; matrix products, arithmetic and copies ran while one was open for 16% -> 14% of each run, Pallas kernels for 52% -> 53%
where the time goes in v9:
time: 136 us
  Pallas kernels  72.3 us (53%)
  other arithmetic  17.2 us (13%)
  blocking collectives  14.8 us (11%)
  between operations  14.2 us (10%)
  matrix products  10.6 us (8%)
  local copies, waits for them, and re-layouts  6.61 us (5%)
    pallas_call x1, Pallas kernels, relay(): pl.pallas_call(functools.partial(relay_kernel, axis, count), out_shape=ja...  43.6 us
    pallas_call x1, Pallas kernels, reduce_partials(): pl.pallas_call(reduce_kernel, out_shape=(jax.ShapeDtypeStruct((n_e,) + co...  19.2 us
    all_to_all x1, blocking collectives, body(): lax.all_to_all(buffer, 'exp', split_axis=0, concat_axis=1, tiled=True)  14.8 us
    dot_general x1, matrix products, body(): jnp.einsum('lrf,lrd->lfd', hidden_saved, all_rows, preferred_element_type...  6.83 us
    pallas_call x1, Pallas kernels, local_scans(): pl.pallas_call(local_scans_kernel, out_shape=(jax.ShapeDtypeStruct(decays...  5.51 us
    reduce_sum x1, other arithmetic, body(): jnp.sum(adjoint * (-steps[:, None, :] * decays * before), axis=0)  4.13 us
    pallas_call x1, Pallas kernels, adjoint_scan(): pl.pallas_call(adjoint_scan_kernel, out_shape=jax.ShapeDtypeStruct(decays...  3.96 us
    dot_general x1, matrix products, body(): jnp.einsum('lrd,lfd->lrf', all_rows, w_down, preferred_element_type=jnp.f...  3.41 us
  transfers between devices with their start and end apart: 1, of which 0 were waited for; matrix products, arithmetic and copies ran while one was open for 14% of the time, Pallas kernels for 53%

profile of v9, /device:TPU:1, one launch (start us, length us, event | category | flops | bytes accessed | tf_op | source)
XLA Modules:
  0.0 135.7 jit_solution(15060968138948515723)
XLA Ops:
  7.2 0.0 copy-start
  7.2 0.0 copy-start.6
  7.2 0.0 copy-start.1
  7.2 0.0 copy-start.7
  7.2 0.0 copy-start.2
  7.2 0.0 copy-start.3
  7.2 0.0 all-gather.2.cloned.1.call-start
  7.3 0.9 copy.33
  8.2 0.1 reshape.70
  8.2 0.1 fusion.26
  8.4 0.2 select_reduce_fusion
  8.5 0.9 mul.177
  9.5 0.2 mul.178
  9.7 0.8 copy.34
  10.4 0.1 mul.175
  10.5 0.3 convolution_convert_fusion
  10.9 0.2 reshape.71
  11.0 14.8 %all_to_all.12 = bf16[16,2,4096]{2,1,0:T(2,128)(2,1)S(1)} all-to-all(bf16[16,2,4096]{2,1,0:T(2,128)(2,1)S(1)} %reshape.71), channel_id=1, replica_groups=mesh['ctx'=32,'exp'=16] {'exp'}, dimensions={0} | all-to-all | bytes 524288 | tf_op jit(solution)/shard_map/all_to_all | solution.py:279
  25.8 0.0 copy-start.4
  25.8 0.8 all_to_all.10
  26.6 0.0 all-gather.2.cloned.1.call-update
  26.6 0.0 copy-done.6
  26.6 0.1 copy.29
  26.7 0.0 copy-done.1
  26.8 0.0 copy-done.7
  26.8 0.1 copy.30
  26.9 0.0 copy-done.2
  26.9 0.0 copy-done.3
  27.0 1.7 %broadcast_multiply_fusion.1.source_ref = f32[128,16,256]{2,1,0:T(8,128)} fusion(f32[128,256]{1,0:T(8,128)S(1)} %convert_element_type.45, f32[128,16]{1,0:T(8,128)S(1)} %copy.30), kind=kLoop, calls=%fused_computation.17 | loop fusion | flops 524288 | bytes 2236416 | tf_op jit(solution)/shard_map/mul | solution.py:249
  28.7 0.0 copy-done.4
  28.7 2.6 %multiply_exponential_fusion = (f32[128,16,256]{2,1,0:T(8,128)}, f32[128,16,256]{2,1,0:T(8,128)}) fusion(f32[16,256]{1,0:T(8,128)S(1)} %copy-done.4, f32[128,256]{1,0:T(8,128)S(1)} %get-tuple-element.23, f32[128,16]{1,0:T(8,128)S(1)} %copy.29, f32[128,256]{1,0:T(8,128)S(1)} %get-tuple-element.22), kind=kLoop, calls=%fused_computation.12 | loop fusion | flops 1048576 | bytes 4481024 | tf_op jit(solution)/shard_map/exp | solution.py:247
  31.3 0.0 copy-start.5
  31.3 5.5 %shard_map.189 = (f32[128,16,256]{2,1,0:T(8,128)}, f32[128,16,256]{2,1,0:T(8,128)}, f32[16,256]{1,0:T(8,128)}) custom-call(f32[128,16,256]{2,1,0:T(8,128)} %get-tuple-element.28.decay_ref, f32[128,16,256]{2,1,0:T(8,128)} %get-tuple-element.29.drive_ref, f32[128,16,256]{2,1,0:T(8,128)} %broadcast_multiply_fusion.1.source_ref, f32[16,256]{1,0:T(8,128)} %bitcast.48), custom_call_target="tpu_custom_call" | custom-call | flops 2097152 | bytes 10485760 | tf_op jit(solution)/shard_map/pallas_call | solution.py:32
  36.8 0.0 copy-done.5
  36.8 0.7 select_bitcast_fusion
  37.6 0.6 pad_maximum_fusion.pair_ref
  38.2 43.6 %shard_map.190 = f32[16,256]{1,0:T(8,128)} custom-call(f32[2,16,256]{2,1,0:T(8,128)} %pad_maximum_fusion.pair_ref), custom_call_target="tpu_custom_call" | custom-call | tf_op jit(solution)/shard_map/pallas_call | solution.py:125
  81.8 1.3 broadcast_select_fusion.entering_ref
  83.1 4.0 %shard_map.191 = f32[128,16,256]{2,1,0:T(8,128)} custom-call(f32[128,16,256]{2,1,0:T(8,128)} %get-tuple-element.28.decay_ref, f32[128,16,256]{2,1,0:T(8,128)} %broadcast_multiply_fusion.1.source_ref, f32[16,256]{1,0:T(8,128)} %broadcast_select_fusion.entering_ref), custom_call_target="tpu_custom_call" | custom-call | flops 1048576 | bytes 6291456 | tf_op jit(solution)/shard_map/pallas_call | solution.py:58
  87.1 4.1 %multiply_reduce_fusion = (f32[16,256]{1,0:T(8,128)S(1)}, bf16[128,256]{1,0:T(8,128)(2,1)}, f32[128,256]{1,0:T(8,128)S(1)}, f32[128,16]{1,0:T(8,128)S(1)}) fusion(f32[128,16,256]{2,1,0:T(8,128)} %shard_map.191, f32[128,16,256]{2,1,0:T(8,128)} %get-tuple-element.13, f32[16,256]{1,0:T(8,128)S(1)} %copy-done.4, f32[128,256]{1,0:T(8,128)S(1)} %get-tuple-element.23, ...), kind=kLoop, calls=%fused_computation.7 | loop fusion | flops 7792640 | bytes 4833280 | tf_op jit(solution)/shard_map/reduce_sum | solution.py:269
  91.2 0.0 copy-start.8
  91.2 0.0 copy-start.10
  91.3 2.1 %multiply_reduce_fusion.1 = f32[128,16]{1,0:T(8,128)S(1)} fusion(f32[128,16,256]{2,1,0:T(8,128)} %get-tuple-element.14, f32[128,256]{1,0:T(8,128)S(1)} %convert_element_type.45), kind=kLoop, calls=%fused_computation.8 | loop fusion | flops 1046528 | bytes 2236416 | tf_op jit(solution)/shard_map/reduce_sum | solution.py:251
  93.3 0.1 copy.32
  93.4 0.6 reshape.68.parts_ref
  94.0 0.6 pad_maximum_fusion.1.cols_ref
  94.6 19.2 %shard_map.192 = (f32[16,2,16,128]{3,2,1,0:T(8,128)}, f32[32,1,128]{2,1,0:T(1,128)}) custom-call(f32[2,16,128]{2,1,0:T(8,128)} %pad_maximum_fusion.1.cols_ref, f32[32,1,128]{2,1,0:T(1,128)} %reshape.68.parts_ref), custom_call_target="tpu_custom_call" | custom-call | tf_op jit(solution)/shard_map/pallas_call | solution.py:187
  113.8 0.5 broadcast.29
  114.3 1.4 %reduce.3 = f32[32,128]{1,0:T(8,128)S(1)} reduce(f32[32,1,128]{2,1,0:T(1,128)} %get-tuple-element.16, f32[]{:T(128)} %broadcast.29), dimensions={1}, to_apply=%get-tuple-element.16.reduce_sub_computation.3 | reduce | bytes 32772 | tf_op jit(solution)/shard_map/pallas_call | solution.py:187
  115.8 0.6 reshape.69
  116.4 1.0 reduce_sum.78
  117.3 0.6 slice_bitcast_fusion
  117.9 0.0 copy-done.8
  118.0 0.7 fusion.23
  118.6 0.0 all-gather.2.cloned.1.call-done
  118.6 0.0 copy-done.10
  118.6 0.0 copy-start.9
  118.6 6.8 %fusion.7 = bf16[1,224,4096]{2,1,0:T(8,128)(2,1)} fusion(bf16[1,1024,4096]{2,1,0:T(8,128)(2,1)} %all-gather.2.cloned.1.call-done, bf16[1,1024,224]{1,2,0:T(8,128)(2,1)S(1)} %copy-done.10), kind=kOutput, calls=%fused_computation.5 | convolution fusion | flops 1879965696 | bytes 10682368 | tf_op jit(solution)/shard_map/lrf,lrd->lfd/dot_general | solution.py:281
  125.4 0.0 copy-done
  125.4 0.0 copy-done.9
  125.5 3.4 %fusion.16 = bf16[1,1024,224]{1,2,0:T(8,128)(2,1)} fusion(bf16[1,224,4096]{2,1,0:T(8,128)(2,1)S(1)} %copy-done, bf16[1,1024,4096]{2,1,0:T(8,128)(2,1)S(1)} %copy-done.9), kind=kOutput, calls=%fused_computation.15 | convolution fusion | flops 1879277568 | bytes 10682368 | tf_op jit(solution)/shard_map/lrd,lfd->lrf/dot_general | solution.py:284
  (6 shorter events, 0.2 us)
Async XLA Ops:
  7.2 118.3 %copy-start = (bf16[1,224,4096]{2,1,0:T(8,128)(2,1)S(1)}, bf16[1,224,4096]{2,1,0:T(8,128)(2,1)}, u32[]{:S(2)}) copy-start(bf16[1,224,4096]{2,1,0:T(8,128)(2,1)} %param.26) | copy-start | bytes 5505028
  7.2 19.4 %copy-start.6 = (f32[16,128]{1,0:T(8,128)S(1)}, f32[16,128]{1,0:T(8,128)}, u32[]{:S(2)}) copy-start(f32[16,128]{1,0:T(8,128)} %param.17) | copy-start | bytes 24580
  7.2 19.5 %copy-start.1 = (bf16[128,256]{1,0:T(8,128)(2,1)S(1)}, bf16[128,256]{1,0:T(8,128)(2,1)}, u32[]{:S(2)}) copy-start(bf16[128,256]{1,0:T(8,128)(2,1)} %param.22) | copy-start | bytes 196612
  7.2 19.6 %copy-start.7 = (f32[16,128]{1,0:T(8,128)S(1)}, f32[16,128]{1,0:T(8,128)}, u32[]{:S(2)}) copy-start(f32[16,128]{1,0:T(8,128)} %param.18) | copy-start | bytes 24580
  7.2 19.7 %copy-start.2 = (bf16[128,256]{1,0:T(8,128)(2,1)S(1)}, bf16[128,256]{1,0:T(8,128)(2,1)}, u32[]{:S(2)}) copy-start(bf16[128,256]{1,0:T(8,128)(2,1)} %param.14) | copy-start | bytes 196612
  7.2 19.7 %copy-start.3 = (bf16[128,256]{1,0:T(8,128)(2,1)S(1)}, bf16[128,256]{1,0:T(8,128)(2,1)}, u32[]{:S(2)}) copy-start(bf16[128,256]{1,0:T(8,128)(2,1)} %param.15) | copy-start | bytes 196612
  7.2 111.4 %all-gather.2.cloned.1.call-start = ((), (), s32[]{:S(2)}) async-start(), calls=%async_computation.1 | async-start | bytes 8650752 | tf_op jit(solution)/shard_map/all_gather | solution.py:280
  25.8 2.9 %copy-start.4 = (f32[16,256]{1,0:T(8,128)S(1)}, f32[16,256]{1,0:T(8,128)}, u32[]{:S(2)}) copy-start(f32[16,256]{1,0:T(8,128)} %param.16) | copy-start | bytes 49156
  31.3 5.5 %copy-start.5 = (f32[16,256]{1,0:T(8,128)S(1)}, f32[16,256]{1,0:T(8,128)}, u32[]{:S(2)}) copy-start(f32[16,256]{1,0:T(8,128)} %param.21) | copy-start | bytes 49156
  91.2 26.7 %copy-start.8 = (f32[256]{0:T(256)S(1)}, f32[256]{0:T(256)}, u32[]{:S(2)}) copy-start(f32[256]{0:T(256)} %param.19) | copy-start | bytes 3076
  91.2 27.4 %copy-start.10 = (bf16[1,1024,224]{1,2,0:T(8,128)(2,1)S(1)}, bf16[1,1024,224]{1,2,0:T(8,128)(2,1)}, u32[]{:S(2)}) copy-start(bf16[1,1024,224]{1,2,0:T(8,128)(2,1)} %param.27) | copy-start | bytes 1376260
  118.6 6.8 %copy-start.9 = (bf16[1,1024,4096]{2,1,0:T(8,128)(2,1)S(1)}, bf16[1,1024,4096]{2,1,0:T(8,128)(2,1)}, u32[]{:S(2)}) copy-start(bf16[1,1024,4096]{2,1,0:T(8,128)(2,1)} %all-gather.2.cloned.1.call-done) | copy-start | bytes 25165828
Sparse Core Ops, SparseCore 0:
  26.7 88.3 all-gather.1

commit v10 on v9

--- a/solution.py
+++ b/solution.py
@@ -62,6 +62,55 @@
             flops=2 * decays.size, bytes_accessed=12 * decays.size, transcendentals=0
         ),
     )(decays, sources, entering)
+
+
+def adjoint_full_kernel(
+    decay_ref, source_ref, entering_ref, bmat_ref, inp_ref, step_ref, grad_ref, before_ref,
+    rate_ref, skip_ref, input_out, step_out, in_cols_out, rate_out, adjoint_ref,
+):
+    count = decay_ref.shape[0]
+
+    def backward(i, running):
+        t = count - 1 - i
+        value = source_ref[t] + running
+        adjoint_ref[t] = value
+        return decay_ref[t] * value
+
+    lax.fori_loop(0, count, backward, entering_ref[...], unroll=8)
+    width = 16
+
+    def reduce(c, total):
+        ts = pl.ds(pl.multiple_of(c * width, width), width)
+        adj, bcol = adjoint_ref[ts], bmat_ref[ts]
+        inp, stp, grad = inp_ref[ts], step_ref[ts], grad_ref[ts]
+        dec, bef = decay_ref[ts], before_ref[ts]
+        input_out[ts] = (
+            stp * jnp.sum(bcol * adj, axis=1) + skip_ref[...] * grad
+        ).astype(input_out.dtype)
+        step_out[ts] = jnp.sum(
+            adj * (bcol * inp[:, None, :] - rate_ref[...][None] * dec * bef), axis=1
+        ).astype(step_out.dtype)
+        in_cols_out[ts] = jnp.sum(adj * (stp * inp)[:, None, :], axis=2)
+        return total + jnp.sum(adj * (-stp[:, None, :] * dec * bef), axis=0)
+
+    rate_out[...] = lax.fori_loop(0, count // width, reduce, jnp.zeros_like(rate_ref[...]))
+
+
+def adjoint_full(decays, sources, entering, bmats, inputs, steps, grads, before, rate, skip):
+    count, states, width = decays.shape
+    return pl.pallas_call(
+        adjoint_full_kernel,
+        out_shape=(
+            jax.ShapeDtypeStruct((count, width), jnp.bfloat16),
+            jax.ShapeDtypeStruct((count, width), jnp.bfloat16),
+            jax.ShapeDtypeStruct((count, states), jnp.float32),
+            jax.ShapeDtypeStruct((states, width), jnp.float32),
+        ),
+        scratch_shapes=[pltpu.VMEM(decays.shape, jnp.float32)],
+        cost_estimate=pl.CostEstimate(
+            flops=16 * decays.size, bytes_accessed=12 * decays.size, transcendentals=0
+        ),
+    )(decays, sources, entering, bmats[:, :, None], inputs, steps, grads, before, rate, skip[None])
 
 
 def relay_kernel(axis, count, pair_ref, out_ref, held, land, send_sems, recv_sems):
@@ -257,16 +306,9 @@
         [jnp.where(is_last, 0.0, shrink), jnp.where(is_last, shrink * end_grad + seed, seed)]
     )
     entering = jnp.where(is_last, end_grad, relay(pair, "ctx", 4))
-    adjoint = adjoint_scan(decays, sources, entering)
-    input_grad = (
-        steps * jnp.sum(bmats[:, :, None] * adjoint, axis=1) + skip_gain[None] * grads
-    ).astype(jnp.bfloat16)
-    step_grad = jnp.sum(
-        adjoint * (bmats[:, :, None] * inputs[:, None, :] - decay_rate[None] * decays * before),
-        axis=1,
-    ).astype(jnp.bfloat16)
-    in_cols = jnp.sum(adjoint * (steps * inputs)[:, None, :], axis=2)
-    rate_local = jnp.sum(adjoint * (-steps[:, None, :] * decays * before), axis=0)
+    input_grad, step_grad, in_cols, rate_local = adjoint_full(
+        decays, sources, entering, bmats, inputs, steps, grads, before, decay_rate, skip_gain
+    )
     ctx_count = lax.axis_size("ctx")
     rate_parts = rate_local.reshape(ctx_count, 1, rate_local.size // ctx_count)
     col_parts, rate_chunks = reduce_partials(jnp.stack([in_cols.T, out_cols.T]), rate_parts, 1)

time: 136 us -> 137 us (level)
  other arithmetic: 17.2 us -> 13.6 us
  Pallas kernels: 72.3 us -> 74.7 us
  local copies, waits for them, and re-layouts: 6.61 us -> 8.92 us
    reduce_sum x1 -> x0, other arithmetic: 4.13 us -> none  [body(): jnp.sum(adjoint * (-steps[:, None, :] * decays * before), axis=0)]
    pallas_call x1, Pallas kernels: 3.96 us -> 6.21 us  [adjoint_full(): pl.pallas_call(adjoint_full_kernel, out_shape=(jax.ShapeDtypeStruct((coun...]
    broadcast_in_dim x0 -> x1, local copies, waits for them, and re-layouts: none -> 1.41 us  [body(): driving = (steps * inputs)[:, None, :] * bmats[:, :, None]]
  transfers between devices with their start and end apart: 1 -> 1, of which waited for: 0 -> 0; matrix products, arithmetic and copies ran while one was open for 14% -> 13% of each run, Pallas kernels for 53% -> 55%
where the time goes in v10:
time: 137 us
  Pallas kernels  74.7 us (55%)
  blocking collectives  14.8 us (11%)
  between operations  14.2 us (10%)
  other arithmetic  13.6 us (10%)
  matrix products  10.6 us (8%)
  local copies, waits for them, and re-layouts  8.92 us (7%)
    pallas_call x1, Pallas kernels, relay(): pl.pallas_call(functools.partial(relay_kernel, axis, count), out_shape=ja...  43.2 us
    pallas_call x1, Pallas kernels, reduce_partials(): pl.pallas_call(reduce_kernel, out_shape=(jax.ShapeDtypeStruct((n_e,) + co...  19.7 us
    all_to_all x1, blocking collectives, body(): lax.all_to_all(buffer, 'exp', split_axis=0, concat_axis=1, tiled=True)  14.8 us
    dot_general x1, matrix products, body(): jnp.einsum('lrf,lrd->lfd', hidden_saved, all_rows, preferred_element_type...  6.86 us
    pallas_call x1, Pallas kernels, adjoint_full(): pl.pallas_call(adjoint_full_kernel, out_shape=(jax.ShapeDtypeStruct((coun...  6.21 us
    pallas_call x1, Pallas kernels, local_scans(): pl.pallas_call(local_scans_kernel, out_shape=(jax.ShapeDtypeStruct(decays...  5.61 us
    dot_general x1, matrix products, body(): jnp.einsum('lrd,lfd->lrf', all_rows, w_down, preferred_element_type=jnp.f...  3.42 us
  transfers between devices with their start and end apart: 1, of which 0 were waited for; matrix products, arithmetic and copies ran while one was open for 13% of the time, Pallas kernels for 55%

profile of v10, /device:TPU:1, one launch (start us, length us, event | category | flops | bytes accessed | tf_op | source)
XLA Modules:
  0.0 136.8 jit_solution(9778319850304832478)
XLA Ops:
  7.2 0.0 copy-start
  7.2 0.0 copy-start.8
  7.2 0.0 copy-start.6
  7.2 0.0 copy-start.10
  7.2 0.0 copy-start.3
  7.2 0.0 copy-start.4
  7.2 0.0 all-gather.2.cloned.1.call-start
  7.3 0.9 copy.37
  8.2 0.1 reshape.68
  8.2 0.1 fusion.24
  8.4 0.2 select_reduce_fusion
  8.5 0.9 mul.105
  9.5 0.2 mul.106
  9.7 0.8 copy.38
  10.4 0.1 mul.103
  10.5 0.3 convolution_convert_fusion
  10.9 0.2 reshape.69
  11.0 14.8 %all_to_all.12 = bf16[16,2,4096]{2,1,0:T(2,128)(2,1)S(1)} all-to-all(bf16[16,2,4096]{2,1,0:T(2,128)(2,1)S(1)} %reshape.69), channel_id=1, replica_groups=mesh['ctx'=32,'exp'=16] {'exp'}, dimensions={0} | all-to-all | bytes 524288 | tf_op jit(solution)/shard_map/all_to_all | solution.py:321
  25.8 0.0 copy-start.5
  25.8 0.8 all_to_all.10
  26.6 0.0 all-gather.2.cloned.1.call-update
  26.6 0.0 copy-done.8
  26.6 0.1 copy.33
  26.7 0.0 copy-done.6
  26.8 0.0 copy-start.1
  26.8 0.0 copy-done.10
  26.8 0.1 copy.32
  26.9 0.0 copy-done.3
  26.9 0.7 convert_element_type.38.step_ref
  27.5 0.0 copy-done.4
  27.5 0.6 convert_element_type.40.inp_ref
  28.2 1.7 %broadcast_multiply_fusion.1.source_ref = f32[128,16,256]{2,1,0:T(8,128)} fusion(f32[128,256]{1,0:T(8,128)S(1)} %convert_element_type.39.grad_ref, f32[128,16]{1,0:T(8,128)S(1)} %copy.32), kind=kLoop, calls=%fused_computation.13 | loop fusion | flops 524288 | bytes 2236416 | tf_op jit(solution)/shard_map/mul | solution.py:298
  29.9 0.0 copy-done.5
  29.9 2.6 %multiply_exponential_fusion = (f32[128,16,256]{2,1,0:T(8,128)}, f32[128,16,256]{2,1,0:T(8,128)}) fusion(f32[16,256]{1,0:T(8,128)S(1)} %copy-done.5, f32[128,256]{1,0:T(8,128)S(1)} %get-tuple-element.26, f32[128,16]{1,0:T(8,128)S(1)} %copy.33, f32[128,256]{1,0:T(8,128)S(1)} %get-tuple-element.27), kind=kLoop, calls=%fused_computation.8 | loop fusion | flops 1048576 | bytes 4481024 | tf_op jit(solution)/shard_map/exp | solution.py:296
  32.5 0.0 copy-done.1
  32.5 0.0 copy-start.7
  32.5 5.6 %shard_map.189 = (f32[128,16,256]{2,1,0:T(8,128)}, f32[128,16,256]{2,1,0:T(8,128)}, f32[16,256]{1,0:T(8,128)}) custom-call(f32[128,16,256]{2,1,0:T(8,128)} %get-tuple-element.32.decay_ref, f32[128,16,256]{2,1,0:T(8,128)} %get-tuple-element.33.drive_ref, f32[128,16,256]{2,1,0:T(8,128)} %broadcast_multiply_fusion.1.source_ref, f32[16,256]{1,0:T(8,128)} %bitcast.53), custom_call_target="tpu_custom_call" | custom-call | flops 2097152 | bytes 10485760 | tf_op jit(solution)/shard_map/pallas_call | solution.py:32
  38.1 0.0 copy-done.7
  38.1 0.7 select_bitcast_fusion
  38.8 0.6 pad_maximum_fusion.pair_ref
  39.4 43.2 %shard_map.190 = f32[16,256]{1,0:T(8,128)} custom-call(f32[2,16,256]{2,1,0:T(8,128)} %pad_maximum_fusion.pair_ref), custom_call_target="tpu_custom_call" | custom-call | tf_op jit(solution)/shard_map/pallas_call | solution.py:174
  82.6 1.4 %copy.34.bmat_ref = f32[128,16,1]{2,1,0:T(8,128)} copy(f32[128,16,1]{0,1,2:T(8,128)S(1)} %bitcast.50) | data formatting | bytes 16384 | tf_op jit(solution)/shard_map/broadcast_in_dim | solution.py:297
  84.0 1.3 broadcast_select_fusion.entering_ref
  85.3 0.0 copy-start.2
  85.3 6.2 %shard_map.191 = (bf16[128,256]{1,0:T(8,128)(2,1)}, bf16[128,256]{1,0:T(8,128)(2,1)}, f32[128,16]{1,0:T(8,128)}, f32[16,256]{1,0:T(8,128)}) custom-call(f32[128,16,256]{2,1,0:T(8,128)} %get-tuple-element.32.decay_ref, f32[128,16,256]{2,1,0:T(8,128)} %broadcast_multiply_fusion.1.source_ref, f32[16,256]{1,0:T(8,128)} %broadcast_select_fusion.entering_ref, ...), custom_call_target="tpu_custom_call" | custom-call | flops 8388608 | bytes 6291456 | tf_op jit(solution)/shard_map/pallas_call | solution.py:101
  91.5 0.0 copy-start.9
  91.5 0.9 copy.35
  92.5 0.0 copy-done.2
  92.5 2.0 %multiply_reduce_fusion = f32[128,16]{1,0:T(8,128)S(1)} fusion(f32[128,16,256]{2,1,0:T(8,128)} %get-tuple-element.21, f32[128,256]{1,0:T(8,128)S(1)} %copy-done.2), kind=kLoop, calls=%fused_computation.7 | loop fusion | flops 1046528 | bytes 2236416 | tf_op jit(solution)/shard_map/reduce_sum | solution.py:300
  94.5 0.1 copy.36
  94.6 0.0 copy-done.9
  94.6 0.6 reshape.66.parts_ref
  95.2 0.6 pad_maximum_fusion.1.cols_ref
  95.8 19.7 %shard_map.192 = (f32[16,2,16,128]{3,2,1,0:T(8,128)}, f32[32,1,128]{2,1,0:T(1,128)}) custom-call(f32[2,16,128]{2,1,0:T(8,128)} %pad_maximum_fusion.1.cols_ref, f32[32,1,128]{2,1,0:T(1,128)} %reshape.66.parts_ref), custom_call_target="tpu_custom_call" | custom-call | tf_op jit(solution)/shard_map/pallas_call | solution.py:236
  115.5 0.5 broadcast.27
  116.0 1.4 %reduce.3 = f32[32,128]{1,0:T(8,128)S(1)} reduce(f32[32,1,128]{2,1,0:T(1,128)} %get-tuple-element.24, f32[]{:T(128)} %broadcast.27), dimensions={1}, to_apply=%get-tuple-element.24.reduce_sub_computation.3 | reduce | bytes 32772 | tf_op jit(solution)/shard_map/pallas_call | solution.py:236
  117.4 0.6 reshape.67
  118.1 1.0 reduce_sum.38
  119.0 0.6 slice_bitcast_fusion
  119.6 0.0 copy-done.12
  119.6 6.9 %fusion.7 = bf16[1,224,4096]{2,1,0:T(8,128)(2,1)} fusion(bf16[1,1024,4096]{2,1,0:T(8,128)(2,1)} %all-gather.2.cloned.1.call-done, bf16[1,1024,224]{1,2,0:T(8,128)(2,1)S(1)} %copy-done.12), kind=kOutput, calls=%fused_computation.5 | convolution fusion | flops 1879965696 | bytes 10682368 | tf_op jit(solution)/shard_map/lrf,lrd->lfd/dot_general | solution.py:323
  126.5 0.0 copy-done
  126.5 0.0 copy-done.11
  126.5 3.4 %fusion.16 = bf16[1,1024,224]{1,2,0:T(8,128)(2,1)} fusion(bf16[1,224,4096]{2,1,0:T(8,128)(2,1)S(1)} %copy-done, bf16[1,1024,4096]{2,1,0:T(8,128)(2,1)S(1)} %copy-done.11), kind=kOutput, calls=%fused_computation.11 | convolution fusion | flops 1879277568 | bytes 10682368 | tf_op jit(solution)/shard_map/lrd,lfd->lrf/dot_general | solution.py:326
  (7 shorter events, 0.1 us)
Async XLA Ops:
  7.2 119.3 %copy-start = (bf16[1,224,4096]{2,1,0:T(8,128)(2,1)S(1)}, bf16[1,224,4096]{2,1,0:T(8,128)(2,1)}, u32[]{:S(2)}) copy-start(bf16[1,224,4096]{2,1,0:T(8,128)(2,1)} %param.26) | copy-start | bytes 5505028
  7.2 19.4 %copy-start.8 = (f32[16,128]{1,0:T(8,128)S(1)}, f32[16,128]{1,0:T(8,128)}, u32[]{:S(2)}) copy-start(f32[16,128]{1,0:T(8,128)} %param.17) | copy-start | bytes 24580
  7.2 19.5 %copy-start.6 = (bf16[128,256]{1,0:T(8,128)(2,1)S(1)}, bf16[128,256]{1,0:T(8,128)(2,1)}, u32[]{:S(2)}) copy-start(bf16[128,256]{1,0:T(8,128)(2,1)} %param.22) | copy-start | bytes 196612
  7.2 19.6 %copy-start.10 = (f32[16,128]{1,0:T(8,128)S(1)}, f32[16,128]{1,0:T(8,128)}, u32[]{:S(2)}) copy-start(f32[16,128]{1,0:T(8,128)} %param.18) | copy-start | bytes 24580
  7.2 19.7 %copy-start.3 = (bf16[128,256]{1,0:T(8,128)(2,1)S(1)}, bf16[128,256]{1,0:T(8,128)(2,1)}, u32[]{:S(2)}) copy-start(bf16[128,256]{1,0:T(8,128)(2,1)} %param.15) | copy-start | bytes 196612
  7.2 20.3 %copy-start.4 = (bf16[128,256]{1,0:T(8,128)(2,1)S(1)}, bf16[128,256]{1,0:T(8,128)(2,1)}, u32[]{:S(2)}) copy-start(bf16[128,256]{1,0:T(8,128)(2,1)} %param.14) | copy-start | bytes 196612
  7.2 112.4 %all-gather.2.cloned.1.call-start = ((), (), s32[]{:S(2)}) async-start(), calls=%async_computation.1 | async-start | bytes 8650752 | tf_op jit(solution)/shard_map/all_gather | solution.py:322
  25.8 4.1 %copy-start.5 = (f32[16,256]{1,0:T(8,128)S(1)}, f32[16,256]{1,0:T(8,128)}, u32[]{:S(2)}) copy-start(f32[16,256]{1,0:T(8,128)} %rate_ref.1) | copy-start | bytes 49156
  26.8 5.7 %copy-start.1 = (f32[128,256]{1,0:T(8,128)}, f32[128,256]{1,0:T(8,128)S(1)}, u32[]{:S(2)}) copy-start(f32[128,256]{1,0:T(8,128)S(1)} %convert_element_type.39.grad_ref) | copy-start | bytes 393220
  32.5 5.6 %copy-start.7 = (f32[16,256]{1,0:T(8,128)S(1)}, f32[16,256]{1,0:T(8,128)}, u32[]{:S(2)}) copy-start(f32[16,256]{1,0:T(8,128)} %param.21) | copy-start | bytes 49156
  85.3 7.2 %copy-start.2 = (f32[128,256]{1,0:T(8,128)S(1)}, f32[128,256]{1,0:T(8,128)}, u32[]{:S(2)}) copy-start(f32[128,256]{1,0:T(8,128)} %copy-done.1) | copy-start | bytes 393220
  91.5 3.0 %copy-start.9 = (f32[16,256]{1,0:T(8,128)S(1)}, f32[16,256]{1,0:T(8,128)}, u32[]{:S(2)}) copy-start(f32[16,256]{1,0:T(8,128)} %get-tuple-element.22) | copy-start | bytes 49156
  91.5 28.1 %copy-start.12 = (bf16[1,1024,224]{1,2,0:T(8,128)(2,1)S(1)}, bf16[1,1024,224]{1,2,0:T(8,128)(2,1)}, u32[]{:S(2)}) copy-start(bf16[1,1024,224]{1,2,0:T(8,128)(2,1)} %param.27) | copy-start | bytes 1376260
  119.6 6.9 %copy-start.11 = (bf16[1,1024,4096]{2,1,0:T(8,128)(2,1)S(1)}, bf16[1,1024,4096]{2,1,0:T(8,128)(2,1)}, u32[]{:S(2)}) copy-start(bf16[1,1024,4096]{2,1,0:T(8,128)(2,1)} %all-gather.2.cloned.1.call-done) | copy-start | bytes 25165828
Sparse Core Ops, SparseCore 0:
  26.7 87.6 all-gather.1

commit v11 on v9

--- a/solution.py
+++ b/solution.py
@@ -10,12 +10,19 @@
 EXPERTS = 16
 
 
-def local_scans_kernel(decay_ref, drive_ref, source_ref, first_ref, states_ref, before_ref, seed_ref):
-    count = decay_ref.shape[0]
+def local_scans_kernel(
+    step_ref, inp_ref, grad_ref, bcol_ref, ccol_ref, rate_ref, first_ref,
+    decay_ref, source_ref, states_ref, before_ref, seed_ref,
+):
+    count = step_ref.shape[0]
 
     def forward(t, state):
+        stp, inp = step_ref[pl.ds(t, 1), :], inp_ref[pl.ds(t, 1), :]
+        decay = jnp.exp(-stp * rate_ref[...])
+        decay_ref[t] = decay
+        source_ref[t] = ccol_ref[t] * grad_ref[pl.ds(t, 1), :]
         before_ref[t] = state
-        state = decay_ref[t] * state + drive_ref[t]
+        state = decay * state + (stp * inp) * bcol_ref[t]
         states_ref[t] = state
         return state
 
@@ -28,18 +35,17 @@
     seed_ref[...] = lax.fori_loop(0, count, backward, jnp.zeros_like(first_ref[...]), unroll=8)
 
 
-def local_scans(decays, driving, sources, first_state):
+def local_scans(steps, inputs, grads, bmats, cmats, rate, first_state):
+    full = jax.ShapeDtypeStruct((steps.shape[0],) + rate.shape, jnp.float32)
     return pl.pallas_call(
         local_scans_kernel,
-        out_shape=(
-            jax.ShapeDtypeStruct(decays.shape, jnp.float32),
-            jax.ShapeDtypeStruct(decays.shape, jnp.float32),
-            jax.ShapeDtypeStruct(first_state.shape, jnp.float32),
+        out_shape=(full, full, full, full, jax.ShapeDtypeStruct(first_state.shape, jnp.float32)),
+        cost_estimate=pl.CostEstimate(
+            flops=8 * steps.shape[0] * rate.size,
+            bytes_accessed=16 * steps.shape[0] * rate.size,
+            transcendentals=steps.shape[0] * rate.size,
         ),
-        cost_estimate=pl.CostEstimate(
-            flops=4 * decays.size, bytes_accessed=20 * decays.size, transcendentals=0
-        ),
-    )(decays, driving, sources, first_state)
+    )(steps, inputs, grads, bmats[:, :, None], cmats[:, :, None], rate, first_state)
 
 
 def adjoint_scan_kernel(decay_ref, source_ref, entering_ref, adjoint_ref):
@@ -244,10 +250,9 @@
     bmats = input_proj.T
     cmats = output_proj.T
     first_state = block_states[0]
-    decays = jnp.exp(-steps[:, None, :] * decay_rate[None])
-    driving = (steps * inputs)[:, None, :] * bmats[:, :, None]
-    sources = cmats[:, :, None] * grads[:, None, :]
-    states, before, seed = local_scans(decays, driving, sources, first_state)
+    decays, sources, states, before, seed = local_scans(
+        steps, inputs, grads, bmats, cmats, decay_rate, first_state
+    )
     out_cols = jnp.sum(states * grads[:, None, :], axis=2)
     shrink = jnp.exp(-decay_rate * jnp.sum(steps, axis=0)[None])
     position = lax.axis_index("ctx")

time: 136 us -> 139 us (1.022)
  local copies, waits for them, and re-layouts: 6.61 us -> 9.35 us
  other arithmetic: 17.2 us -> 15.2 us
  Pallas kernels: 72.3 us -> 74.2 us
    broadcast_in_dim x0 -> x2, local copies, waits for them, and re-layouts: none -> 2.83 us  [the longest x1 1.43 us: local_scans(): cmats[:, :, None]]
    exp x1 -> x0, other arithmetic: 2.62 us -> none  [body(): decays = jnp.exp(-steps[:, None, :] * decay_rate[None])]
    mul x1, other arithmetic: 1.73 us -> 0.04 us  [body(): in_cols = jnp.sum(adjoint * (steps * inputs)[:, None, :], axis=2)]
    pallas_call x1, Pallas kernels: 5.51 us -> 7.01 us  [local_scans(): pl.pallas_call(local_scans_kernel, out_shape=(full, full, full, full, jax...]
  transfers between devices with their start and end apart: 1 -> 1, of which waited for: 0 -> 0; matrix products, arithmetic and copies ran while one was open for 14% -> 15% of each run, Pallas kernels for 53% -> 54%
where the time goes in v11:
time: 139 us; the launch traced here: 138 us
  Pallas kernels  74.2 us (53%)
  other arithmetic  15.2 us (11%)
  blocking collectives  14.8 us (11%)
  between operations  14.2 us (10%)
  matrix products  10.6 us (8%)
  local copies, waits for them, and re-layouts  9.35 us (7%)
    pallas_call x1, Pallas kernels, relay(): pl.pallas_call(functools.partial(relay_kernel, axis, count), out_shape=ja...  43.1 us
    pallas_call x1, Pallas kernels, reduce_partials(): pl.pallas_call(reduce_kernel, out_shape=(jax.ShapeDtypeStruct((n_e,) + co...  20.1 us
    all_to_all x1, blocking collectives, body(): lax.all_to_all(buffer, 'exp', split_axis=0, concat_axis=1, tiled=True)  14.8 us
    pallas_call x1, Pallas kernels, local_scans(): pl.pallas_call(local_scans_kernel, out_shape=(full, full, full, full, jax...  7.01 us
    dot_general x1, matrix products, body(): jnp.einsum('lrf,lrd->lfd', hidden_saved, all_rows, preferred_element_type...  6.83 us
    reduce_sum x1, other arithmetic, body(): jnp.sum(adjoint * (-steps[:, None, :] * decays * before), axis=0)  4.45 us
    pallas_call x1, Pallas kernels, adjoint_scan(): pl.pallas_call(adjoint_scan_kernel, out_shape=jax.ShapeDtypeStruct(decays...  4.02 us
    dot_general x1, matrix products, body(): jnp.einsum('lrd,lfd->lrf', all_rows, w_down, preferred_element_type=jnp.f...  3.42 us
  transfers between devices with their start and end apart: 1, of which 0 were waited for; matrix products, arithmetic and copies ran while one was open for 15% of the time, Pallas kernels for 54%

profile of v11, /device:TPU:1, one launch (start us, length us, event | category | flops | bytes accessed | tf_op | source)
XLA Modules:
  0.0 138.3 jit_solution(9072218681086794406)
XLA Ops:
  7.2 0.0 copy-start
  7.2 0.0 copy-start.5
  7.2 0.0 copy-start.4
  7.2 0.0 copy-start.8
  7.2 0.0 all-gather.2.cloned.1.call-start
  7.3 0.9 copy.35
  8.1 0.1 reshape.69
  8.2 0.1 fusion.24
  8.3 0.2 select_reduce_fusion
  8.5 0.9 mul.143
  9.5 0.0 copy-start.9
  9.5 0.2 mul.144
  9.7 0.8 copy.36
  10.4 0.1 mul.141
  10.5 0.3 convolution_convert_fusion
  10.8 0.0 copy-start.3
  10.9 0.2 reshape.70
  11.0 14.8 %all_to_all.12 = bf16[16,2,4096]{2,1,0:T(2,128)(2,1)S(1)} all-to-all(bf16[16,2,4096]{2,1,0:T(2,128)(2,1)S(1)} %reshape.70), channel_id=1, replica_groups=mesh['ctx'=32,'exp'=16] {'exp'}, dimensions={0} | all-to-all | bytes 524288 | tf_op jit(solution)/shard_map/all_to_all | solution.py:284
  25.8 0.8 all_to_all.10
  26.6 0.0 all-gather.2.cloned.1.call-update
  26.6 0.0 copy-done.5
  26.6 0.7 convert_element_type.45.inp_ref
  27.3 0.0 copy-done.4
  27.3 0.7 convert_element_type.46.grad_ref
  27.9 0.0 copy-done.8
  28.0 1.4 %copy.31.bcol_ref = f32[128,16,1]{2,1,0:T(8,128)} copy(f32[128,16,1]{0,1,2:T(8,128)S(1)} %bitcast.50) | data formatting | bytes 16384 | tf_op jit(solution)/shard_map/broadcast_in_dim | solution.py:267
  29.4 0.0 copy-start.6
  29.4 0.0 copy-start.7
  29.4 0.0 copy-done.9
  29.4 1.4 %copy.32.ccol_ref = f32[128,16,1]{2,1,0:T(8,128)} copy(f32[128,16,1]{0,1,2:T(8,128)S(1)} %bitcast.55) | data formatting | bytes 16384 | tf_op jit(solution)/shard_map/broadcast_in_dim | solution.py:48
  30.8 0.0 copy-done.3
  30.8 0.7 convert_element_type.44.step_ref
  31.5 7.0 %shard_map.189 = (f32[128,16,256]{2,1,0:T(8,128)}, f32[128,16,256]{2,1,0:T(8,128)}, f32[128,16,256]{2,1,0:T(8,128)}, f32[128,16,256]{2,1,0:T(8,128)}, f32[16,256]{1,0:T(8,128)}) custom-call(f32[128,256]{1,0:T(8,128)} %convert_element_type.44.step_ref, f32[128,256]{1,0:T(8,128)} %convert_element_type.45.inp_ref, f32[128,256]{1,0:T(8,128)} %convert_element_type.46.grad_ref, ...), custom_call_target="tpu_custom_call" | custom-call | flops 4194304 | bytes 8388608 | tf_op jit(solution)/shard_map/pallas_call | solution.py:40
  38.5 0.0 copy-done.6
  38.5 0.0 copy-done.7
  38.5 0.7 select_bitcast_fusion
  39.3 0.6 pad_maximum_fusion.pair_ref
  39.9 43.1 %shard_map.190 = f32[16,256]{1,0:T(8,128)} custom-call(f32[2,16,256]{2,1,0:T(8,128)} %pad_maximum_fusion.pair_ref), custom_call_target="tpu_custom_call" | custom-call | tf_op jit(solution)/shard_map/pallas_call | solution.py:131
  83.0 0.1 copy.30
  83.1 1.3 broadcast_select_fusion.entering_ref
  84.4 0.0 copy-start.1
  84.4 4.0 %shard_map.191 = f32[128,16,256]{2,1,0:T(8,128)} custom-call(f32[128,16,256]{2,1,0:T(8,128)} %get-tuple-element.14.decay_ref, f32[128,16,256]{2,1,0:T(8,128)} %get-tuple-element.15.source_ref, f32[16,256]{1,0:T(8,128)} %broadcast_select_fusion.entering_ref), custom_call_target="tpu_custom_call" | custom-call | flops 1048576 | bytes 6291456 | tf_op jit(solution)/shard_map/pallas_call | solution.py:64
  88.4 0.0 copy-done.1
  88.4 0.0 copy-start.2
  88.4 4.5 %multiply_reduce_fusion = (f32[16,256]{1,0:T(8,128)S(1)}, bf16[128,256]{1,0:T(8,128)(2,1)}, f32[128,256]{1,0:T(8,128)S(1)}, f32[128,16]{1,0:T(8,128)S(1)}) fusion(f32[128,16,256]{2,1,0:T(8,128)} %shard_map.191, f32[128,16,256]{2,1,0:T(8,128)} %get-tuple-element.17, f32[128,16,256]{2,1,0:T(8,128)} %get-tuple-element.14.decay_ref, ...), kind=kLoop, calls=%fused_computation.7 | loop fusion | flops 7268352 | bytes 6930432 | tf_op jit(solution)/shard_map/reduce_sum | solution.py:274
  92.9 0.0 copy-start.10
  92.9 0.0 copy-done.2
  92.9 2.1 %multiply_reduce_fusion.1 = f32[128,16]{1,0:T(8,128)S(1)} fusion(f32[128,16,256]{2,1,0:T(8,128)} %get-tuple-element.18, f32[128,256]{1,0:T(8,128)S(1)} %copy-done.2), kind=kLoop, calls=%fused_computation.8 | loop fusion | flops 1046528 | bytes 2236416 | tf_op jit(solution)/shard_map/reduce_sum | solution.py:256
  95.0 0.1 copy.34
  95.1 0.6 reshape.67.parts_ref
  95.7 0.6 pad_maximum_fusion.1.cols_ref
  96.3 20.1 %shard_map.192 = (f32[16,2,16,128]{3,2,1,0:T(8,128)}, f32[32,1,128]{2,1,0:T(1,128)}) custom-call(f32[2,16,128]{2,1,0:T(8,128)} %pad_maximum_fusion.1.cols_ref, f32[32,1,128]{2,1,0:T(1,128)} %reshape.67.parts_ref), custom_call_target="tpu_custom_call" | custom-call | tf_op jit(solution)/shard_map/pallas_call | solution.py:193
  116.4 0.5 broadcast.28
  116.9 1.4 %reduce.3 = f32[32,128]{1,0:T(8,128)S(1)} reduce(f32[32,1,128]{2,1,0:T(1,128)} %get-tuple-element.20, f32[]{:T(128)} %broadcast.28), dimensions={1}, to_apply=%get-tuple-element.20.reduce_sub_computation.3 | reduce | bytes 32772 | tf_op jit(solution)/shard_map/pallas_call | solution.py:193
  118.3 0.6 reshape.68
  119.0 1.0 reduce_sum.78
  119.9 0.6 slice_bitcast_fusion
  120.5 0.0 copy-done.10
  120.5 0.7 add_convert_fusion
  121.2 0.0 copy-done.12
  121.2 6.8 %fusion.7 = bf16[1,224,4096]{2,1,0:T(8,128)(2,1)} fusion(bf16[1,1024,4096]{2,1,0:T(8,128)(2,1)} %all-gather.2.cloned.1.call-done, bf16[1,1024,224]{1,2,0:T(8,128)(2,1)S(1)} %copy-done.12), kind=kOutput, calls=%fused_computation.5 | convolution fusion | flops 1879965696 | bytes 10682368 | tf_op jit(solution)/shard_map/lrf,lrd->lfd/dot_general | solution.py:286
  128.0 0.0 copy-done
  128.0 0.0 copy-done.11
  128.0 3.4 %fusion.16 = bf16[1,1024,224]{1,2,0:T(8,128)(2,1)} fusion(bf16[1,224,4096]{2,1,0:T(8,128)(2,1)S(1)} %copy-done, bf16[1,1024,4096]{2,1,0:T(8,128)(2,1)S(1)} %copy-done.11), kind=kOutput, calls=%fused_computation.14 | convolution fusion | flops 1879277568 | bytes 10682368 | tf_op jit(solution)/shard_map/lrd,lfd->lrf/dot_general | solution.py:289
  (7 shorter events, 0.1 us)
Async XLA Ops:
  7.2 120.9 %copy-start = (bf16[1,224,4096]{2,1,0:T(8,128)(2,1)S(1)}, bf16[1,224,4096]{2,1,0:T(8,128)(2,1)}, u32[]{:S(2)}) copy-start(bf16[1,224,4096]{2,1,0:T(8,128)(2,1)} %param.26) | copy-start | bytes 5505028
  7.2 19.4 %copy-start.5 = (bf16[128,256]{1,0:T(8,128)(2,1)S(1)}, bf16[128,256]{1,0:T(8,128)(2,1)}, u32[]{:S(2)}) copy-start(bf16[128,256]{1,0:T(8,128)(2,1)} %param.14) | copy-start | bytes 196612
  7.2 20.1 %copy-start.4 = (bf16[128,256]{1,0:T(8,128)(2,1)S(1)}, bf16[128,256]{1,0:T(8,128)(2,1)}, u32[]{:S(2)}) copy-start(bf16[128,256]{1,0:T(8,128)(2,1)} %param.22) | copy-start | bytes 196612
  7.2 20.7 %copy-start.8 = (f32[16,128]{1,0:T(8,128)S(1)}, f32[16,128]{1,0:T(8,128)}, u32[]{:S(2)}) copy-start(f32[16,128]{1,0:T(8,128)} %param.17) | copy-start | bytes 24580
  7.2 114.0 %all-gather.2.cloned.1.call-start = ((), (), s32[]{:S(2)}) async-start(), calls=%async_computation.1 | async-start | bytes 8650752 | tf_op jit(solution)/shard_map/all_gather | solution.py:285
  9.5 19.9 %copy-start.9 = (f32[16,128]{1,0:T(8,128)S(1)}, f32[16,128]{1,0:T(8,128)}, u32[]{:S(2)}) copy-start(f32[16,128]{1,0:T(8,128)} %param.18) | copy-start | bytes 24580
  10.8 20.0 %copy-start.3 = (bf16[128,256]{1,0:T(8,128)(2,1)S(1)}, bf16[128,256]{1,0:T(8,128)(2,1)}, u32[]{:S(2)}) copy-start(bf16[128,256]{1,0:T(8,128)(2,1)} %param.15) | copy-start | bytes 196612
  29.4 9.1 %copy-start.6 = (f32[16,256]{1,0:T(8,128)S(1)}, f32[16,256]{1,0:T(8,128)}, u32[]{:S(2)}) copy-start(f32[16,256]{1,0:T(8,128)} %rate_ref.1) | copy-start | bytes 49156
  29.4 9.2 %copy-start.7 = (f32[16,256]{1,0:T(8,128)S(1)}, f32[16,256]{1,0:T(8,128)}, u32[]{:S(2)}) copy-start(f32[16,256]{1,0:T(8,128)} %param.21) | copy-start | bytes 49156
  84.4 4.0 %copy-start.1 = (f32[128,256]{1,0:T(8,128)S(1)}, f32[128,256]{1,0:T(8,128)}, u32[]{:S(2)}) copy-start(f32[128,256]{1,0:T(8,128)} %convert_element_type.45.inp_ref) | copy-start | bytes 393220
  88.4 4.5 %copy-start.2 = (f32[128,256]{1,0:T(8,128)S(1)}, f32[128,256]{1,0:T(8,128)}, u32[]{:S(2)}) copy-start(f32[128,256]{1,0:T(8,128)} %convert_element_type.46.grad_ref) | copy-start | bytes 393220
  92.9 27.6 %copy-start.10 = (f32[256]{0:T(256)S(1)}, f32[256]{0:T(256)}, u32[]{:S(2)}) copy-start(f32[256]{0:T(256)} %param.19) | copy-start | bytes 3076
  92.9 28.3 %copy-start.12 = (bf16[1,1024,224]{1,2,0:T(8,128)(2,1)S(1)}, bf16[1,1024,224]{1,2,0:T(8,128)(2,1)}, u32[]{:S(2)}) copy-start(bf16[1,1024,224]{1,2,0:T(8,128)(2,1)} %param.27) | copy-start | bytes 1376260
  121.2 6.8 %copy-start.11 = (bf16[1,1024,4096]{2,1,0:T(8,128)(2,1)S(1)}, bf16[1,1024,4096]{2,1,0:T(8,128)(2,1)}, u32[]{:S(2)}) copy-start(bf16[1,1024,4096]{2,1,0:T(8,128)(2,1)} %all-gather.2.cloned.1.call-done) | copy-start | bytes 25165828
Sparse Core Ops, SparseCore 0:
  26.7 87.9 all-gather.1

commit v12 on v9

--- a/solution.py
+++ b/solution.py
@@ -62,6 +62,32 @@
             flops=2 * decays.size, bytes_accessed=12 * decays.size, transcendentals=0
         ),
     )(decays, sources, entering)
+
+
+def weight_grad_kernel(saved_ref, rows_ref, out_ref):
+    out_ref[...] = jnp.dot(
+        saved_ref[...], rows_ref[...], preferred_element_type=jnp.float32
+    ).astype(out_ref.dtype)
+
+
+def weight_grad(saved_t, rows, tile=512):
+    features, slots = saved_t.shape
+    width = rows.shape[1]
+    return pl.pallas_call(
+        weight_grad_kernel,
+        out_shape=jax.ShapeDtypeStruct((features, width), jnp.bfloat16),
+        grid=(width // tile,),
+        in_specs=[
+            pl.BlockSpec((features, slots), lambda j: (0, 0)),
+            pl.BlockSpec((slots, tile), lambda j: (0, j)),
+        ],
+        out_specs=pl.BlockSpec((features, tile), lambda j: (0, j)),
+        cost_estimate=pl.CostEstimate(
+            flops=2 * features * slots * width,
+            bytes_accessed=2 * (features * slots + slots * width + features * width),
+            transcendentals=0,
+        ),
+    )(saved_t, rows)
 
 
 def relay_kernel(axis, count, pair_ref, out_ref, held, land, send_sems, recv_sems):
@@ -278,13 +304,10 @@
     buffer = slot_buffer(moe_grad, route, gate_prob, capacity)
     received_rows = lax.all_to_all(buffer, "exp", split_axis=0, concat_axis=1, tiled=True)
     all_rows = lax.all_gather(received_rows, "ctx", axis=1, tiled=True)
-    weight_total = jnp.einsum(
-        "lrf,lrd->lfd", hidden_saved, all_rows, preferred_element_type=jnp.float32
-    )
+    down_grad = weight_grad(hidden_saved[0].T, all_rows[0])[None]
     hidden_grad = jnp.einsum(
         "lrd,lfd->lrf", all_rows, w_down, preferred_element_type=jnp.float32
     ).astype(jnp.bfloat16)
-    down_grad = weight_total.astype(jnp.bfloat16)
     return (input_grad, step_grad, in_proj_grad, out_proj_grad, decay_grad, down_grad, hidden_grad)
 
 

time: 136 us -> 141 us (1.037)
  Pallas kernels: 72.3 us -> 80.7 us
  matrix products: 10.6 us -> 7.1 us
    pallas_call x0 -> x1, Pallas kernels: none -> 8.44 us  [weight_grad(): pl.pallas_call(weight_grad_kernel, out_shape=jax.ShapeDtypeStruct((featur...]
    dot_general x1 -> x0, matrix products: 6.83 us -> none  [body(): jnp.einsum('lrf,lrd->lfd', hidden_saved, all_rows, preferred_element_type...]
    dot_general x1, matrix products: 3.41 us -> 6.77 us  [body(): jnp.einsum('lrd,lfd->lrf', all_rows, w_down, preferred_element_type=jnp.f...]
  transfers between devices with their start and end apart: 1 -> 1, of which waited for: 0 -> 0; matrix products, arithmetic and copies ran while one was open for 14% -> 14% of each run, Pallas kernels for 53% -> 51%
where the time goes in v12:
time: 141 us
  Pallas kernels  80.7 us (57%)
  other arithmetic  17.2 us (12%)
  blocking collectives  14.8 us (10%)
  between operations  14.2 us (10%)
  matrix products  7.1 us (5%)
  local copies, waits for them, and re-layouts  6.6 us (5%)
    pallas_call x1, Pallas kernels, relay(): pl.pallas_call(functools.partial(relay_kernel, axis, count), out_shape=ja...  43.6 us
    pallas_call x1, Pallas kernels, reduce_partials(): pl.pallas_call(reduce_kernel, out_shape=(jax.ShapeDtypeStruct((n_e,) + co...  19.2 us
    all_to_all x1, blocking collectives, body(): lax.all_to_all(buffer, 'exp', split_axis=0, concat_axis=1, tiled=True)  14.8 us
    pallas_call x1, Pallas kernels, weight_grad(): pl.pallas_call(weight_grad_kernel, out_shape=jax.ShapeDtypeStruct((featur...  8.44 us
    dot_general x1, matrix products, body(): jnp.einsum('lrd,lfd->lrf', all_rows, w_down, preferred_element_type=jnp.f...  6.77 us
    pallas_call x1, Pallas kernels, local_scans(): pl.pallas_call(local_scans_kernel, out_shape=(jax.ShapeDtypeStruct(decays...  5.51 us
    reduce_sum x1, other arithmetic, body(): jnp.sum(adjoint * (-steps[:, None, :] * decays * before), axis=0)  4.13 us
    pallas_call x1, Pallas kernels, adjoint_scan(): pl.pallas_call(adjoint_scan_kernel, out_shape=jax.ShapeDtypeStruct(decays...  3.96 us
  transfers between devices with their start and end apart: 1, of which 0 were waited for; matrix products, arithmetic and copies ran while one was open for 14% of the time, Pallas kernels for 51%

profile of v12, /device:TPU:1, one launch (start us, length us, event | category | flops | bytes accessed | tf_op | source)
XLA Modules:
  0.0 140.6 jit_solution(1515170774523752825)
XLA Ops:
  7.2 0.0 copy-start
  7.2 0.0 copy-start.6
  7.2 0.0 copy-start.1
  7.2 0.0 copy-start.7
  7.2 0.0 copy-start.2
  7.2 0.0 copy-start.3
  7.2 0.0 all-gather.2.cloned.1.call-start
  7.3 0.9 copy.33
  8.2 0.1 reshape.62
  8.2 0.1 fusion.12
  8.4 0.2 select_reduce_fusion
  8.5 0.9 mul.177
  9.5 0.2 mul.178
  9.7 0.8 copy.34
  10.4 0.1 mul.175
  10.5 0.3 convolution_convert_fusion
  10.9 0.2 reshape.63
  11.0 14.8 %all_to_all.12 = bf16[16,2,4096]{2,1,0:T(2,128)(2,1)S(1)} all-to-all(bf16[16,2,4096]{2,1,0:T(2,128)(2,1)S(1)} %reshape.63), channel_id=1, replica_groups=mesh['ctx'=32,'exp'=16] {'exp'}, dimensions={0} | all-to-all | bytes 524288 | tf_op jit(solution)/shard_map/all_to_all | solution.py:305
  25.8 0.0 copy-start.4
  25.8 0.8 all_to_all.10
  26.6 0.0 all-gather.2.cloned.1.call-update
  26.6 0.0 copy-done.6
  26.6 0.1 copy.29
  26.7 0.0 copy-done.1
  26.8 0.0 copy-done.7
  26.8 0.1 copy.30
  26.9 0.0 copy-done.2
  26.9 0.0 copy-done.3
  27.0 1.7 %broadcast_multiply_fusion.1.source_ref = f32[128,16,256]{2,1,0:T(8,128)} fusion(f32[128,256]{1,0:T(8,128)S(1)} %convert_element_type.36, f32[128,16]{1,0:T(8,128)S(1)} %copy.30), kind=kLoop, calls=%fused_computation.12 | loop fusion | flops 524288 | bytes 2236416 | tf_op jit(solution)/shard_map/mul | solution.py:275
  28.7 0.0 copy-done.4
  28.7 2.6 %multiply_exponential_fusion = (f32[128,16,256]{2,1,0:T(8,128)}, f32[128,16,256]{2,1,0:T(8,128)}) fusion(f32[16,256]{1,0:T(8,128)S(1)} %copy-done.4, f32[128,256]{1,0:T(8,128)S(1)} %get-tuple-element.23, f32[128,16]{1,0:T(8,128)S(1)} %copy.29, f32[128,256]{1,0:T(8,128)S(1)} %get-tuple-element.22), kind=kLoop, calls=%fused_computation.6 | loop fusion | flops 1048576 | bytes 4481024 | tf_op jit(solution)/shard_map/exp | solution.py:273
  31.3 0.0 copy-start.5
  31.3 5.5 %shard_map.189 = (f32[128,16,256]{2,1,0:T(8,128)}, f32[128,16,256]{2,1,0:T(8,128)}, f32[16,256]{1,0:T(8,128)}) custom-call(f32[128,16,256]{2,1,0:T(8,128)} %get-tuple-element.28.decay_ref, f32[128,16,256]{2,1,0:T(8,128)} %get-tuple-element.29.drive_ref, f32[128,16,256]{2,1,0:T(8,128)} %broadcast_multiply_fusion.1.source_ref, f32[16,256]{1,0:T(8,128)} %bitcast.38), custom_call_target="tpu_custom_call" | custom-call | flops 2097152 | bytes 10485760 | tf_op jit(solution)/shard_map/pallas_call | solution.py:32
  36.8 0.0 copy-done.5
  36.8 0.7 select_bitcast_fusion
  37.6 0.6 pad_maximum_fusion.pair_ref
  38.2 43.6 %shard_map.190 = f32[16,256]{1,0:T(8,128)} custom-call(f32[2,16,256]{2,1,0:T(8,128)} %pad_maximum_fusion.pair_ref), custom_call_target="tpu_custom_call" | custom-call | tf_op jit(solution)/shard_map/pallas_call | solution.py:151
  81.8 1.3 broadcast_select_fusion.entering_ref
  83.1 4.0 %shard_map.191 = f32[128,16,256]{2,1,0:T(8,128)} custom-call(f32[128,16,256]{2,1,0:T(8,128)} %get-tuple-element.28.decay_ref, f32[128,16,256]{2,1,0:T(8,128)} %broadcast_multiply_fusion.1.source_ref, f32[16,256]{1,0:T(8,128)} %broadcast_select_fusion.entering_ref), custom_call_target="tpu_custom_call" | custom-call | flops 1048576 | bytes 6291456 | tf_op jit(solution)/shard_map/pallas_call | solution.py:58
  87.1 4.1 %multiply_reduce_fusion = (f32[16,256]{1,0:T(8,128)S(1)}, bf16[128,256]{1,0:T(8,128)(2,1)}, f32[128,256]{1,0:T(8,128)S(1)}, f32[128,16]{1,0:T(8,128)S(1)}) fusion(f32[128,16,256]{2,1,0:T(8,128)} %shard_map.191, f32[128,16,256]{2,1,0:T(8,128)} %get-tuple-element.13, f32[16,256]{1,0:T(8,128)S(1)} %copy-done.4, f32[128,256]{1,0:T(8,128)S(1)} %get-tuple-element.23, ...), kind=kLoop, calls=%fused_computation.1 | loop fusion | flops 7792640 | bytes 4833280 | tf_op jit(solution)/shard_map/reduce_sum | solution.py:295
  91.2 0.0 copy-start.8
  91.3 2.0 %multiply_reduce_fusion.1 = f32[128,16]{1,0:T(8,128)S(1)} fusion(f32[128,16,256]{2,1,0:T(8,128)} %get-tuple-element.14, f32[128,256]{1,0:T(8,128)S(1)} %convert_element_type.36), kind=kLoop, calls=%fused_computation.2 | loop fusion | flops 1046528 | bytes 2236416 | tf_op jit(solution)/shard_map/reduce_sum | solution.py:277
  93.3 0.1 copy.32
  93.3 0.6 reshape.60.parts_ref
  94.0 0.6 pad_maximum_fusion.1.cols_ref
  94.6 19.2 %shard_map.192 = (f32[16,2,16,128]{3,2,1,0:T(8,128)}, f32[32,1,128]{2,1,0:T(1,128)}) custom-call(f32[2,16,128]{2,1,0:T(8,128)} %pad_maximum_fusion.1.cols_ref, f32[32,1,128]{2,1,0:T(1,128)} %reshape.60.parts_ref), custom_call_target="tpu_custom_call" | custom-call | tf_op jit(solution)/shard_map/pallas_call | solution.py:213
  113.8 0.5 broadcast.29
  114.3 1.4 reduce.3
  115.7 0.6 reshape.61
  116.3 1.0 reduce_sum.78
  117.3 0.6 slice_bitcast_fusion
  117.9 0.0 copy-done.8
  117.9 0.7 fusion.9
  118.6 0.0 all-gather.2.cloned.1.call-done
  118.6 8.4 %shard_map.193 = bf16[224,4096]{1,0:T(8,128)(2,1)} custom-call(bf16[224,1024]{1,0:T(8,128)(2,1)} %bitcast.35, bf16[1024,4096]{1,0:T(8,128)(2,1)} %bitcast.33), custom_call_target="tpu_custom_call" | custom-call | flops 1879048192 | bytes 10682368 | tf_op jit(solution)/shard_map/pallas_call | solution.py:76
  127.0 0.0 copy-done
  127.0 6.8 %fusion.5 = bf16[1,1024,224]{1,2,0:T(8,128)(2,1)} fusion(bf16[1,224,4096]{2,1,0:T(8,128)(2,1)S(1)} %copy-done, bf16[1,1024,4096]{2,1,0:T(8,128)(2,1)} %all-gather.2.cloned.1.call-done), kind=kOutput, calls=%fused_computation.10 | convolution fusion | flops 1879277568 | bytes 10682368 | tf_op jit(solution)/shard_map/lrd,lfd->lrf/dot_general | solution.py:308
  (6 shorter events, 0.2 us)
Async XLA Ops:
  7.2 119.8 %copy-start = (bf16[1,224,4096]{2,1,0:T(8,128)(2,1)S(1)}, bf16[1,224,4096]{2,1,0:T(8,128)(2,1)}, u32[]{:S(2)}) copy-start(bf16[1,224,4096]{2,1,0:T(8,128)(2,1)} %param.26) | copy-start | bytes 5505028
  7.2 19.4 %copy-start.6 = (f32[16,128]{1,0:T(8,128)S(1)}, f32[16,128]{1,0:T(8,128)}, u32[]{:S(2)}) copy-start(f32[16,128]{1,0:T(8,128)} %param.17) | copy-start | bytes 24580
  7.2 19.5 %copy-start.1 = (bf16[128,256]{1,0:T(8,128)(2,1)S(1)}, bf16[128,256]{1,0:T(8,128)(2,1)}, u32[]{:S(2)}) copy-start(bf16[128,256]{1,0:T(8,128)(2,1)} %param.22) | copy-start | bytes 196612
  7.2 19.6 %copy-start.7 = (f32[16,128]{1,0:T(8,128)S(1)}, f32[16,128]{1,0:T(8,128)}, u32[]{:S(2)}) copy-start(f32[16,128]{1,0:T(8,128)} %param.18) | copy-start | bytes 24580
  7.2 19.7 %copy-start.2 = (bf16[128,256]{1,0:T(8,128)(2,1)S(1)}, bf16[128,256]{1,0:T(8,128)(2,1)}, u32[]{:S(2)}) copy-start(bf16[128,256]{1,0:T(8,128)(2,1)} %param.14) | copy-start | bytes 196612
  7.2 19.7 %copy-start.3 = (bf16[128,256]{1,0:T(8,128)(2,1)S(1)}, bf16[128,256]{1,0:T(8,128)(2,1)}, u32[]{:S(2)}) copy-start(bf16[128,256]{1,0:T(8,128)(2,1)} %param.15) | copy-start | bytes 196612
  7.2 111.3 %all-gather.2.cloned.1.call-start = ((), (), s32[]{:S(2)}) async-start(), calls=%async_computation.1 | async-start | bytes 8650752 | tf_op jit(solution)/shard_map/all_gather | solution.py:306
  25.8 2.9 %copy-start.4 = (f32[16,256]{1,0:T(8,128)S(1)}, f32[16,256]{1,0:T(8,128)}, u32[]{:S(2)}) copy-start(f32[16,256]{1,0:T(8,128)} %param.16) | copy-start | bytes 49156
  31.3 5.5 %copy-start.5 = (f32[16,256]{1,0:T(8,128)S(1)}, f32[16,256]{1,0:T(8,128)}, u32[]{:S(2)}) copy-start(f32[16,256]{1,0:T(8,128)} %param.21) | copy-start | bytes 49156
  91.2 26.7 %copy-start.8 = (f32[256]{0:T(256)S(1)}, f32[256]{0:T(256)}, u32[]{:S(2)}) copy-start(f32[256]{0:T(256)} %param.19) | copy-start | bytes 3076
Sparse Core Ops, SparseCore 0:
  26.7 88.3 all-gather.1

commit v13 on v9

--- a/solution.py
+++ b/solution.py
@@ -19,13 +19,13 @@
         states_ref[t] = state
         return state
 
-    lax.fori_loop(0, count, forward, first_ref[...], unroll=8)
+    lax.fori_loop(0, count, forward, first_ref[...], unroll=16)
 
     def backward(i, running):
         t = count - 1 - i
         return decay_ref[t] * (source_ref[t] + running)
 
-    seed_ref[...] = lax.fori_loop(0, count, backward, jnp.zeros_like(first_ref[...]), unroll=8)
+    seed_ref[...] = lax.fori_loop(0, count, backward, jnp.zeros_like(first_ref[...]), unroll=16)
 
 
 def local_scans(decays, driving, sources, first_state):
@@ -51,7 +51,7 @@
         adjoint_ref[t] = value
         return decay_ref[t] * value
 
-    lax.fori_loop(0, count, backward, entering_ref[...], unroll=8)
+    lax.fori_loop(0, count, backward, entering_ref[...], unroll=16)
 
 
 def adjoint_scan(decays, sources, entering):

time: 136 us -> 136 us (level)
  transfers between devices with their start and end apart: 1 -> 1, of which waited for: 0 -> 0; matrix products, arithmetic and copies ran while one was open for 14% -> 15% of each run, Pallas kernels for 53% -> 53%
where the time goes in v13:
time: 136 us; the launch traced here: 135 us
  Pallas kernels  71.9 us (53%)
  other arithmetic  17.3 us (13%)
  blocking collectives  14.8 us (11%)
  between operations  14.2 us (10%)
  matrix products  10.6 us (8%)
  local copies, waits for them, and re-layouts  6.61 us (5%)
    pallas_call x1, Pallas kernels, relay(): pl.pallas_call(functools.partial(relay_kernel, axis, count), out_shape=ja...  43.8 us
    pallas_call x1, Pallas kernels, reduce_partials(): pl.pallas_call(reduce_kernel, out_shape=(jax.ShapeDtypeStruct((n_e,) + co...  18.7 us
    all_to_all x1, blocking collectives, body(): lax.all_to_all(buffer, 'exp', split_axis=0, concat_axis=1, tiled=True)  14.8 us
    dot_general x1, matrix products, body(): jnp.einsum('lrf,lrd->lfd', hidden_saved, all_rows, preferred_element_type...  6.83 us
    pallas_call x1, Pallas kernels, local_scans(): pl.pallas_call(local_scans_kernel, out_shape=(jax.ShapeDtypeStruct(decays...  5.44 us
    reduce_sum x1, other arithmetic, body(): jnp.sum(adjoint * (-steps[:, None, :] * decays * before), axis=0)  4.14 us
    pallas_call x1, Pallas kernels, adjoint_scan(): pl.pallas_call(adjoint_scan_kernel, out_shape=jax.ShapeDtypeStruct(decays...  3.92 us
    dot_general x1, matrix products, body(): jnp.einsum('lrd,lfd->lrf', all_rows, w_down, preferred_element_type=jnp.f...  3.42 us
  transfers between devices with their start and end apart: 1, of which 0 were waited for; matrix products, arithmetic and copies ran while one was open for 15% of the time, Pallas kernels for 53%

profile of v13, /device:TPU:1, one launch (start us, length us, event | category | flops | bytes accessed | tf_op | source)
XLA Modules:
  0.0 135.4 jit_solution(14483505461283593999)
XLA Ops:
  7.2 0.0 copy-start
  7.2 0.0 copy-start.6
  7.2 0.0 copy-start.1
  7.2 0.0 copy-start.7
  7.2 0.0 copy-start.2
  7.2 0.0 copy-start.3
  7.2 0.0 all-gather.2.cloned.1.call-start
  7.3 0.9 copy.33
  8.2 0.1 reshape.70
  8.2 0.1 fusion.26
  8.4 0.2 select_reduce_fusion
  8.5 0.9 mul.177
  9.5 0.2 mul.178
  9.7 0.8 copy.34
  10.4 0.1 mul.175
  10.5 0.3 convolution_convert_fusion
  10.9 0.2 reshape.71
  11.0 14.8 %all_to_all.12 = bf16[16,2,4096]{2,1,0:T(2,128)(2,1)S(1)} all-to-all(bf16[16,2,4096]{2,1,0:T(2,128)(2,1)S(1)} %reshape.71), channel_id=1, replica_groups=mesh['ctx'=32,'exp'=16] {'exp'}, dimensions={0} | all-to-all | bytes 524288 | tf_op jit(solution)/shard_map/all_to_all | solution.py:279
  25.8 0.0 copy-start.4
  25.8 0.8 all_to_all.10
  26.6 0.0 all-gather.2.cloned.1.call-update
  26.6 0.0 copy-done.6
  26.6 0.1 copy.29
  26.7 0.0 copy-done.1
  26.8 0.0 copy-done.7
  26.8 0.1 copy.30
  26.9 0.0 copy-done.2
  26.9 0.0 copy-done.3
  27.0 1.7 %broadcast_multiply_fusion.1.source_ref = f32[128,16,256]{2,1,0:T(8,128)} fusion(f32[128,256]{1,0:T(8,128)S(1)} %convert_element_type.45, f32[128,16]{1,0:T(8,128)S(1)} %copy.30), kind=kLoop, calls=%fused_computation.17 | loop fusion | flops 524288 | bytes 2236416 | tf_op jit(solution)/shard_map/mul | solution.py:249
  28.7 0.0 copy-done.4
  28.7 2.6 %multiply_exponential_fusion = (f32[128,16,256]{2,1,0:T(8,128)}, f32[128,16,256]{2,1,0:T(8,128)}) fusion(f32[16,256]{1,0:T(8,128)S(1)} %copy-done.4, f32[128,256]{1,0:T(8,128)S(1)} %get-tuple-element.23, f32[128,16]{1,0:T(8,128)S(1)} %copy.29, f32[128,256]{1,0:T(8,128)S(1)} %get-tuple-element.22), kind=kLoop, calls=%fused_computation.12 | loop fusion | flops 1048576 | bytes 4481024 | tf_op jit(solution)/shard_map/exp | solution.py:247
  31.3 0.0 copy-start.5
  31.3 5.4 %shard_map.189 = (f32[128,16,256]{2,1,0:T(8,128)}, f32[128,16,256]{2,1,0:T(8,128)}, f32[16,256]{1,0:T(8,128)}) custom-call(f32[128,16,256]{2,1,0:T(8,128)} %get-tuple-element.28.decay_ref, f32[128,16,256]{2,1,0:T(8,128)} %get-tuple-element.29.drive_ref, f32[128,16,256]{2,1,0:T(8,128)} %broadcast_multiply_fusion.1.source_ref, f32[16,256]{1,0:T(8,128)} %bitcast.48), custom_call_target="tpu_custom_call" | custom-call | flops 2097152 | bytes 10485760 | tf_op jit(solution)/shard_map/pallas_call | solution.py:32
  36.8 0.0 copy-done.5
  36.8 0.7 select_bitcast_fusion
  37.5 0.6 pad_maximum_fusion.pair_ref
  38.1 43.8 %shard_map.190 = f32[16,256]{1,0:T(8,128)} custom-call(f32[2,16,256]{2,1,0:T(8,128)} %pad_maximum_fusion.pair_ref), custom_call_target="tpu_custom_call" | custom-call | tf_op jit(solution)/shard_map/pallas_call | solution.py:125
  82.0 1.3 broadcast_select_fusion.entering_ref
  83.3 3.9 %shard_map.191 = f32[128,16,256]{2,1,0:T(8,128)} custom-call(f32[128,16,256]{2,1,0:T(8,128)} %get-tuple-element.28.decay_ref, f32[128,16,256]{2,1,0:T(8,128)} %broadcast_multiply_fusion.1.source_ref, f32[16,256]{1,0:T(8,128)} %broadcast_select_fusion.entering_ref), custom_call_target="tpu_custom_call" | custom-call | flops 1048576 | bytes 6291456 | tf_op jit(solution)/shard_map/pallas_call | solution.py:58
  87.2 4.1 %multiply_reduce_fusion = (f32[16,256]{1,0:T(8,128)S(1)}, bf16[128,256]{1,0:T(8,128)(2,1)}, f32[128,256]{1,0:T(8,128)S(1)}, f32[128,16]{1,0:T(8,128)S(1)}) fusion(f32[128,16,256]{2,1,0:T(8,128)} %shard_map.191, f32[128,16,256]{2,1,0:T(8,128)} %get-tuple-element.13, f32[16,256]{1,0:T(8,128)S(1)} %copy-done.4, f32[128,256]{1,0:T(8,128)S(1)} %get-tuple-element.23, ...), kind=kLoop, calls=%fused_computation.7 | loop fusion | flops 7792640 | bytes 4833280 | tf_op jit(solution)/shard_map/reduce_sum | solution.py:269
  91.4 0.0 copy-start.8
  91.4 0.0 copy-start.10
  91.4 2.1 %multiply_reduce_fusion.1 = f32[128,16]{1,0:T(8,128)S(1)} fusion(f32[128,16,256]{2,1,0:T(8,128)} %get-tuple-element.14, f32[128,256]{1,0:T(8,128)S(1)} %convert_element_type.45), kind=kLoop, calls=%fused_computation.8 | loop fusion | flops 1046528 | bytes 2236416 | tf_op jit(solution)/shard_map/reduce_sum | solution.py:251
  93.5 0.1 copy.32
  93.5 0.6 reshape.68.parts_ref
  94.2 0.6 pad_maximum_fusion.1.cols_ref
  94.8 18.7 %shard_map.192 = (f32[16,2,16,128]{3,2,1,0:T(8,128)}, f32[32,1,128]{2,1,0:T(1,128)}) custom-call(f32[2,16,128]{2,1,0:T(8,128)} %pad_maximum_fusion.1.cols_ref, f32[32,1,128]{2,1,0:T(1,128)} %reshape.68.parts_ref), custom_call_target="tpu_custom_call" | custom-call | tf_op jit(solution)/shard_map/pallas_call | solution.py:187
  113.5 0.5 broadcast.29
  114.0 1.4 %reduce.3 = f32[32,128]{1,0:T(8,128)S(1)} reduce(f32[32,1,128]{2,1,0:T(1,128)} %get-tuple-element.16, f32[]{:T(128)} %broadcast.29), dimensions={1}, to_apply=%get-tuple-element.16.reduce_sub_computation.3 | reduce | bytes 32772 | tf_op jit(solution)/shard_map/pallas_call | solution.py:187
  115.4 0.6 reshape.69
  116.0 1.0 reduce_sum.78
  117.0 0.6 slice_bitcast_fusion
  117.6 0.0 copy-done.8
  117.6 0.7 fusion.23
  118.2 0.0 all-gather.2.cloned.1.call-done
  118.2 0.0 copy-done.10
  118.3 0.0 copy-start.9
  118.3 6.8 %fusion.7 = bf16[1,224,4096]{2,1,0:T(8,128)(2,1)} fusion(bf16[1,1024,4096]{2,1,0:T(8,128)(2,1)} %all-gather.2.cloned.1.call-done, bf16[1,1024,224]{1,2,0:T(8,128)(2,1)S(1)} %copy-done.10), kind=kOutput, calls=%fused_computation.5 | convolution fusion | flops 1879965696 | bytes 10682368 | tf_op jit(solution)/shard_map/lrf,lrd->lfd/dot_general | solution.py:281
  125.1 0.0 copy-done
  125.1 0.0 copy-done.9
  125.1 3.4 %fusion.16 = bf16[1,1024,224]{1,2,0:T(8,128)(2,1)} fusion(bf16[1,224,4096]{2,1,0:T(8,128)(2,1)S(1)} %copy-done, bf16[1,1024,4096]{2,1,0:T(8,128)(2,1)S(1)} %copy-done.9), kind=kOutput, calls=%fused_computation.15 | convolution fusion | flops 1879277568 | bytes 10682368 | tf_op jit(solution)/shard_map/lrd,lfd->lrf/dot_general | solution.py:284
  (6 shorter events, 0.2 us)
Async XLA Ops:
  7.2 117.9 %copy-start = (bf16[1,224,4096]{2,1,0:T(8,128)(2,1)S(1)}, bf16[1,224,4096]{2,1,0:T(8,128)(2,1)}, u32[]{:S(2)}) copy-start(bf16[1,224,4096]{2,1,0:T(8,128)(2,1)} %param.26) | copy-start | bytes 5505028
  7.2 19.4 %copy-start.6 = (f32[16,128]{1,0:T(8,128)S(1)}, f32[16,128]{1,0:T(8,128)}, u32[]{:S(2)}) copy-start(f32[16,128]{1,0:T(8,128)} %param.17) | copy-start | bytes 24580
  7.2 19.5 %copy-start.1 = (bf16[128,256]{1,0:T(8,128)(2,1)S(1)}, bf16[128,256]{1,0:T(8,128)(2,1)}, u32[]{:S(2)}) copy-start(bf16[128,256]{1,0:T(8,128)(2,1)} %param.22) | copy-start | bytes 196612
  7.2 19.6 %copy-start.7 = (f32[16,128]{1,0:T(8,128)S(1)}, f32[16,128]{1,0:T(8,128)}, u32[]{:S(2)}) copy-start(f32[16,128]{1,0:T(8,128)} %param.18) | copy-start | bytes 24580
  7.2 19.7 %copy-start.2 = (bf16[128,256]{1,0:T(8,128)(2,1)S(1)}, bf16[128,256]{1,0:T(8,128)(2,1)}, u32[]{:S(2)}) copy-start(bf16[128,256]{1,0:T(8,128)(2,1)} %param.14) | copy-start | bytes 196612
  7.2 19.7 %copy-start.3 = (bf16[128,256]{1,0:T(8,128)(2,1)S(1)}, bf16[128,256]{1,0:T(8,128)(2,1)}, u32[]{:S(2)}) copy-start(bf16[128,256]{1,0:T(8,128)(2,1)} %param.15) | copy-start | bytes 196612
  7.2 111.0 %all-gather.2.cloned.1.call-start = ((), (), s32[]{:S(2)}) async-start(), calls=%async_computation.1 | async-start | bytes 8650752 | tf_op jit(solution)/shard_map/all_gather | solution.py:280
  25.8 2.9 %copy-start.4 = (f32[16,256]{1,0:T(8,128)S(1)}, f32[16,256]{1,0:T(8,128)}, u32[]{:S(2)}) copy-start(f32[16,256]{1,0:T(8,128)} %param.16) | copy-start | bytes 49156
  31.3 5.4 %copy-start.5 = (f32[16,256]{1,0:T(8,128)S(1)}, f32[16,256]{1,0:T(8,128)}, u32[]{:S(2)}) copy-start(f32[16,256]{1,0:T(8,128)} %param.21) | copy-start | bytes 49156
  91.4 26.2 %copy-start.8 = (f32[256]{0:T(256)S(1)}, f32[256]{0:T(256)}, u32[]{:S(2)}) copy-start(f32[256]{0:T(256)} %param.19) | copy-start | bytes 3076
  91.4 26.9 %copy-start.10 = (bf16[1,1024,224]{1,2,0:T(8,128)(2,1)S(1)}, bf16[1,1024,224]{1,2,0:T(8,128)(2,1)}, u32[]{:S(2)}) copy-start(bf16[1,1024,224]{1,2,0:T(8,128)(2,1)} %param.27) | copy-start | bytes 1376260
  118.3 6.8 %copy-start.9 = (bf16[1,1024,4096]{2,1,0:T(8,128)(2,1)S(1)}, bf16[1,1024,4096]{2,1,0:T(8,128)(2,1)}, u32[]{:S(2)}) copy-start(bf16[1,1024,4096]{2,1,0:T(8,128)(2,1)} %all-gather.2.cloned.1.call-done) | copy-start | bytes 25165828
Sparse Core Ops, SparseCore 0:
  26.7 87.8 all-gather.1
